TPU v7x, 256 devices: a whole 4x4x8 slice. The times are simulated.
256 devices in a mesh: dp: 32 (over y, z), segment: 2 (over x_lo), chan: 4 (over x_hi, core).
Axes of the slice: x: 4 (x_hi: 2, x_lo: 2; x = x_hi * 2 + x_lo), y: 4, z: 8, core: 2. Of those that a mesh axis runs over, the one named last changes fastest.
Arguments:
- base: bfloat16 [64, 512, 256], P('dp', 'chan'), may hold values from -6 to 6
- style: float32 [2, 64, 512], P('segment', 'dp'), may hold values from -3 to 3
- noise: float32 [2, 64, 256], P('segment', 'dp'), may hold values from -6 to 6
- conv_weight: bfloat16 [2, 4608, 512], P('segment', None, 'chan'), may hold values from -0.09375 to 0.09375
- conv_bias: float32 [2, 512], P('segment', 'chan'), may hold values from -3 to 3
- noise_gain: float32 [2, 512], P('segment', 'chan'), may hold values from 0.1 to 1
- rgb_weight: bfloat16 [2, 3, 512], P('segment', None, 'chan'), may hold values from -0.25 to 0.25
- disc_weight: float32 [3, 256], replicated, may hold values from -3.5 to 3.5
- disc_bias: float32 [256], replicated, may hold values from -3 to 3
- disc_out: float32 [256], replicated, may hold values from -3 to 3
Outputs:
- conv_grad: float32 [2, 4608, 512], P('segment', 'dp', 'chan')
- logits: float32 [64], P('dp')
- section_input_grads: bfloat16 [2, 64, 512, 256], P('segment', 'dp', 'chan')
All inputs are finite; a program needn't handle non-finite values.
Results may differ from a plain program's by a relative error of at most 0.015.
Values may be sent and summed in bfloat16 or wider, within the bound.
No kernel may reach another device: no remote copies, remote signals or barrier semaphores. Data moves between devices by JAX's collectives and lax.ppermute only.
A program may use at most 64 MiB of HBM per device.

v0:
```python
import functools

import jax
import jax.numpy as jnp
from jax import lax
from jax.experimental import pallas as pl
from jax.experimental.pallas import tpu as pltpu
from jax.sharding import PartitionSpec as P


RES = 16
PIX = RES * RES
TAPS = 9
EXTRA = 16
TAIL = 32
epsilon = 1e-06
root_two = 1.4142135623730951
f32 = jnp.float32
bf16 = jnp.bfloat16


NT = (((1,), (1,)), ((), ()))


def act_parts(t):
    e = jnp.exp(-jnp.abs(t))
    r = 1.0 / (1.0 + e)
    soft = jnp.maximum(t, 0.0) + jnp.log(1.0 + e)
    sig = jnp.where(t >= 0.0, r, e * r)
    return soft, sig


def row_shift(v, a):
    if a == 0:
        return v
    zeros = jnp.zeros((RES, v.shape[1]), v.dtype)
    parts = []
    for b in range(v.shape[0] // PIX):
        base = b * PIX
        if a > 0:
            parts += [v[base + RES : base + PIX], zeros]
        else:
            parts += [zeros, v[base : base + PIX - RES]]
    return jnp.concatenate(parts, axis=0)


def col_shift(v, b):
    if b == 0:
        return v
    x = lax.broadcasted_iota(jnp.int32, v.shape, 0) & (RES - 1)
    if b > 0:
        return jnp.where(x < RES - 1, pltpu.roll(v, v.shape[0] - 1, 0), 0.0)
    return jnp.where(x > 0, pltpu.roll(v, 1, 0), 0.0)


def pad_rows(v, rows):
    return jnp.concatenate([v, jnp.zeros((rows - v.shape[0], v.shape[1]), v.dtype)], axis=0)


def prep_kernel(idx, *refs):
    number = (len(refs) - 8) // 2
    sources, outs, copies = refs[:number], refs[number : number + 7], refs[number + 7 : -1]
    sem = refs[-1]
    moves = [
        pltpu.make_async_copy(src, dst, sem.at[n]) for n, (src, dst) in enumerate(zip(sources, copies))
    ]
    for move in moves:
        move.start()
    for move in moves:
        move.wait()
    w_ref, sty_ref, noise_ref, gain_ref, bias_ref, dw_ref, db_ref, do_ref, rgb_ref = copies
    wslot_ref, stys_ref, demod_ref, nb_ref, disc_ref, rgbp_ref, stycopy_ref = outs
    rgbp_ref[...] = pad_rows(rgb_ref[...], EXTRA)
    stycopy_ref[...] = sty_ref[...]
    chan = idx[1]
    own = w_ref.shape[1]
    full = w_ref.shape[0] // TAPS
    count = sty_ref.shape[0]
    chans = full // own
    for d in range(chans):
        part = chan ^ d
        for k in range(TAPS):
            start = pl.multiple_of(k * full + part * own, own)
            wslot_ref[d * own : (d + 1) * own, k * own : (k + 1) * own] = w_ref[pl.ds(start, own), :]
        stys_ref[:, d * own : (d + 1) * own] = sty_ref[:, pl.ds(pl.multiple_of(part * own, own), own)]
    squares = jnp.zeros((full, own), f32)
    for k in range(TAPS):
        w = w_ref[k * full : (k + 1) * full, :].astype(f32)
        squares = squares + w * w
    sty = sty_ref[...]
    cols = pad_rows(sty * sty, own).T
    for b in range(count):
        total = jnp.sum(cols[:, b : b + 1] * squares, axis=0, keepdims=True)
        demod_ref[b : b + 1, :] = lax.rsqrt(total + epsilon)
        noise = jnp.broadcast_to(noise_ref[b : b + 1, :], (own, PIX)).T
        nb_ref[b * PIX : (b + 1) * PIX, :] = gain_ref[...] * noise + bias_ref[...]
    rows = [dw_ref[0:1, :], dw_ref[1:2, :], dw_ref[2:3, :], db_ref[...], do_ref[...]]
    for n, row in enumerate(rows):
        disc_ref[n] = jnp.broadcast_to(row, (own, row.shape[1])).T


def conv_kernel(second, *refs):
    x_refs = refs[:4]
    stys_ref, wslot_ref, demod_ref, nb_ref, rgb_ref = refs[4:9]
    pay_ref, slope_ref, z_ref, xm_ref = refs[9:13]
    count = stys_ref.shape[0]
    own = demod_ref.shape[1]
    pixels = count * PIX
    for d in range(4):
        for b in range(count):
            sty = stys_ref[b : b + 1, d * own : (d + 1) * own]
            x = x_refs[d][b * PIX : (b + 1) * PIX, :] if second else x_refs[d][b].T
            x = x.astype(f32)
            xm_ref[b * PIX : (b + 1) * PIX, d * own : (d + 1) * own] = (x * sty).astype(bf16)
    products = jnp.dot(xm_ref[...], wslot_ref[...], preferred_element_type=f32)
    z = None
    for kx in range(3):
        total = None
        for ky in range(3):
            k = 3 * ky + kx
            moved = row_shift(products[:, k * own : (k + 1) * own], ky - 1)
            total = moved if total is None else total + moved
        total = col_shift(total, kx - 1)
        z = total if z is None else z + total
    z_ref[...] = z
    demod = jnp.concatenate(
        [jnp.broadcast_to(demod_ref[b : b + 1, :], (PIX, own)) for b in range(count)], axis=0
    )
    pre = demod * z + nb_ref[...]
    soft, sig = act_parts(pre)
    y = (root_two * (0.2 * pre + 0.8 * soft)).astype(bf16)
    slope_ref[...] = root_two * (0.2 + 0.8 * sig)
    rgb = rgb_ref[...]
    pay_ref[:pixels, :] = y
    pay_ref[pixels:, :] = rgb
    if second:
        refs[13][...] = lax.dot_general(rgb, y, NT, preferred_element_type=f32)[:8]


def first_image_kernel(*refs):
    out_ref = refs[-1]
    pixels = out_ref.shape[1]
    parts = [
        lax.dot_general(ref[pixels:, :], ref[:pixels, :], NT, preferred_element_type=f32)[:8]
        for ref in refs[:4]
    ]
    out_ref[...] = (parts[0] + parts[1]) + (parts[2] + parts[3])


def head_grad(dimage, rgb_ref):
    own = rgb_ref.shape[1]
    hi = dimage.astype(bf16).astype(f32)
    lo = dimage - hi
    left = pad_rows(jnp.concatenate([hi, lo], axis=0), own).T.astype(bf16)
    rgb = rgb_ref[...].astype(f32)[:8]
    right = jnp.concatenate([rgb, rgb], axis=0)
    return jnp.dot(left, pad_rows(right, own).astype(bf16), preferred_element_type=f32)


def store_gz(da, z, demod_ref, pay_ref):
    count, own = demod_ref.shape
    rows = []
    for b in range(count):
        demod = demod_ref[b : b + 1, :]
        part = da[b * PIX : (b + 1) * PIX]
        pay_ref[b * PIX : (b + 1) * PIX, :] = (part * demod).astype(bf16)
        d_demod = jnp.sum(part * z[b * PIX : (b + 1) * PIX], axis=0, keepdims=True)
        rows.append(-d_demod * demod * demod * demod)
    coef = jnp.concatenate(rows + [jnp.zeros((8 - count, own), f32)], axis=0)
    hi = coef.astype(bf16).astype(f32)
    pay_ref[count * PIX :, :] = jnp.concatenate([hi, coef - hi], axis=0).astype(bf16)


def store_dx(gz, wslot_ref, stys_ref, put):
    count = stys_ref.shape[0]
    own = gz.shape[1]
    gz = gz.astype(f32)
    by_col = [col_shift(gz, 1 - kx).astype(bf16) for kx in range(3)]
    cols = jnp.concatenate(
        [row_shift(by_col[k % 3], 1 - k // 3) for k in range(TAPS)], axis=1
    )
    share = lax.dot_general(cols, wslot_ref[...], NT, preferred_element_type=f32)
    for d in range(4):
        for b in range(count):
            sty = stys_ref[b : b + 1, d * own : (d + 1) * own]
            put(d, b, share[b * PIX : (b + 1) * PIX, d * own : (d + 1) * own] * sty)


def disc_kernel(
    own_ref, r1_ref, r2_ref, r3_ref, first_ref, disc_ref, rgb_ref, slope_ref, z_ref, demod_ref,
    wslot_ref, stys_ref, tail_ref, pay_ref, keep_ref, send_ref,
):
    image = ((own_ref[...] + r1_ref[...]) + (r2_ref[...] + r3_ref[...])) + first_ref[...]
    lanes = 128
    per = PIX // lanes
    count = stys_ref.shape[0]
    out_rows, logits = [], []
    for b in range(count):
        logit = jnp.zeros((1, 1), f32)
        chunks = []
        for n in range(per):
            at = b * PIX + n * lanes
            q = disc_ref[3]
            for ch in range(3):
                q = q + disc_ref[ch] * image[ch : ch + 1, at : at + lanes]
            soft, sig = act_parts(q)
            hidden = 0.2 * q + 0.8 * soft
            logit = logit + jnp.sum(disc_ref[4] * hidden, keepdims=True)
            dq = (disc_ref[4] / PIX) * (0.2 + 0.8 * sig)
            chunks.append(
                [jnp.sum(disc_ref[ch] * dq, axis=0, keepdims=True) for ch in range(3)]
            )
        logit = logit / PIX
        e = jnp.exp(-jnp.abs(logit))
        g = -jnp.where(logit >= 0.0, e, 1.0) / (1.0 + e)
        rows = [jnp.concatenate([c[ch] for c in chunks], axis=1) * g for ch in range(3)]
        out_rows.append(jnp.concatenate(rows + [jnp.zeros((5, PIX), f32)], axis=0))
        wide = jnp.broadcast_to(logit, (1, lanes))
        hi = wide.astype(bf16).astype(f32)
        mid = (wide - hi).astype(bf16).astype(f32)
        logits += [hi, mid, wide - hi - mid]
    dimage = jnp.concatenate(out_rows, axis=1)
    pieces = [
        dimage[ch : ch + 1, n * lanes : (n + 1) * lanes] for ch in range(3) for n in range(count * per)
    ]
    high = jnp.concatenate(pieces, axis=0)
    low = high - high.astype(bf16).astype(f32)
    spare = TAIL - 2 * len(pieces) - len(logits)
    tail_ref[...] = jnp.concatenate(
        [high, low] + logits + [jnp.zeros((spare, lanes), f32)], axis=0
    ).astype(bf16)
    da = head_grad(dimage, rgb_ref) * slope_ref[...]
    store_gz(da, z_ref[...], demod_ref, pay_ref)

    def put(d, b, block):
        at = (d // 2) * count * PIX + b * PIX
        if d % 2 == 0:
            keep_ref[at : at + PIX, :] = block
        else:
            send_ref[at : at + PIX, :] = block.astype(bf16)

    store_dx(pay_ref[: count * PIX, :], wslot_ref, stys_ref, put)


def pair_kernel(keep_ref, got_ref, tail_ref, near_ref, far_ref):
    rows = far_ref.shape[0]
    near_ref[rows:, :] = tail_ref[...]
    near_ref[:rows, :] = (keep_ref[:rows] + got_ref[:rows].astype(f32)).astype(bf16)
    far_ref[...] = (keep_ref[rows:] + got_ref[rows:].astype(f32)).astype(bf16)


def first_grad_kernel(
    idx, s0_ref, s1_ref, rgb_ref, slope_ref, z_ref, demod_ref, other_ref, tail_ref,
    pay_ref, logit_ref,
):
    count = demod_ref.shape[0]
    pixels = count * PIX
    chunks = pixels // 128

    def put_logits(tail):
        for b in range(count):
            at = 6 * chunks + 3 * b
            logit_ref[b] = jnp.max((tail[at : at + 1] + tail[at + 1 : at + 2]) + tail[at + 2 : at + 3])

    @pl.when(idx[0] == 0)
    def _():
        dx = (s0_ref[:pixels, :].astype(f32) + s1_ref[...].astype(f32)).astype(bf16)
        tail = s0_ref[pixels:, :].astype(f32)
        put_logits(tail)
        both = tail[: 3 * chunks] + tail[3 * chunks : 6 * chunks]
        rows = [
            jnp.concatenate(
                [both[ch * chunks + n : ch * chunks + n + 1] for n in range(chunks)], axis=1
            )
            for ch in range(3)
        ]
        dimage = jnp.concatenate(rows + [jnp.zeros((5, pixels), f32)], axis=0)
        da = (head_grad(dimage, rgb_ref) + dx.astype(f32)) * slope_ref[...]
        store_gz(da, z_ref[...], demod_ref, pay_ref)

    @pl.when(idx[0] != 0)
    def _():
        put_logits(tail_ref[...].astype(f32))
        pay_ref[...] = other_ref[...]


def share_kernel(pay_ref, wslot_ref, stys_ref, *out_refs):
    pixels = stys_ref.shape[0] * PIX

    def put(d, b, block):
        out_refs[d][b * PIX : (b + 1) * PIX, :] = block.astype(bf16)

    store_dx(pay_ref[:pixels, :], wslot_ref, stys_ref, put)


def turn_kernel(idx, xa_ref, xb_ref, sty_ref, out_ref, half_ref):
    chan = idx[1]
    full = xa_ref.shape[1]
    count = sty_ref.shape[0]
    own = full // 4

    def turn(ref):
        for d in range(4):
            start = pl.multiple_of((chan ^ d) * own, own)
            out_ref[pl.ds(start, own), :] = ref[:, d * own : (d + 1) * own].T

    @pl.when(idx[0] == 0)
    def _():
        turn(xa_ref)

    @pl.when(idx[0] != 0)
    def _():
        turn(xb_ref)

    sty = sty_ref[...]
    hi = sty.astype(bf16).astype(f32)
    mid = (sty - hi).astype(bf16).astype(f32)
    lo = sty - hi - mid
    rows = [hi, mid, lo]
    tail = jnp.concatenate(
        rows + [jnp.zeros((EXTRA - 3 * count, full), f32)], axis=0
    ).astype(bf16)
    out_ref[full:, :] = tail
    half = full // 2
    start = pl.multiple_of((chan & 1) * half, half)
    half_ref[:half, :] = out_ref[pl.ds(start, half), :]
    half_ref[half:, :] = tail


def taps_of(pay_ref, y, g_ref):
    own = pay_ref.shape[1]
    pixels = pay_ref.shape[0] - EXTRA
    count = pixels // PIX
    stride = PIX + 2 * RES
    zeros = jnp.zeros((RES, own), bf16)
    gz = pay_ref[:pixels, :].astype(f32)
    for kx in range(3):
        moved = col_shift(gz, 1 - kx).astype(bf16)
        for b in range(count):
            at = b * stride
            g_ref[kx, at : at + RES, :] = zeros
            g_ref[kx, at + RES : at + RES + PIX, :] = moved[b * PIX : (b + 1) * PIX]
            g_ref[kx, at + RES + PIX : at + stride, :] = zeros
    taps = []
    for j in range(3):
        k = 2 * y + j
        ky = k // 3
        kx = k - 3 * ky
        rows = []
        for b in range(count):
            start = b * stride + (2 - ky) * RES
            rows.append(g_ref[kx, pl.ds(pl.multiple_of(start, RES), PIX), :])
        taps.append(jnp.concatenate(rows, axis=0))
    return jnp.concatenate(taps, axis=1)


def own_weight_kernel(idx, pay_ref, own_ref, acc_ref, g_ref):
    full = own_ref.shape[0] - EXTRA
    acc_ref[...] = jnp.dot(
        own_ref[:full, :], taps_of(pay_ref, idx[2], g_ref), preferred_element_type=f32
    )


def weight_kernel(idx, *refs):
    pays, own_ref, near, far, w_ref, first_ref = refs[:4], refs[4], refs[5:8], refs[8:11], refs[11], refs[12]
    keep_ref, send_ref = refs[13:15]
    g_ref, acc_ref, sum_ref = refs[15:18]
    core, y, z = idx[1] & 1, idx[2], idx[3]
    full = own_ref.shape[0] - EXTRA
    half = full // 2
    own = pays[0].shape[1]
    pixels = pays[0].shape[0] - EXTRA
    count = pixels // PIX
    rest = [taps_of(pays[n], y, g_ref.at[n - 1]) for n in (1, 2, 3)]
    for refs_, where in ((near, core), (far, 1 - core)):
        part = None
        for ref, taps in zip(refs_, rest):
            more = jnp.dot(ref[:half, :], taps, preferred_element_type=f32)
            part = more if part is None else part + more
        at = pl.ds(pl.multiple_of(where * half, half), half)
        acc_ref[at, :] = first_ref[at, :] + part
    sty_rows, coef_rows = [], []
    for n in range(4):
        tail = own_ref[full:, :] if n == 0 else near[n - 1][half:, :]
        tail = tail.astype(f32)
        sty = tail[:count] + tail[count : 2 * count] + tail[2 * count : 3 * count]
        sty_rows.append(sty * sty)
        tail = pays[n][pixels:, :].astype(f32)
        coef_rows.append(tail[:count] + tail[8 : 8 + count])
    left = pad_rows(jnp.concatenate(sty_rows, axis=0), own).T
    right = pad_rows(jnp.concatenate(coef_rows, axis=0), own)
    demod_term = jnp.dot(left, right, precision=lax.Precision.HIGHEST, preferred_element_type=f32)
    for j in range(3):
        start = pl.multiple_of((2 * y + j) * full, full)
        w = w_ref[pl.ds(start, full), :].astype(f32)
        sum_ref[j * full : (j + 1) * full, :] = (
            acc_ref[:, j * own : (j + 1) * own] + w * demod_term
        )
    rows = keep_ref.shape[0] // 4
    for e in range(4):
        for ref, first in ((keep_ref, z), (send_ref, z ^ 1)):
            start = y * own + ((first + 2 * e) & 7) * rows
            block = sum_ref[pl.ds(pl.multiple_of(start, RES), rows), :]
            ref[e * rows : (e + 1) * rows, :] = block.astype(ref.dtype)


def z_pair_kernel(keep_ref, got_ref, own_ref, *out_refs):
    rows = own_ref.shape[0]
    own_ref[...] = keep_ref[:rows] + got_ref[:rows].astype(f32)
    for e, ref in enumerate(out_refs):
        at = slice((e + 1) * rows, (e + 2) * rows)
        ref[...] = (keep_ref[at] + got_ref[at].astype(f32)).astype(bf16)


def total_kernel(count, *refs):
    grad_ref, dx_ref = refs[-2:]
    total = refs[0][...].astype(f32)
    for ref in refs[1:count]:
        total = total + ref[...].astype(f32)
    grad_ref[...] = total
    shares = [ref[...].astype(f32) for ref in refs[count : count + 4]]
    dx = ((shares[0] + shares[1]) + (shares[2] + shares[3])).astype(bf16)
    for b in range(dx_ref.shape[0]):
        dx_ref[b] = dx[b * PIX : (b + 1) * PIX].T


def call(kernel, outs, args, scratch=(), scalars=0, raws=0, keep=True):
    smem = pl.BlockSpec(memory_space=pltpu.SMEM)
    vmem = pl.BlockSpec(memory_space=pltpu.VMEM)
    plain = scalars + raws
    args = (
        list(args[:scalars])
        + [pltpu.with_memory_space_constraint(a, pltpu.HBM) for a in args[scalars:plain]]
        + [pltpu.with_memory_space_constraint(a, pltpu.VMEM) for a in args[plain:]]
    )
    hbm = pl.BlockSpec(memory_space=pltpu.HBM)
    place = pltpu.VMEM if keep else jax.ShapeDtypeStruct
    return pl.pallas_call(
        kernel,
        out_shape=[
            jax.ShapeDtypeStruct(*o[:2]) if len(o) > 2 else place(*o) for o in outs
        ],
        in_specs=[smem] * scalars + [hbm] * raws + [vmem] * (len(args) - plain),
        out_specs=[smem if len(o) > 2 else vmem for o in outs],
        scratch_shapes=list(scratch),
        compiler_params=pltpu.CompilerParams(vmem_limit_bytes=20 * 2**20),
    )(*args)


def body(
    base, style, noise, conv_weight, conv_bias, noise_gain, rgb_weight, disc_weight, disc_bias,
    disc_out,
):
    weight, styles, noises, rgb = conv_weight[0], style[0], noise[0], rgb_weight[0]
    own = weight.shape[1]
    full = weight.shape[0] // TAPS
    count = base.shape[0]
    pixels = count * PIX
    dp_index = lax.axis_index("dp")
    idx = jnp.stack(
        [lax.axis_index("segment"), lax.axis_index("chan"), dp_index // 8, dp_index % 8]
    ).astype(jnp.int32)

    def across(value, links):
        return lax.ppermute(value, ("segment", "chan"), links)

    def over_y(value, d):
        return lax.ppermute(
            value, "dp", [(y * 8 + z, (y + d) % 4 * 8 + z) for y in range(4) for z in range(8)]
        )

    def over_z(value, d):
        return lax.ppermute(
            value, "dp", [(y * 8 + z, y * 8 + (z + d) % 8) for y in range(4) for z in range(8)]
        )

    def flip(value, d):
        return across(value, [(s * 4 + c, (1 - s) * 4 + (c ^ d)) for s in range(2) for c in range(4)])

    def within(value, d):
        return across(value, [(s * 4 + c, s * 4 + (c ^ d)) for s in range(2) for c in range(4)])

    x2 = flip(base, 2)
    x1 = within(base, 1)
    x3 = within(x2, 1)
    sources = [
        weight, styles, noises, noise_gain, conv_bias, disc_weight, disc_bias[None], disc_out[None],
        rgb,
    ]
    wslot, stys, demod, nb, disc, rgbp, sty = call(
        prep_kernel,
        [
            ((full, TAPS * own), bf16),
            ((count, full), f32),
            ((count, own), f32),
            ((pixels, own), f32),
            ((5, disc_weight.shape[1], own), f32),
            ((EXTRA, own), bf16),
            ((count, full), f32),
        ],
        [idx, *sources],
        scratch=[pltpu.VMEM(a.shape, a.dtype) for a in sources]
        + [pltpu.SemaphoreType.DMA((len(sources),))],
        scalars=1,
        raws=len(sources),
    )
    conv_outs = [
        ((pixels + EXTRA, own), bf16),
        ((pixels, own), f32),
        ((pixels, own), f32),
        ((pixels, full), bf16),
    ]
    pay, slope_a, z_a, xm_a = call(
        functools.partial(conv_kernel, False),
        conv_outs,
        [base, x1, x2, x3, stys, wslot, demod, nb, rgbp],
    )
    y0 = flip(pay, 0)
    y2 = flip(pay, 2)
    y1 = within(y0, 1)
    y3 = within(y2, 1)
    _, slope_b, z_b, xm_b, image_own = call(
        functools.partial(conv_kernel, True),
        conv_outs + [((8, pixels), f32)],
        [y0, y1, y2, y3, stys, wslot, demod, nb, rgbp],
    )
    images = [within(image_own, d) for d in (1, 2, 3)]
    xm, xm_half = call(
        turn_kernel,
        [((full + EXTRA, pixels), bf16), ((full // 2 + EXTRA, pixels), bf16)],
        [idx, xm_a, xm_b, sty],
        scalars=1,
    )
    (image_first,) = call(first_image_kernel, [((8, pixels), f32)], [y0, y1, y2, y3])
    near = [over_y(xm_half, d) for d in (1, 2, 3)]
    far = [within(near[n], 1) for n in range(3)]
    two = (2 * pixels, own)
    tail, pay_b, dx_keep, dx_send = call(
        disc_kernel,
        [((TAIL, own), bf16), ((pixels + EXTRA, own), bf16), (two, f32), (two, bf16)],
        [image_own, *images, image_first, disc, rgbp, slope_b, z_b, demod, wslot, stys],
    )
    dx_got = within(dx_send, 1)
    share = ((pixels, own), bf16)
    dx_near, dx_far = call(
        pair_kernel, [((pixels + TAIL, own), bf16), share], [dx_keep, dx_got, tail]
    )
    got = [flip(dx_near, 0), flip(dx_far, 2)]
    pay_g, logits = call(
        first_grad_kernel,
        [((pixels + EXTRA, own), bf16), ((count,), f32, True)],
        [idx, *got, rgbp, slope_a, z_a, demod, pay_b, tail],
        scalars=1,
    )
    pays = [pay_g] + [over_y(pay_g, d) for d in (1, 2, 3)]
    shares = call(share_kernel, [share] * 4, [pay_g, wslot, stys])
    mine = [shares[0]] + [within(shares[d], d) for d in (1, 2, 3)]
    rows = weight.shape[0] // 32
    taps = (3, count * (PIX + 2 * RES), own)
    (first,) = call(
        own_weight_kernel,
        [((full, 3 * own), f32)],
        [idx, pay_g, xm],
        scratch=[pltpu.VMEM(taps, bf16)],
        scalars=1,
    )
    z_keep, z_send = call(
        weight_kernel,
        [((4 * rows, own), f32), ((4 * rows, own), bf16)],
        [idx, *pays, xm, *near, *far, weight, first],
        scratch=[
            pltpu.VMEM((3, *taps), bf16),
            pltpu.VMEM((full, 3 * own), f32),
            pltpu.VMEM((3 * full, own), f32),
        ],
        scalars=1,
    )
    z_got = lax.ppermute(z_send, "dp", [(n, n ^ 1) for n in range(32)])
    block = (rows, own)
    z_own, *z_outs = call(z_pair_kernel, [(block, f32)] + [(block, bf16)] * 3, [z_keep, z_got])
    parts = [z_own] + [over_z(z_outs[e - 1], 2 * e) for e in (1, 2, 3)]
    grad_rows, dx = call(
        functools.partial(total_kernel, len(parts)),
        [((rows, own), f32), ((count, own, PIX), bf16)],
        [*parts, *mine],
        keep=False,
    )
    return (grad_rows[None], logits, dx[None])


def solution(mesh):
    placed = (
        P("dp", "chan", None),
        P("segment", "dp", None),
        P("segment", "dp", None),
        P("segment", None, "chan"),
        P("segment", "chan"),
        P("segment", "chan"),
        P("segment", None, "chan"),
        P(),
        P(),
        P(),
    )
    return jax.shard_map(
        body,
        mesh=mesh,
        in_specs=placed,
        out_specs=(P("segment", "dp", "chan"), P("dp"), P("segment", "dp", "chan", None)),
        check_vma=False,
    )
```

profile of v0, /device:TPU:4, one launch (start us, length us, event | category | flops | bytes accessed | tf_op | source)
XLA Modules:
  0.0 86.7 jit_solution(8825703552850070881)
XLA Ops:
  1.3 4.9 %collective-permute-done.1.refs_2_ = bf16[2,128,256]{2,1,0:T(8,128)(2,1)S(1)} collective-permute-done((bf16[2,128,256]{2,1,0:T(8,128)(2,1)}, bf16[2,128,256]{2,1,0:T(8,128)(2,1)S(1)}, u32[]{:S(2)}, u32[]{:S(2)}) %collective-permute-start.1) | collective-permute-done | bytes 131104 | tf_op jit(solution)/shard_map/ppermute | solution.py:465
  6.3 2.6 %shard_map.121 = (bf16[512,1152]{1,0:T(8,128)(2,1)S(1)}, f32[2,512]{1,0:T(2,128)S(1)}, f32[2,128]{1,0:T(2,128)S(1)}, f32[512,128]{1,0:T(8,128)S(1)}, f32[5,256,1...) custom-call(s32[4]{0:T(128)S(1)} %pad_add_fusion.idx, bf16[4608,128]{1,0:T(8,128)(2,1)} %bitcast.12, ...), custom_call_target="tpu_custom_call" | custom-call | tf_op jit(solution)/shard_map/pallas_call | solution.py:438
  8.9 1.1 %shard_map.122 = (bf16[528,128]{1,0:T(8,128)(2,1)S(1)}, f32[512,128]{1,0:T(8,128)S(1)}, f32[512,128]{1,0:T(8,128)S(1)}, bf16[512,512]{1,0:T(8,128)(2,1)S(1)}) custom-call(bf16[2,128,256]{2,1,0:T(8,128)(2,1)S(1)} %copy-done.1, bf16[2,128,256]{2,1,0:T(8,128)(2,1)S(1)} %collective-permute-done.refs_1_, bf16[2,128,256]{2,1,0:T(8,128)(2,1)S(1)} %collective-permute-done.1.refs_2_, ...), custom_call_target="tpu_custom_call" | custom-call | tf_op jit(solution)/shard_map/pallas_call | solution.py:438
  10.6 3.8 %collective-permute-start.3 = (bf16[528,128]{1,0:T(8,128)(2,1)S(1)}, bf16[528,128]{1,0:T(8,128)(2,1)S(1)}, u32[]{:S(2)}, u32[]{:S(2)}) collective-permute-start(bf16[528,128]{1,0:T(8,128)(2,1)S(1)} %get-tuple-element.45), channel_id=1, source_target_pairs={{0,4},{1,5},{2,6},{3,7},{4,0},{5,1},{6,2},{7,3},{8,12},{9,13},{10,... | collective-permute-start | bytes 405512 | tf_op jit(solution)/shard_map/ppermute | solution.py:465
  14.4 1.7 %collective-permute-done.5.refs_2_ = bf16[528,128]{1,0:T(8,128)(2,1)S(1)} collective-permute-done((bf16[528,128]{1,0:T(8,128)(2,1)S(1)}, bf16[528,128]{1,0:T(8,128)(2,1)S(1)}, u32[]{:S(2)}, u32[]{:S(2)}) %collective-permute-start.5) | collective-permute-done | bytes 135200 | tf_op jit(solution)/shard_map/ppermute | solution.py:465
  16.1 2.3 %collective-permute-done.3.refs_0_ = bf16[528,128]{1,0:T(8,128)(2,1)S(1)} collective-permute-done((bf16[528,128]{1,0:T(8,128)(2,1)S(1)}, bf16[528,128]{1,0:T(8,128)(2,1)S(1)}, u32[]{:S(2)}, u32[]{:S(2)}) %collective-permute-start.3) | collective-permute-done | bytes 135200 | tf_op jit(solution)/shard_map/ppermute | solution.py:465
  18.4 1.3 %collective-permute-done.4.refs_1_ = bf16[528,128]{1,0:T(8,128)(2,1)S(1)} collective-permute-done((bf16[528,128]{1,0:T(8,128)(2,1)S(1)}, bf16[528,128]{1,0:T(8,128)(2,1)S(1)}, u32[]{:S(2)}, u32[]{:S(2)}) %collective-permute-start.4) | collective-permute-done | bytes 135200 | tf_op jit(solution)/shard_map/ppermute | solution.py:465
  19.8 1.7 %shard_map.123 = (bf16[528,128]{1,0:T(8,128)(2,1)}, f32[512,128]{1,0:T(8,128)S(1)}, f32[512,128]{1,0:T(8,128)S(1)}, bf16[512,512]{1,0:T(8,128)(2,1)S(1)}, f32[8,512]{1,0:T(8,128)S(1)}) custom-call(bf16[528,128]{1,0:T(8,128)(2,1)S(1)} %collective-permute-done.3.refs_0_, bf16[528,128]{1,0:T(8,128)(2,1)S(1)} %collective-permute-done.4.refs_1_, ...), custom_call_target="tpu_custom_call" | custom-call | tf_op jit(solution)/shard_map/pallas_call | solution.py:438
  21.4 2.2 %collective-permute-start.9 = (f32[8,512]{1,0:T(8,128)S(1)}, f32[8,512]{1,0:T(8,128)S(1)}, u32[]{:S(2)}, u32[]{:S(2)}) collective-permute-start(f32[8,512]{1,0:T(8,128)S(1)} %get-tuple-element.46.own_ref), channel_id=1, source_target_pairs={{0,3},{1,2},{2,1},{3,0},{4,7},{5,6},{6,5},{7,4},{8,11},{9,10},{10,... | collective-permute-start | bytes 49160 | tf_op jit(solution)/shard_map/ppermute | solution.py:465
  23.6 1.1 %collective-permute-start.8 = (f32[8,512]{1,0:T(8,128)S(1)}, f32[8,512]{1,0:T(8,128)S(1)}, u32[]{:S(2)}, u32[]{:S(2)}) collective-permute-start(f32[8,512]{1,0:T(8,128)S(1)} %get-tuple-element.46.own_ref), channel_id=1, source_target_pairs={{0,2},{1,3},{2,0},{3,1},{4,6},{5,7},{6,4},{7,5},{8,10},{9,11},{10,... | collective-permute-start | bytes 49160 | tf_op jit(solution)/shard_map/ppermute | solution.py:465
  25.0 1.1 %collective-permute-done.9.r3_ref = f32[8,512]{1,0:T(8,128)S(1)} collective-permute-done((f32[8,512]{1,0:T(8,128)S(1)}, f32[8,512]{1,0:T(8,128)S(1)}, u32[]{:S(2)}, u32[]{:S(2)}) %collective-permute-start.9) | collective-permute-done | bytes 16416 | tf_op jit(solution)/shard_map/ppermute | solution.py:465
  26.1 2.8 %collective-permute-done.8.r2_ref = f32[8,512]{1,0:T(8,128)S(1)} collective-permute-done((f32[8,512]{1,0:T(8,128)S(1)}, f32[8,512]{1,0:T(8,128)S(1)}, u32[]{:S(2)}, u32[]{:S(2)}) %collective-permute-start.8) | collective-permute-done | bytes 16416 | tf_op jit(solution)/shard_map/ppermute | solution.py:465
  28.9 1.7 %shard_map.125 = (bf16[32,128]{1,0:T(8,128)(2,1)S(1)}, bf16[528,128]{1,0:T(8,128)(2,1)S(1)}, f32[1024,128]{1,0:T(8,128)S(1)}, bf16[1024,128]{1,0:T(8,128)(2,1)S(1)}) custom-call(f32[8,512]{1,0:T(8,128)S(1)} %get-tuple-element.46.own_ref, f32[8,512]{1,0:T(8,128)S(1)} %collective-permute-done.7.r1_ref, f32[8,512]{1,0:T(8,128)S(1)} %collective-permute-done.8.r2_ref, ...), custom_call_target="tpu_custom_call" | custom-call | tf_op jit(solution)/shard_map/pallas_call | solution.py:438
  30.7 0.8 shard_map.128
  31.5 2.6 %collective-permute-start.18 = (bf16[272,512]{1,0:T(8,128)(2,1)S(1)}, bf16[272,512]{1,0:T(8,128)(2,1)S(1)}, u32[]{:S(2)}, u32[]{:S(2)}) collective-permute-start(bf16[272,512]{1,0:T(8,128)(2,1)S(1)} %get-tuple-element.63), channel_id=1, source_target_pairs={{0,192},{8,200},{16,208},{24,216},{32,224},{40,232},{48,240},{56,2... | collective-permute-start | bytes 835592 | tf_op jit(solution)/shard_map/ppermute | solution.py:468
  34.6 1.0 %collective-permute-start.16 = (bf16[272,512]{1,0:T(8,128)(2,1)S(1)}, bf16[272,512]{1,0:T(8,128)(2,1)S(1)}, u32[]{:S(2)}, u32[]{:S(2)}) collective-permute-start(bf16[272,512]{1,0:T(8,128)(2,1)S(1)} %get-tuple-element.63), channel_id=1, source_target_pairs={{0,64},{8,72},{16,80},{24,88},{32,96},{40,104},{48,112},{56,120},{... | collective-permute-start | bytes 835592 | tf_op jit(solution)/shard_map/ppermute | solution.py:468
  35.7 1.0 %collective-permute-start.11 = (bf16[544,128]{1,0:T(8,128)(2,1)S(1)}, bf16[544,128]{1,0:T(8,128)(2,1)S(1)}, u32[]{:S(2)}, u32[]{:S(2)}) collective-permute-start(bf16[544,128]{1,0:T(8,128)(2,1)S(1)} %get-tuple-element.53), channel_id=1, source_target_pairs={{0,4},{1,5},{2,6},{3,7},{4,0},{5,1},{6,2},{7,3},{8,12},{9,13},{10,... | collective-permute-start | bytes 417800 | tf_op jit(solution)/shard_map/ppermute | solution.py:465
  37.1 9.5 %collective-permute-done.18.refs_7_ = bf16[272,512]{1,0:T(8,128)(2,1)S(1)} collective-permute-done((bf16[272,512]{1,0:T(8,128)(2,1)S(1)}, bf16[272,512]{1,0:T(8,128)(2,1)S(1)}, u32[]{:S(2)}, u32[]{:S(2)}) %collective-permute-start.18) | collective-permute-done | bytes 278560 | tf_op jit(solution)/shard_map/ppermute | solution.py:468
  47.1 3.2 %collective-permute-done.16.refs_5_ = bf16[272,512]{1,0:T(8,128)(2,1)S(1)} collective-permute-done((bf16[272,512]{1,0:T(8,128)(2,1)S(1)}, bf16[272,512]{1,0:T(8,128)(2,1)S(1)}, u32[]{:S(2)}, u32[]{:S(2)}) %collective-permute-start.16) | collective-permute-done | bytes 278560 | tf_op jit(solution)/shard_map/ppermute | solution.py:468
  50.3 1.4 %shard_map.127 = (bf16[528,128]{1,0:T(8,128)(2,1)S(1)}, f32[2]{0:T(128)}) custom-call(s32[4]{0:T(128)S(1)} %pad_add_fusion.idx, bf16[544,128]{1,0:T(8,128)(2,1)S(1)} %collective-permute-done.11.s0_ref, bf16[512,128]{1,0:T(8,128)(2,1)S(1)} %collective-permute-done.12.s1_ref, bf16[16,128]{1,0:T(8,128)(2,1)S(1)} %get-tuple-element.44.refs_8_.rgb_ref, ...), custom_call_target="tpu_custom_call" | custom-call | tf_op jit(solution)/shard_map/pallas_call | solution.py:438
  53.0 5.2 %collective-permute-done.15.refs_3_ = bf16[528,128]{1,0:T(8,128)(2,1)S(1)} collective-permute-done((bf16[528,128]{1,0:T(8,128)(2,1)S(1)}, bf16[528,128]{1,0:T(8,128)(2,1)S(1)}, u32[]{:S(2)}, u32[]{:S(2)}) %collective-permute-start.15) | collective-permute-done | bytes 135200 | tf_op jit(solution)/shard_map/ppermute | solution.py:468
  58.2 1.1 %shard_map.129.refs_12_ = f32[512,384]{1,0:T(8,128)S(1)} custom-call(s32[4]{0:T(128)S(1)} %pad_add_fusion.idx, bf16[528,128]{1,0:T(8,128)(2,1)S(1)} %get-tuple-element.58.pay_ref.refs_0_, bf16[528,512]{1,0:T(8,128)(2,1)S(1)} %get-tuple-element.62.own_ref.refs_4_), custom_call_target="tpu_custom_call" | custom-call | tf_op jit(solution)/shard_map/pallas_call | solution.py:438
  59.5 4.9 %collective-permute-done.13.refs_1_ = bf16[528,128]{1,0:T(8,128)(2,1)S(1)} collective-permute-done((bf16[528,128]{1,0:T(8,128)(2,1)S(1)}, bf16[528,128]{1,0:T(8,128)(2,1)S(1)}, u32[]{:S(2)}, u32[]{:S(2)}) %collective-permute-start.13) | collective-permute-done | bytes 135200 | tf_op jit(solution)/shard_map/ppermute | solution.py:468
  64.4 2.4 %shard_map.130 = (f32[576,128]{1,0:T(8,128)S(1)}, bf16[576,128]{1,0:T(8,128)(2,1)S(1)}) custom-call(s32[4]{0:T(128)S(1)} %pad_add_fusion.idx, bf16[528,128]{1,0:T(8,128)(2,1)S(1)} %get-tuple-element.58.pay_ref.refs_0_, bf16[528,128]{1,0:T(8,128)(2,1)S(1)} %collective-permute-done.13.refs_1_, bf16[528,128]{1,0:T(8,128)(2,1)S(1)} %collective-permute-done.14.refs_2_, ...), custom_call_target="tpu_custom_call" | custom-call | tf_op jit(solution)/shard_map/pallas_call | solution.py:438
  66.8 2.0 %collective-permute-start.22 = (bf16[576,128]{1,0:T(8,128)(2,1)S(1)}, bf16[576,128]{1,0:T(8,128)(2,1)S(1)}, u32[]{:S(2)}, u32[]{:S(2)}) collective-permute-start(bf16[576,128]{1,0:T(8,128)(2,1)S(1)} %get-tuple-element.65), channel_id=1, source_target_pairs={{0,8},{8,0},{16,24},{24,16},{32,40},{40,32},{48,56},{56,48},{64,72... | collective-permute-start | bytes 442376 | tf_op jit(solution)/shard_map/ppermute | solution.py:578
  68.8 0.9 %shard_map.132 = (bf16[512,128]{1,0:T(8,128)(2,1)S(1)}, bf16[512,128]{1,0:T(8,128)(2,1)S(1)}, bf16[512,128]{1,0:T(8,128)(2,1)S(1)}, bf16[512,128]{1,0:T(8,128)(2,1)S(1)}) custom-call(bf16[528,128]{1,0:T(8,128)(2,1)S(1)} %get-tuple-element.58.pay_ref.refs_0_, bf16[512,1152]{1,0:T(8,128)(2,1)S(1)} %get-tuple-element.41.refs_5_.wslot_ref, ...), custom_call_target="tpu_custom_call" | custom-call | tf_op jit(solution)/shard_map/pallas_call | solution.py:438
  70.1 3.0 %collective-permute-start.28 = (bf16[512,128]{1,0:T(8,128)(2,1)S(1)}, bf16[512,128]{1,0:T(8,128)(2,1)S(1)}, u32[]{:S(2)}, u32[]{:S(2)}) collective-permute-start(bf16[512,128]{1,0:T(8,128)(2,1)S(1)} %get-tuple-element.73), channel_id=1, source_target_pairs={{0,3},{1,2},{2,1},{3,0},{4,7},{5,6},{6,5},{7,4},{8,11},{9,10},{10,... | collective-permute-start | bytes 393224 | tf_op jit(solution)/shard_map/ppermute | solution.py:465
  73.2 3.4 %collective-permute-start.23 = (bf16[144,128]{1,0:T(8,128)(2,1)S(1)}, bf16[144,128]{1,0:T(8,128)(2,1)S(1)}, u32[]{:S(2)}, u32[]{:S(2)}) collective-permute-start(bf16[144,128]{1,0:T(8,128)(2,1)S(1)} %get-tuple-element.67), channel_id=1, source_target_pairs={{0,16},{8,24},{16,32},{24,40},{32,48},{40,56},{48,0},{56,8},{64,80... | collective-permute-start | bytes 110600 | tf_op jit(solution)/shard_map/ppermute | solution.py:473
  76.5 4.5 %collective-permute-start.24 = (bf16[144,128]{1,0:T(8,128)(2,1)S(1)}, bf16[144,128]{1,0:T(8,128)(2,1)S(1)}, u32[]{:S(2)}, u32[]{:S(2)}) collective-permute-start(bf16[144,128]{1,0:T(8,128)(2,1)S(1)} %get-tuple-element.68), channel_id=1, source_target_pairs={{0,32},{8,40},{16,48},{24,56},{32,0},{40,8},{48,16},{56,24},{64,96... | collective-permute-start | bytes 110600 | tf_op jit(solution)/shard_map/ppermute | solution.py:473
  81.0 2.7 %collective-permute-start.25 = (bf16[144,128]{1,0:T(8,128)(2,1)S(1)}, bf16[144,128]{1,0:T(8,128)(2,1)S(1)}, u32[]{:S(2)}, u32[]{:S(2)}) collective-permute-start(bf16[144,128]{1,0:T(8,128)(2,1)S(1)} %get-tuple-element.69), channel_id=1, source_target_pairs={{0,48},{8,56},{16,0},{24,8},{32,16},{40,24},{48,32},{56,40},{64,11... | collective-permute-start | bytes 110600 | tf_op jit(solution)/shard_map/ppermute | solution.py:473
  84.4 1.5 %collective-permute-done.25.refs_3_ = bf16[144,128]{1,0:T(8,128)(2,1)S(1)} collective-permute-done((bf16[144,128]{1,0:T(8,128)(2,1)S(1)}, bf16[144,128]{1,0:T(8,128)(2,1)S(1)}, u32[]{:S(2)}, u32[]{:S(2)}) %collective-permute-start.25) | collective-permute-done | bytes 36896 | tf_op jit(solution)/shard_map/ppermute | solution.py:473
  85.9 0.8 shard_map.133
  (44 shorter events, 6.2 us)
Async XLA Ops:
  0.6 8.3 %copy-start.1 = (bf16[2,128,256]{2,1,0:T(8,128)(2,1)S(1)}, bf16[2,128,256]{2,1,0:T(8,128)(2,1)}, u32[]{:S(2)}) copy-start(bf16[2,128,256]{2,1,0:T(8,128)(2,1)} %refs_0_.1) | copy-start | bytes 393220
  0.6 5.5 %collective-permute-start.1 = (bf16[2,128,256]{2,1,0:T(8,128)(2,1)}, bf16[2,128,256]{2,1,0:T(8,128)(2,1)S(1)}, u32[]{:S(2)}, u32[]{:S(2)}) collective-permute-start(bf16[2,128,256]{2,1,0:T(8,128)(2,1)} %refs_0_.1), channel_id=1, source_target_pairs={{0,6},{1,7},{2,4},{3,5},{4,2},{5,3},{6,0},{7,1},{8,14},{9,15},{10,... | collective-permute-start | bytes 393224 | tf_op jit(solution)/shard_map/ppermute | solution.py:465
  1.3 7.6 %collective-permute-start = (bf16[2,128,256]{2,1,0:T(8,128)(2,1)}, bf16[2,128,256]{2,1,0:T(8,128)(2,1)S(1)}, u32[]{:S(2)}, u32[]{:S(2)}) collective-permute-start(bf16[2,128,256]{2,1,0:T(8,128)(2,1)} %refs_0_.1), channel_id=1, source_target_pairs={{0,1},{1,0},{2,3},{3,2},{4,5},{5,4},{6,7},{7,6},{8,9},{9,8},{10,11... | collective-permute-start | bytes 393224 | tf_op jit(solution)/shard_map/ppermute | solution.py:465
  6.2 2.7 %collective-permute-start.2 = (bf16[2,128,256]{2,1,0:T(8,128)(2,1)S(1)}, bf16[2,128,256]{2,1,0:T(8,128)(2,1)S(1)}, u32[]{:S(2)}, u32[]{:S(2)}) collective-permute-start(bf16[2,128,256]{2,1,0:T(8,128)(2,1)S(1)} %collective-permute-done.1.refs_2_), channel_id=1, source_target_pairs={{0,1},{1,0},{2,3},{3,2},{4,5},{5,4},{6,7},{7,6},{8,9},{9,8},{10,11... | collective-permute-start | bytes 393224 | tf_op jit(solution)/shard_map/ppermute | solution.py:465
  10.0 6.1 %collective-permute-start.5 = (bf16[528,128]{1,0:T(8,128)(2,1)S(1)}, bf16[528,128]{1,0:T(8,128)(2,1)S(1)}, u32[]{:S(2)}, u32[]{:S(2)}) collective-permute-start(bf16[528,128]{1,0:T(8,128)(2,1)S(1)} %get-tuple-element.45), channel_id=1, source_target_pairs={{0,6},{1,7},{2,4},{3,5},{4,2},{5,3},{6,0},{7,1},{8,14},{9,15},{10,... | collective-permute-start | bytes 405512 | tf_op jit(solution)/shard_map/ppermute | solution.py:465
  10.6 7.8 %collective-permute-start.3 = (bf16[528,128]{1,0:T(8,128)(2,1)S(1)}, bf16[528,128]{1,0:T(8,128)(2,1)S(1)}, u32[]{:S(2)}, u32[]{:S(2)}) collective-permute-start(bf16[528,128]{1,0:T(8,128)(2,1)S(1)} %get-tuple-element.45), channel_id=1, source_target_pairs={{0,4},{1,5},{2,6},{3,7},{4,0},{5,1},{6,2},{7,3},{8,12},{9,13},{10,... | collective-permute-start | bytes 405512 | tf_op jit(solution)/shard_map/ppermute | solution.py:465
  16.1 2.3 %collective-permute-start.6 = (bf16[528,128]{1,0:T(8,128)(2,1)S(1)}, bf16[528,128]{1,0:T(8,128)(2,1)S(1)}, u32[]{:S(2)}, u32[]{:S(2)}) collective-permute-start(bf16[528,128]{1,0:T(8,128)(2,1)S(1)} %collective-permute-done.5.refs_2_), channel_id=1, source_target_pairs={{0,1},{1,0},{2,3},{3,2},{4,5},{5,4},{6,7},{7,6},{8,9},{9,8},{10,11... | collective-permute-start | bytes 405512 | tf_op jit(solution)/shard_map/ppermute | solution.py:465
  18.4 1.4 %collective-permute-start.4 = (bf16[528,128]{1,0:T(8,128)(2,1)S(1)}, bf16[528,128]{1,0:T(8,128)(2,1)S(1)}, u32[]{:S(2)}, u32[]{:S(2)}) collective-permute-start(bf16[528,128]{1,0:T(8,128)(2,1)S(1)} %collective-permute-done.3.refs_0_), channel_id=1, source_target_pairs={{0,1},{1,0},{2,3},{3,2},{4,5},{5,4},{6,7},{7,6},{8,9},{9,8},{10,11... | collective-permute-start | bytes 405512 | tf_op jit(solution)/shard_map/ppermute | solution.py:465
  21.4 4.7 %collective-permute-start.9 = (f32[8,512]{1,0:T(8,128)S(1)}, f32[8,512]{1,0:T(8,128)S(1)}, u32[]{:S(2)}, u32[]{:S(2)}) collective-permute-start(f32[8,512]{1,0:T(8,128)S(1)} %get-tuple-element.46.own_ref), channel_id=1, source_target_pairs={{0,3},{1,2},{2,1},{3,0},{4,7},{5,6},{6,5},{7,4},{8,11},{9,10},{10,... | collective-permute-start | bytes 49160 | tf_op jit(solution)/shard_map/ppermute | solution.py:465
  23.6 5.2 %collective-permute-start.8 = (f32[8,512]{1,0:T(8,128)S(1)}, f32[8,512]{1,0:T(8,128)S(1)}, u32[]{:S(2)}, u32[]{:S(2)}) collective-permute-start(f32[8,512]{1,0:T(8,128)S(1)} %get-tuple-element.46.own_ref), channel_id=1, source_target_pairs={{0,2},{1,3},{2,0},{3,1},{4,6},{5,7},{6,4},{7,5},{8,10},{9,11},{10,... | collective-permute-start | bytes 49160 | tf_op jit(solution)/shard_map/ppermute | solution.py:465
  24.7 4.1 %collective-permute-start.7 = (f32[8,512]{1,0:T(8,128)S(1)}, f32[8,512]{1,0:T(8,128)S(1)}, u32[]{:S(2)}, u32[]{:S(2)}) collective-permute-start(f32[8,512]{1,0:T(8,128)S(1)} %get-tuple-element.46.own_ref), channel_id=1, source_target_pairs={{0,1},{1,0},{2,3},{3,2},{4,5},{5,4},{6,7},{7,6},{8,9},{9,8},{10,11... | collective-permute-start | bytes 49160 | tf_op jit(solution)/shard_map/ppermute | solution.py:465
  30.6 5.0 %collective-permute-start.10 = (bf16[1024,128]{1,0:T(8,128)(2,1)S(1)}, bf16[1024,128]{1,0:T(8,128)(2,1)S(1)}, u32[]{:S(2)}, u32[]{:S(2)}) collective-permute-start(bf16[1024,128]{1,0:T(8,128)(2,1)S(1)} %get-tuple-element.51), channel_id=1, source_target_pairs={{0,1},{1,0},{2,3},{3,2},{4,5},{5,4},{6,7},{7,6},{8,9},{9,8},{10,11... | collective-permute-start | bytes 786440 | tf_op jit(solution)/shard_map/ppermute | solution.py:465
  31.5 15.1 %collective-permute-start.18 = (bf16[272,512]{1,0:T(8,128)(2,1)S(1)}, bf16[272,512]{1,0:T(8,128)(2,1)S(1)}, u32[]{:S(2)}, u32[]{:S(2)}) collective-permute-start(bf16[272,512]{1,0:T(8,128)(2,1)S(1)} %get-tuple-element.63), channel_id=1, source_target_pairs={{0,192},{8,200},{16,208},{24,216},{32,224},{40,232},{48,240},{56,2... | collective-permute-start | bytes 835592 | tf_op jit(solution)/shard_map/ppermute | solution.py:468
  34.0 12.6 %collective-permute-start.17 = (bf16[272,512]{1,0:T(8,128)(2,1)S(1)}, bf16[272,512]{1,0:T(8,128)(2,1)S(1)}, u32[]{:S(2)}, u32[]{:S(2)}) collective-permute-start(bf16[272,512]{1,0:T(8,128)(2,1)S(1)} %get-tuple-element.63), channel_id=1, source_target_pairs={{0,128},{8,136},{16,144},{24,152},{32,160},{40,168},{48,176},{56,1... | collective-permute-start | bytes 835592 | tf_op jit(solution)/shard_map/ppermute | solution.py:468
  34.6 15.6 %collective-permute-start.16 = (bf16[272,512]{1,0:T(8,128)(2,1)S(1)}, bf16[272,512]{1,0:T(8,128)(2,1)S(1)}, u32[]{:S(2)}, u32[]{:S(2)}) collective-permute-start(bf16[272,512]{1,0:T(8,128)(2,1)S(1)} %get-tuple-element.63), channel_id=1, source_target_pairs={{0,64},{8,72},{16,80},{24,88},{32,96},{40,104},{48,112},{56,120},{... | collective-permute-start | bytes 835592 | tf_op jit(solution)/shard_map/ppermute | solution.py:468
  35.7 14.6 %collective-permute-start.11 = (bf16[544,128]{1,0:T(8,128)(2,1)S(1)}, bf16[544,128]{1,0:T(8,128)(2,1)S(1)}, u32[]{:S(2)}, u32[]{:S(2)}) collective-permute-start(bf16[544,128]{1,0:T(8,128)(2,1)S(1)} %get-tuple-element.53), channel_id=1, source_target_pairs={{0,4},{1,5},{2,6},{3,7},{4,0},{5,1},{6,2},{7,3},{8,12},{9,13},{10,... | collective-permute-start | bytes 417800 | tf_op jit(solution)/shard_map/ppermute | solution.py:465
  36.7 13.6 %collective-permute-start.12 = (bf16[512,128]{1,0:T(8,128)(2,1)S(1)}, bf16[512,128]{1,0:T(8,128)(2,1)S(1)}, u32[]{:S(2)}, u32[]{:S(2)}) collective-permute-start(bf16[512,128]{1,0:T(8,128)(2,1)S(1)} %get-tuple-element.54), channel_id=1, source_target_pairs={{0,6},{1,7},{2,4},{3,5},{4,2},{5,3},{6,0},{7,1},{8,14},{9,15},{10,... | collective-permute-start | bytes 393224 | tf_op jit(solution)/shard_map/ppermute | solution.py:465
  46.6 17.8 %collective-permute-start.21 = (bf16[272,512]{1,0:T(8,128)(2,1)S(1)}, bf16[272,512]{1,0:T(8,128)(2,1)S(1)}, u32[]{:S(2)}, u32[]{:S(2)}) collective-permute-start(bf16[272,512]{1,0:T(8,128)(2,1)S(1)} %collective-permute-done.18.refs_7_), channel_id=1, source_target_pairs={{0,1},{1,0},{2,3},{3,2},{4,5},{5,4},{6,7},{7,6},{8,9},{9,8},{10,11... | collective-permute-start | bytes 835592 | tf_op jit(solution)/shard_map/ppermute | solution.py:465
  46.6 17.8 %collective-permute-start.20 = (bf16[272,512]{1,0:T(8,128)(2,1)S(1)}, bf16[272,512]{1,0:T(8,128)(2,1)S(1)}, u32[]{:S(2)}, u32[]{:S(2)}) collective-permute-start(bf16[272,512]{1,0:T(8,128)(2,1)S(1)} %collective-permute-done.17.refs_6_), channel_id=1, source_target_pairs={{0,1},{1,0},{2,3},{3,2},{4,5},{5,4},{6,7},{7,6},{8,9},{9,8},{10,11... | collective-permute-start | bytes 835592 | tf_op jit(solution)/shard_map/ppermute | solution.py:465
  50.3 14.2 %collective-permute-start.19 = (bf16[272,512]{1,0:T(8,128)(2,1)S(1)}, bf16[272,512]{1,0:T(8,128)(2,1)S(1)}, u32[]{:S(2)}, u32[]{:S(2)}) collective-permute-start(bf16[272,512]{1,0:T(8,128)(2,1)S(1)} %collective-permute-done.16.refs_5_), channel_id=1, source_target_pairs={{0,1},{1,0},{2,3},{3,2},{4,5},{5,4},{6,7},{7,6},{8,9},{9,8},{10,11... | collective-permute-start | bytes 835592 | tf_op jit(solution)/shard_map/ppermute | solution.py:465
  50.3 14.1 %copy-start = (bf16[1,4608,128]{2,1,0:T(8,128)(2,1)S(1)}, bf16[1,4608,128]{2,1,0:T(8,128)(2,1)}, u32[]{:S(2)}) copy-start(bf16[1,4608,128]{2,1,0:T(8,128)(2,1)} %param.13) | copy-start | bytes 3538948
  51.7 6.5 %collective-permute-start.15 = (bf16[528,128]{1,0:T(8,128)(2,1)S(1)}, bf16[528,128]{1,0:T(8,128)(2,1)S(1)}, u32[]{:S(2)}, u32[]{:S(2)}) collective-permute-start(bf16[528,128]{1,0:T(8,128)(2,1)S(1)} %get-tuple-element.58.pay_ref.refs_0_), channel_id=1, source_target_pairs={{0,192},{8,200},{16,208},{24,216},{32,224},{40,232},{48,240},{56,2... | collective-permute-start | bytes 405512 | tf_op jit(solution)/shard_map/ppermute | solution.py:468
  52.3 7.2 %collective-permute-start.14 = (bf16[528,128]{1,0:T(8,128)(2,1)S(1)}, bf16[528,128]{1,0:T(8,128)(2,1)S(1)}, u32[]{:S(2)}, u32[]{:S(2)}) collective-permute-start(bf16[528,128]{1,0:T(8,128)(2,1)S(1)} %get-tuple-element.58.pay_ref.refs_0_), channel_id=1, source_target_pairs={{0,128},{8,136},{16,144},{24,152},{32,160},{40,168},{48,176},{56,1... | collective-permute-start | bytes 405512 | tf_op jit(solution)/shard_map/ppermute | solution.py:468
  58.2 6.2 %collective-permute-start.13 = (bf16[528,128]{1,0:T(8,128)(2,1)S(1)}, bf16[528,128]{1,0:T(8,128)(2,1)S(1)}, u32[]{:S(2)}, u32[]{:S(2)}) collective-permute-start(bf16[528,128]{1,0:T(8,128)(2,1)S(1)} %get-tuple-element.58.pay_ref.refs_0_), channel_id=1, source_target_pairs={{0,64},{8,72},{16,80},{24,88},{32,96},{40,104},{48,112},{56,120},{... | collective-permute-start | bytes 405512 | tf_op jit(solution)/shard_map/ppermute | solution.py:468
  66.8 6.3 %collective-permute-start.22 = (bf16[576,128]{1,0:T(8,128)(2,1)S(1)}, bf16[576,128]{1,0:T(8,128)(2,1)S(1)}, u32[]{:S(2)}, u32[]{:S(2)}) collective-permute-start(bf16[576,128]{1,0:T(8,128)(2,1)S(1)} %get-tuple-element.65), channel_id=1, source_target_pairs={{0,8},{8,0},{16,24},{24,16},{32,40},{40,32},{48,56},{56,48},{64,72... | collective-permute-start | bytes 442376 | tf_op jit(solution)/shard_map/ppermute | solution.py:578
  69.7 11.3 %collective-permute-start.26 = (bf16[512,128]{1,0:T(8,128)(2,1)S(1)}, bf16[512,128]{1,0:T(8,128)(2,1)S(1)}, u32[]{:S(2)}, u32[]{:S(2)}) collective-permute-start(bf16[512,128]{1,0:T(8,128)(2,1)S(1)} %get-tuple-element.71), channel_id=1, source_target_pairs={{0,1},{1,0},{2,3},{3,2},{4,5},{5,4},{6,7},{7,6},{8,9},{9,8},{10,11... | collective-permute-start | bytes 393224 | tf_op jit(solution)/shard_map/ppermute | solution.py:465
  69.8 13.9 %collective-permute-start.27 = (bf16[512,128]{1,0:T(8,128)(2,1)S(1)}, bf16[512,128]{1,0:T(8,128)(2,1)S(1)}, u32[]{:S(2)}, u32[]{:S(2)}) collective-permute-start(bf16[512,128]{1,0:T(8,128)(2,1)S(1)} %get-tuple-element.72), channel_id=1, source_target_pairs={{0,2},{1,3},{2,0},{3,1},{4,6},{5,7},{6,4},{7,5},{8,10},{9,11},{10,... | collective-permute-start | bytes 393224 | tf_op jit(solution)/shard_map/ppermute | solution.py:465
  70.1 13.6 %collective-permute-start.28 = (bf16[512,128]{1,0:T(8,128)(2,1)S(1)}, bf16[512,128]{1,0:T(8,128)(2,1)S(1)}, u32[]{:S(2)}, u32[]{:S(2)}) collective-permute-start(bf16[512,128]{1,0:T(8,128)(2,1)S(1)} %get-tuple-element.73), channel_id=1, source_target_pairs={{0,3},{1,2},{2,1},{3,0},{4,7},{5,6},{6,5},{7,4},{8,11},{9,10},{10,... | collective-permute-start | bytes 393224 | tf_op jit(solution)/shard_map/ppermute | solution.py:465
  73.2 10.5 %collective-permute-start.23 = (bf16[144,128]{1,0:T(8,128)(2,1)S(1)}, bf16[144,128]{1,0:T(8,128)(2,1)S(1)}, u32[]{:S(2)}, u32[]{:S(2)}) collective-permute-start(bf16[144,128]{1,0:T(8,128)(2,1)S(1)} %get-tuple-element.67), channel_id=1, source_target_pairs={{0,16},{8,24},{16,32},{24,40},{32,48},{40,56},{48,0},{56,8},{64,80... | collective-permute-start | bytes 110600 | tf_op jit(solution)/shard_map/ppermute | solution.py:473
  76.5 7.9 %collective-permute-start.24 = (bf16[144,128]{1,0:T(8,128)(2,1)S(1)}, bf16[144,128]{1,0:T(8,128)(2,1)S(1)}, u32[]{:S(2)}, u32[]{:S(2)}) collective-permute-start(bf16[144,128]{1,0:T(8,128)(2,1)S(1)} %get-tuple-element.68), channel_id=1, source_target_pairs={{0,32},{8,40},{16,48},{24,56},{32,0},{40,8},{48,16},{56,24},{64,96... | collective-permute-start | bytes 110600 | tf_op jit(solution)/shard_map/ppermute | solution.py:473
  81.0 4.9 %collective-permute-start.25 = (bf16[144,128]{1,0:T(8,128)(2,1)S(1)}, bf16[144,128]{1,0:T(8,128)(2,1)S(1)}, u32[]{:S(2)}, u32[]{:S(2)}) collective-permute-start(bf16[144,128]{1,0:T(8,128)(2,1)S(1)} %get-tuple-element.69), channel_id=1, source_target_pairs={{0,48},{8,56},{16,0},{24,8},{32,16},{40,24},{48,32},{56,40},{64,11... | collective-permute-start | bytes 110600 | tf_op jit(solution)/shard_map/ppermute | solution.py:473
where the time goes:
time: 87.4 us; the launch traced here: 86.7 us
  waiting for transfers between devices  39.3 us (45%)
  starting transfers between devices  31.9 us (36%)
  Pallas kernels  14.7 us (17%)
    ppermute x6, waiting for transfers between devices, over_y(): lax.ppermute(value, 'dp', [(y * 8 + z, (y + d) % 4 * 8 + z) for y in rang...  22.9 us
    pallas_call x13, Pallas kernels, call(): pl.pallas_call(kernel, out_shape=[jax.ShapeDtypeStruct(*o[:2]) if len(o)...  14.7 us
    ppermute x19, waiting for transfers between devices, across(): return lax.ppermute(value, ('segment', 'chan'), links)  14.1 us
    ppermute x19, starting transfers between devices, across(): return lax.ppermute(value, ('segment', 'chan'), links)  13.9 us
    ppermute x3, starting transfers between devices, over_z(): lax.ppermute(value, 'dp', [(y * 8 + z, y * 8 + (z + d) % 8) for y in rang...  10.5 us
    ppermute x6, starting transfers between devices, over_y(): lax.ppermute(value, 'dp', [(y * 8 + z, (y + d) % 4 * 8 + z) for y in rang...  5.46 us
    ppermute x3, waiting for transfers between devices, over_z(): lax.ppermute(value, 'dp', [(y * 8 + z, y * 8 + (z + d) % 8) for y in rang...  2.21 us
    ppermute x1, starting transfers between devices, body(): z_got = lax.ppermute(z_send, 'dp', [(n, n ^ 1) for n in range(32)])  2 us
  transfers between devices with their start and end apart: 29, of which 13 were waited for; matrix products, arithmetic and copies ran while one was open for 0% of the time, Pallas kernels for 8%

commit v1 on v0

--- a/solution.py
+++ b/solution.py
@@ -361,24 +361,34 @@
     )
 
 
+def add_half_rows(taps, near, far, core, before_ref, after_ref):
+    half = near[0].shape[0] - EXTRA
+    for group, where in ((near, core), (far, 1 - core)):
+        part = None
+        for ref, tap in zip(group, taps):
+            more = jnp.dot(ref[:half, :], tap, preferred_element_type=f32)
+            part = more if part is None else part + more
+        at = pl.ds(pl.multiple_of(where * half, half), half)
+        after_ref[at, :] = before_ref[at, :] + part
+
+
+def near_weight_kernel(idx, p1_ref, p3_ref, n1_ref, n3_ref, f1_ref, f3_ref, before_ref, acc_ref, g_ref):
+    taps = [taps_of(ref, idx[2], g_ref.at[n]) for n, ref in enumerate((p1_ref, p3_ref))]
+    add_half_rows(taps, (n1_ref, n3_ref), (f1_ref, f3_ref), idx[1] & 1, before_ref, acc_ref)
+
+
 def weight_kernel(idx, *refs):
-    pays, own_ref, near, far, w_ref, first_ref = refs[:4], refs[4], refs[5:8], refs[8:11], refs[11], refs[12]
-    keep_ref, send_ref = refs[13:15]
-    g_ref, acc_ref, sum_ref = refs[15:18]
+    pays, own_ref, near, far_ref, w_ref, before_ref = refs[:4], refs[4], refs[5:8], refs[8], refs[9], refs[10]
+    keep_ref, send_ref = refs[11:13]
+    g_ref, acc_ref, sum_ref = refs[13:16]
     core, y, z = idx[1] & 1, idx[2], idx[3]
     full = own_ref.shape[0] - EXTRA
     half = full // 2
     own = pays[0].shape[1]
     pixels = pays[0].shape[0] - EXTRA
     count = pixels // PIX
-    rest = [taps_of(pays[n], y, g_ref.at[n - 1]) for n in (1, 2, 3)]
-    for refs_, where in ((near, core), (far, 1 - core)):
-        part = None
-        for ref, taps in zip(refs_, rest):
-            more = jnp.dot(ref[:half, :], taps, preferred_element_type=f32)
-            part = more if part is None else part + more
-        at = pl.ds(pl.multiple_of(where * half, half), half)
-        acc_ref[at, :] = first_ref[at, :] + part
+    taps = taps_of(pays[2], y, g_ref)
+    add_half_rows((taps,), (near[1],), (far_ref,), core, before_ref, acc_ref)
     sty_rows, coef_rows = [], []
     for n in range(4):
         tail = own_ref[full:, :] if n == 0 else near[n - 1][half:, :]
@@ -398,7 +408,7 @@
         )
     rows = keep_ref.shape[0] // 4
     for e in range(4):
-        for ref, first in ((keep_ref, z), (send_ref, z ^ 1)):
+        for ref, first in ((keep_ref, z), (send_ref, ((z + core) ^ 1) - core)):
             start = y * own + ((first + 2 * e) & 7) * rows
             block = sum_ref[pl.ds(pl.multiple_of(start, RES), rows), :]
             ref[e * rows : (e + 1) * rows, :] = block.astype(ref.dtype)
@@ -464,10 +474,17 @@
     def across(value, links):
         return lax.ppermute(value, ("segment", "chan"), links)
 
+    def by_core(value, place):
+        links = []
+        for y in range(4):
+            for z in range(8):
+                for c in range(4):
+                    to_y, to_z = place(y, z, c % 2)
+                    links.append(((y * 8 + z) * 4 + c, (to_y % 4 * 8 + to_z % 8) * 4 + c))
+        return lax.ppermute(value, ("dp", "chan"), links)
+
     def over_y(value, d):
-        return lax.ppermute(
-            value, "dp", [(y * 8 + z, (y + d) % 4 * 8 + z) for y in range(4) for z in range(8)]
-        )
+        return by_core(value, lambda y, z, core: (y - d if core else y + d, z))
 
     def over_z(value, d):
         return lax.ppermute(
@@ -532,8 +549,12 @@
         scalars=1,
     )
     (image_first,) = call(first_image_kernel, [((8, pixels), f32)], [y0, y1, y2, y3])
-    near = [over_y(xm_half, d) for d in (1, 2, 3)]
-    far = [within(near[n], 1) for n in range(3)]
+    near_1 = over_y(xm_half, 1)
+    near_3 = over_y(xm_half, 3)
+    near_2 = over_y(near_1, 1)
+    far_1 = within(near_3, 1)
+    far_3 = within(near_1, 1)
+    far_2 = within(near_2, 1)
     two = (2 * pixels, own)
     tail, pay_b, dx_keep, dx_send = call(
         disc_kernel,
@@ -552,7 +573,9 @@
         [idx, *got, rgbp, slope_a, z_a, demod, pay_b, tail],
         scalars=1,
     )
-    pays = [pay_g] + [over_y(pay_g, d) for d in (1, 2, 3)]
+    pay_1 = over_y(pay_g, 1)
+    pay_3 = over_y(pay_g, 3)
+    pay_2 = over_y(pay_1, 1)
     shares = call(share_kernel, [share] * 4, [pay_g, wslot, stys])
     mine = [shares[0]] + [within(shares[d], d) for d in (1, 2, 3)]
     rows = weight.shape[0] // 32
@@ -564,18 +587,25 @@
         scratch=[pltpu.VMEM(taps, bf16)],
         scalars=1,
     )
+    (second,) = call(
+        near_weight_kernel,
+        [((full, 3 * own), f32)],
+        [idx, pay_1, pay_3, near_1, near_3, far_1, far_3, first],
+        scratch=[pltpu.VMEM((2, *taps), bf16)],
+        scalars=1,
+    )
     z_keep, z_send = call(
         weight_kernel,
         [((4 * rows, own), f32), ((4 * rows, own), bf16)],
-        [idx, *pays, xm, *near, *far, weight, first],
+        [idx, pay_g, pay_1, pay_2, pay_3, xm, near_1, near_2, near_3, far_2, weight, second],
         scratch=[
-            pltpu.VMEM((3, *taps), bf16),
+            pltpu.VMEM(taps, bf16),
             pltpu.VMEM((full, 3 * own), f32),
             pltpu.VMEM((3 * full, own), f32),
         ],
         scalars=1,
     )
-    z_got = lax.ppermute(z_send, "dp", [(n, n ^ 1) for n in range(32)])
+    z_got = by_core(z_send, lambda y, z, core: (y, ((z + core) ^ 1) - core))
     block = (rows, own)
     z_own, *z_outs = call(z_pair_kernel, [(block, f32)] + [(block, bf16)] * 3, [z_keep, z_got])
     parts = [z_own] + [over_z(z_outs[e - 1], 2 * e) for e in (1, 2, 3)]

time: 87.4 us -> 81.9 us (0.937)
  waiting for transfers between devices: 39.3 us -> 31.2 us
  starting transfers between devices: 31.9 us -> 33.1 us
    ppermute x7, waiting for transfers between devices: 22.9 us -> 14 us  [by_core(): return lax.ppermute(value, ('dp', 'chan'), links)]
    ppermute x19, starting transfers between devices: 13.9 us -> 15 us  [across(): return lax.ppermute(value, ('segment', 'chan'), links)]
    ppermute x19, waiting for transfers between devices: 14.1 us -> 15.1 us  [across(): return lax.ppermute(value, ('segment', 'chan'), links)]
    pallas_call x13 -> x14, Pallas kernels: 14.7 us -> 15.3 us  [call(): pl.pallas_call(kernel, out_shape=[jax.ShapeDtypeStruct(*o[:2]) if len(o)...]
  transfers between devices with their start and end apart: 29 -> 29, of which waited for: 13 -> 12; matrix products, arithmetic and copies ran while one was open for 0% -> 0% of each run, Pallas kernels for 8% -> 12%
where the time goes in v1:
time: 81.9 us; the launch traced here: 80.6 us
  starting transfers between devices  33.1 us (40%)
  waiting for transfers between devices  31.2 us (38%)
  Pallas kernels  15.3 us (19%)
  between operations  0.82 us (1%)
    pallas_call x14, Pallas kernels, call(): pl.pallas_call(kernel, out_shape=[jax.ShapeDtypeStruct(*o[:2]) if len(o)...  15.3 us
    ppermute x19, waiting for transfers between devices, across(): return lax.ppermute(value, ('segment', 'chan'), links)  15.1 us
    ppermute x19, starting transfers between devices, across(): return lax.ppermute(value, ('segment', 'chan'), links)  15 us
    ppermute x7, waiting for transfers between devices, by_core(): return lax.ppermute(value, ('dp', 'chan'), links)  14 us
    ppermute x3, starting transfers between devices, over_z(): lax.ppermute(value, 'dp', [(y * 8 + z, y * 8 + (z + d) % 8) for y in rang...  10.5 us
    ppermute x7, starting transfers between devices, by_core(): return lax.ppermute(value, ('dp', 'chan'), links)  7.64 us
    ppermute x3, waiting for transfers between devices, over_z(): lax.ppermute(value, 'dp', [(y * 8 + z, y * 8 + (z + d) % 8) for y in rang...  2.21 us
  transfers between devices with their start and end apart: 29, of which 12 were waited for; matrix products, arithmetic and copies ran while one was open for 0% of the time, Pallas kernels for 12%

profile of v1, /device:TPU:4, one launch (start us, length us, event | category | flops | bytes accessed | tf_op | source)
XLA Modules:
  0.0 80.6 jit_solution(6760489869528837699)
XLA Ops:
  1.3 4.9 %collective-permute-done.1.refs_2_ = bf16[2,128,256]{2,1,0:T(8,128)(2,1)S(1)} collective-permute-done((bf16[2,128,256]{2,1,0:T(8,128)(2,1)}, bf16[2,128,256]{2,1,0:T(8,128)(2,1)S(1)}, u32[]{:S(2)}, u32[]{:S(2)}) %collective-permute-start.1) | collective-permute-done | bytes 131104 | tf_op jit(solution)/shard_map/ppermute | solution.py:475
  6.3 2.6 %shard_map.121 = (bf16[512,1152]{1,0:T(8,128)(2,1)S(1)}, f32[2,512]{1,0:T(2,128)S(1)}, f32[2,128]{1,0:T(2,128)S(1)}, f32[512,128]{1,0:T(8,128)S(1)}, f32[5,256,1...) custom-call(s32[4]{0:T(128)S(1)} %pad_add_fusion.idx, bf16[4608,128]{1,0:T(8,128)(2,1)} %bitcast.12, ...), custom_call_target="tpu_custom_call" | custom-call | tf_op jit(solution)/shard_map/pallas_call | solution.py:448
  8.9 1.1 %shard_map.122 = (bf16[528,128]{1,0:T(8,128)(2,1)S(1)}, f32[512,128]{1,0:T(8,128)S(1)}, f32[512,128]{1,0:T(8,128)S(1)}, bf16[512,512]{1,0:T(8,128)(2,1)S(1)}) custom-call(bf16[2,128,256]{2,1,0:T(8,128)(2,1)S(1)} %copy-done.1, bf16[2,128,256]{2,1,0:T(8,128)(2,1)S(1)} %collective-permute-done.refs_1_, bf16[2,128,256]{2,1,0:T(8,128)(2,1)S(1)} %collective-permute-done.1.refs_2_, ...), custom_call_target="tpu_custom_call" | custom-call | tf_op jit(solution)/shard_map/pallas_call | solution.py:448
  10.6 3.8 %collective-permute-start.3 = (bf16[528,128]{1,0:T(8,128)(2,1)S(1)}, bf16[528,128]{1,0:T(8,128)(2,1)S(1)}, u32[]{:S(2)}, u32[]{:S(2)}) collective-permute-start(bf16[528,128]{1,0:T(8,128)(2,1)S(1)} %get-tuple-element.45), channel_id=1, source_target_pairs={{0,4},{1,5},{2,6},{3,7},{4,0},{5,1},{6,2},{7,3},{8,12},{9,13},{10,... | collective-permute-start | bytes 405512 | tf_op jit(solution)/shard_map/ppermute | solution.py:475
  14.4 1.7 %collective-permute-done.5.refs_2_ = bf16[528,128]{1,0:T(8,128)(2,1)S(1)} collective-permute-done((bf16[528,128]{1,0:T(8,128)(2,1)S(1)}, bf16[528,128]{1,0:T(8,128)(2,1)S(1)}, u32[]{:S(2)}, u32[]{:S(2)}) %collective-permute-start.5) | collective-permute-done | bytes 135200 | tf_op jit(solution)/shard_map/ppermute | solution.py:475
  16.1 2.3 %collective-permute-done.3.refs_0_ = bf16[528,128]{1,0:T(8,128)(2,1)S(1)} collective-permute-done((bf16[528,128]{1,0:T(8,128)(2,1)S(1)}, bf16[528,128]{1,0:T(8,128)(2,1)S(1)}, u32[]{:S(2)}, u32[]{:S(2)}) %collective-permute-start.3) | collective-permute-done | bytes 135200 | tf_op jit(solution)/shard_map/ppermute | solution.py:475
  18.4 1.3 %collective-permute-done.4.refs_1_ = bf16[528,128]{1,0:T(8,128)(2,1)S(1)} collective-permute-done((bf16[528,128]{1,0:T(8,128)(2,1)S(1)}, bf16[528,128]{1,0:T(8,128)(2,1)S(1)}, u32[]{:S(2)}, u32[]{:S(2)}) %collective-permute-start.4) | collective-permute-done | bytes 135200 | tf_op jit(solution)/shard_map/ppermute | solution.py:475
  19.8 1.7 %shard_map.123 = (bf16[528,128]{1,0:T(8,128)(2,1)}, f32[512,128]{1,0:T(8,128)S(1)}, f32[512,128]{1,0:T(8,128)S(1)}, bf16[512,512]{1,0:T(8,128)(2,1)S(1)}, f32[8,512]{1,0:T(8,128)S(1)}) custom-call(bf16[528,128]{1,0:T(8,128)(2,1)S(1)} %collective-permute-done.3.refs_0_, bf16[528,128]{1,0:T(8,128)(2,1)S(1)} %collective-permute-done.4.refs_1_, ...), custom_call_target="tpu_custom_call" | custom-call | tf_op jit(solution)/shard_map/pallas_call | solution.py:448
  22.4 4.2 %collective-permute-start.9 = (f32[8,512]{1,0:T(8,128)S(1)}, f32[8,512]{1,0:T(8,128)S(1)}, u32[]{:S(2)}, u32[]{:S(2)}) collective-permute-start(f32[8,512]{1,0:T(8,128)S(1)} %get-tuple-element.46.own_ref), channel_id=1, source_target_pairs={{0,3},{1,2},{2,1},{3,0},{4,7},{5,6},{6,5},{7,4},{8,11},{9,10},{10,... | collective-permute-start | bytes 49160 | tf_op jit(solution)/shard_map/ppermute | solution.py:475
  27.1 1.0 %collective-permute-done.9.r3_ref = f32[8,512]{1,0:T(8,128)S(1)} collective-permute-done((f32[8,512]{1,0:T(8,128)S(1)}, f32[8,512]{1,0:T(8,128)S(1)}, u32[]{:S(2)}, u32[]{:S(2)}) %collective-permute-start.9) | collective-permute-done | bytes 16416 | tf_op jit(solution)/shard_map/ppermute | solution.py:475
  28.1 3.8 %collective-permute-done.8.r2_ref = f32[8,512]{1,0:T(8,128)S(1)} collective-permute-done((f32[8,512]{1,0:T(8,128)S(1)}, f32[8,512]{1,0:T(8,128)S(1)}, u32[]{:S(2)}, u32[]{:S(2)}) %collective-permute-start.8) | collective-permute-done | bytes 16416 | tf_op jit(solution)/shard_map/ppermute | solution.py:475
  31.9 1.7 %shard_map.125 = (bf16[32,128]{1,0:T(8,128)(2,1)S(1)}, bf16[528,128]{1,0:T(8,128)(2,1)S(1)}, f32[1024,128]{1,0:T(8,128)S(1)}, bf16[1024,128]{1,0:T(8,128)(2,1)S(1)}) custom-call(f32[8,512]{1,0:T(8,128)S(1)} %get-tuple-element.46.own_ref, f32[8,512]{1,0:T(8,128)S(1)} %collective-permute-done.7.r1_ref, f32[8,512]{1,0:T(8,128)S(1)} %collective-permute-done.8.r2_ref, ...), custom_call_target="tpu_custom_call" | custom-call | tf_op jit(solution)/shard_map/pallas_call | solution.py:448
  33.7 0.8 %collective-permute-start.18 = (bf16[272,512]{1,0:T(8,128)(2,1)S(1)}, bf16[272,512]{1,0:T(8,128)(2,1)S(1)}, u32[]{:S(2)}, u32[]{:S(2)}) collective-permute-start(bf16[272,512]{1,0:T(8,128)(2,1)S(1)} %get-tuple-element.63), channel_id=1, source_target_pairs={{0,192},{1,65},{2,194},{3,67},{8,200},{9,73},{10,202},{11,75},{16,... | collective-permute-start | bytes 835592 | tf_op jit(solution)/shard_map/ppermute | solution.py:484
  34.6 1.3 %collective-permute-start.17 = (bf16[272,512]{1,0:T(8,128)(2,1)S(1)}, bf16[272,512]{1,0:T(8,128)(2,1)S(1)}, u32[]{:S(2)}, u32[]{:S(2)}) collective-permute-start(bf16[272,512]{1,0:T(8,128)(2,1)S(1)} %collective-permute-done.16.n1_ref.refs_5_), channel_id=1, source_target_pairs={{0,64},{1,193},{2,66},{3,195},{8,72},{9,201},{10,74},{11,203},{16,... | collective-permute-start | bytes 835592 | tf_op jit(solution)/shard_map/ppermute | solution.py:484
  35.9 1.0 %collective-permute-start.11 = (bf16[544,128]{1,0:T(8,128)(2,1)S(1)}, bf16[544,128]{1,0:T(8,128)(2,1)S(1)}, u32[]{:S(2)}, u32[]{:S(2)}) collective-permute-start(bf16[544,128]{1,0:T(8,128)(2,1)S(1)} %get-tuple-element.53), channel_id=1, source_target_pairs={{0,4},{1,5},{2,6},{3,7},{4,0},{5,1},{6,2},{7,3},{8,12},{9,13},{10,... | collective-permute-start | bytes 417800 | tf_op jit(solution)/shard_map/ppermute | solution.py:475
  37.4 5.4 %collective-permute-done.18.n3_ref.refs_7_ = bf16[272,512]{1,0:T(8,128)(2,1)S(1)} collective-permute-done((bf16[272,512]{1,0:T(8,128)(2,1)S(1)}, bf16[272,512]{1,0:T(8,128)(2,1)S(1)}, u32[]{:S(2)}, u32[]{:S(2)}) %collective-permute-start.18) | collective-permute-done | bytes 278560 | tf_op jit(solution)/shard_map/ppermute | solution.py:484
  44.0 1.4 %shard_map.127 = (bf16[528,128]{1,0:T(8,128)(2,1)S(1)}, f32[2]{0:T(128)}) custom-call(s32[4]{0:T(128)S(1)} %pad_add_fusion.idx, bf16[544,128]{1,0:T(8,128)(2,1)S(1)} %collective-permute-done.11.s0_ref, bf16[512,128]{1,0:T(8,128)(2,1)S(1)} %collective-permute-done.12.s1_ref, bf16[16,128]{1,0:T(8,128)(2,1)S(1)} %get-tuple-element.44.refs_8_.rgb_ref, ...), custom_call_target="tpu_custom_call" | custom-call | tf_op jit(solution)/shard_map/pallas_call | solution.py:448
  45.5 3.2 %collective-permute-start.15 = (bf16[528,128]{1,0:T(8,128)(2,1)S(1)}, bf16[528,128]{1,0:T(8,128)(2,1)S(1)}, u32[]{:S(2)}, u32[]{:S(2)}) collective-permute-start(bf16[528,128]{1,0:T(8,128)(2,1)S(1)} %get-tuple-element.58.pay_ref.refs_0_), channel_id=1, source_target_pairs={{0,192},{1,65},{2,194},{3,67},{8,200},{9,73},{10,202},{11,75},{16,... | collective-permute-start | bytes 405512 | tf_op jit(solution)/shard_map/ppermute | solution.py:484
  48.7 4.3 %collective-permute-done.13.p1_ref.refs_1_ = bf16[528,128]{1,0:T(8,128)(2,1)S(1)} collective-permute-done((bf16[528,128]{1,0:T(8,128)(2,1)S(1)}, bf16[528,128]{1,0:T(8,128)(2,1)S(1)}, u32[]{:S(2)}, u32[]{:S(2)}) %collective-permute-start.13) | collective-permute-done | bytes 135200 | tf_op jit(solution)/shard_map/ppermute | solution.py:484
  53.0 1.1 %shard_map.129.before_ref = f32[512,384]{1,0:T(8,128)S(1)} custom-call(s32[4]{0:T(128)S(1)} %pad_add_fusion.idx, bf16[528,128]{1,0:T(8,128)(2,1)S(1)} %get-tuple-element.58.pay_ref.refs_0_, bf16[528,512]{1,0:T(8,128)(2,1)S(1)} %get-tuple-element.62.own_ref.refs_4_), custom_call_target="tpu_custom_call" | custom-call | tf_op jit(solution)/shard_map/pallas_call | solution.py:448
  54.2 1.5 %shard_map.130.refs_10_ = f32[512,384]{1,0:T(8,128)S(1)} custom-call(s32[4]{0:T(128)S(1)} %pad_add_fusion.idx, bf16[528,128]{1,0:T(8,128)(2,1)S(1)} %collective-permute-done.13.p1_ref.refs_1_, bf16[528,128]{1,0:T(8,128)(2,1)S(1)} %collective-permute-done.15.p3_ref.refs_3_, bf16[272,512]{1,0:T(8,128)(2,1)S(1)} %collective-permute-done.16.n1_ref.refs_5_, ...), custom_call_target="tpu_custom_call" | custom-call | tf_op jit(solution)/shard_map/pallas_call | solution.py:448
  55.7 3.5 %collective-permute-done.14.refs_2_ = bf16[528,128]{1,0:T(8,128)(2,1)S(1)} collective-permute-done((bf16[528,128]{1,0:T(8,128)(2,1)S(1)}, bf16[528,128]{1,0:T(8,128)(2,1)S(1)}, u32[]{:S(2)}, u32[]{:S(2)}) %collective-permute-start.14) | collective-permute-done | bytes 135200 | tf_op jit(solution)/shard_map/ppermute | solution.py:484
  59.2 1.5 %shard_map.131 = (f32[576,128]{1,0:T(8,128)S(1)}, bf16[576,128]{1,0:T(8,128)(2,1)S(1)}) custom-call(s32[4]{0:T(128)S(1)} %pad_add_fusion.idx, bf16[528,128]{1,0:T(8,128)(2,1)S(1)} %get-tuple-element.58.pay_ref.refs_0_, bf16[528,128]{1,0:T(8,128)(2,1)S(1)} %collective-permute-done.13.p1_ref.refs_1_, bf16[528,128]{1,0:T(8,128)(2,1)S(1)} %collective-permute-done.14.refs_2_, ...), custom_call_target="tpu_custom_call" | custom-call | tf_op jit(solution)/shard_map/pallas_call | solution.py:448
  60.7 2.0 %collective-permute-start.22 = (bf16[576,128]{1,0:T(8,128)(2,1)S(1)}, bf16[576,128]{1,0:T(8,128)(2,1)S(1)}, u32[]{:S(2)}, u32[]{:S(2)}) collective-permute-start(bf16[576,128]{1,0:T(8,128)(2,1)S(1)} %get-tuple-element.65), channel_id=1, source_target_pairs={{0,8},{1,57},{2,10},{3,59},{8,0},{9,17},{10,2},{11,19},{16,24},{17... | collective-permute-start | bytes 442376 | tf_op jit(solution)/shard_map/ppermute | solution.py:484
  62.7 0.9 %shard_map.133 = (bf16[512,128]{1,0:T(8,128)(2,1)S(1)}, bf16[512,128]{1,0:T(8,128)(2,1)S(1)}, bf16[512,128]{1,0:T(8,128)(2,1)S(1)}, bf16[512,128]{1,0:T(8,128)(2,1)S(1)}) custom-call(bf16[528,128]{1,0:T(8,128)(2,1)S(1)} %get-tuple-element.58.pay_ref.refs_0_, bf16[512,1152]{1,0:T(8,128)(2,1)S(1)} %get-tuple-element.41.refs_5_.wslot_ref, ...), custom_call_target="tpu_custom_call" | custom-call | tf_op jit(solution)/shard_map/pallas_call | solution.py:448
  63.7 1.4 %collective-permute-start.27 = (bf16[512,128]{1,0:T(8,128)(2,1)S(1)}, bf16[512,128]{1,0:T(8,128)(2,1)S(1)}, u32[]{:S(2)}, u32[]{:S(2)}) collective-permute-start(bf16[512,128]{1,0:T(8,128)(2,1)S(1)} %get-tuple-element.72), channel_id=1, source_target_pairs={{0,2},{1,3},{2,0},{3,1},{4,6},{5,7},{6,4},{7,5},{8,10},{9,11},{10,... | collective-permute-start | bytes 393224 | tf_op jit(solution)/shard_map/ppermute | solution.py:475
  65.1 2.0 %collective-permute-start.28 = (bf16[512,128]{1,0:T(8,128)(2,1)S(1)}, bf16[512,128]{1,0:T(8,128)(2,1)S(1)}, u32[]{:S(2)}, u32[]{:S(2)}) collective-permute-start(bf16[512,128]{1,0:T(8,128)(2,1)S(1)} %get-tuple-element.73), channel_id=1, source_target_pairs={{0,3},{1,2},{2,1},{3,0},{4,7},{5,6},{6,5},{7,4},{8,11},{9,10},{10,... | collective-permute-start | bytes 393224 | tf_op jit(solution)/shard_map/ppermute | solution.py:475
  67.1 3.3 %collective-permute-start.23 = (bf16[144,128]{1,0:T(8,128)(2,1)S(1)}, bf16[144,128]{1,0:T(8,128)(2,1)S(1)}, u32[]{:S(2)}, u32[]{:S(2)}) collective-permute-start(bf16[144,128]{1,0:T(8,128)(2,1)S(1)} %get-tuple-element.67), channel_id=1, source_target_pairs={{0,16},{8,24},{16,32},{24,40},{32,48},{40,56},{48,0},{56,8},{64,80... | collective-permute-start | bytes 110600 | tf_op jit(solution)/shard_map/ppermute | solution.py:490
  70.4 4.5 %collective-permute-start.24 = (bf16[144,128]{1,0:T(8,128)(2,1)S(1)}, bf16[144,128]{1,0:T(8,128)(2,1)S(1)}, u32[]{:S(2)}, u32[]{:S(2)}) collective-permute-start(bf16[144,128]{1,0:T(8,128)(2,1)S(1)} %get-tuple-element.68), channel_id=1, source_target_pairs={{0,32},{8,40},{16,48},{24,56},{32,0},{40,8},{48,16},{56,24},{64,96... | collective-permute-start | bytes 110600 | tf_op jit(solution)/shard_map/ppermute | solution.py:490
  74.9 2.7 %collective-permute-start.25 = (bf16[144,128]{1,0:T(8,128)(2,1)S(1)}, bf16[144,128]{1,0:T(8,128)(2,1)S(1)}, u32[]{:S(2)}, u32[]{:S(2)}) collective-permute-start(bf16[144,128]{1,0:T(8,128)(2,1)S(1)} %get-tuple-element.69), channel_id=1, source_target_pairs={{0,48},{8,56},{16,0},{24,8},{32,16},{40,24},{48,32},{56,40},{64,11... | collective-permute-start | bytes 110600 | tf_op jit(solution)/shard_map/ppermute | solution.py:490
  78.3 1.5 %collective-permute-done.25.refs_3_ = bf16[144,128]{1,0:T(8,128)(2,1)S(1)} collective-permute-done((bf16[144,128]{1,0:T(8,128)(2,1)S(1)}, bf16[144,128]{1,0:T(8,128)(2,1)S(1)}, u32[]{:S(2)}, u32[]{:S(2)}) %collective-permute-start.25) | collective-permute-done | bytes 36896 | tf_op jit(solution)/shard_map/ppermute | solution.py:490
  79.8 0.8 shard_map.134
  (45 shorter events, 5.5 us)
Async XLA Ops:
  0.6 8.3 %copy-start.1 = (bf16[2,128,256]{2,1,0:T(8,128)(2,1)S(1)}, bf16[2,128,256]{2,1,0:T(8,128)(2,1)}, u32[]{:S(2)}) copy-start(bf16[2,128,256]{2,1,0:T(8,128)(2,1)} %refs_0_.1) | copy-start | bytes 393220
  0.6 5.5 %collective-permute-start.1 = (bf16[2,128,256]{2,1,0:T(8,128)(2,1)}, bf16[2,128,256]{2,1,0:T(8,128)(2,1)S(1)}, u32[]{:S(2)}, u32[]{:S(2)}) collective-permute-start(bf16[2,128,256]{2,1,0:T(8,128)(2,1)} %refs_0_.1), channel_id=1, source_target_pairs={{0,6},{1,7},{2,4},{3,5},{4,2},{5,3},{6,0},{7,1},{8,14},{9,15},{10,... | collective-permute-start | bytes 393224 | tf_op jit(solution)/shard_map/ppermute | solution.py:475
  1.3 7.6 %collective-permute-start = (bf16[2,128,256]{2,1,0:T(8,128)(2,1)}, bf16[2,128,256]{2,1,0:T(8,128)(2,1)S(1)}, u32[]{:S(2)}, u32[]{:S(2)}) collective-permute-start(bf16[2,128,256]{2,1,0:T(8,128)(2,1)} %refs_0_.1), channel_id=1, source_target_pairs={{0,1},{1,0},{2,3},{3,2},{4,5},{5,4},{6,7},{7,6},{8,9},{9,8},{10,11... | collective-permute-start | bytes 393224 | tf_op jit(solution)/shard_map/ppermute | solution.py:475
  6.2 2.7 %collective-permute-start.2 = (bf16[2,128,256]{2,1,0:T(8,128)(2,1)S(1)}, bf16[2,128,256]{2,1,0:T(8,128)(2,1)S(1)}, u32[]{:S(2)}, u32[]{:S(2)}) collective-permute-start(bf16[2,128,256]{2,1,0:T(8,128)(2,1)S(1)} %collective-permute-done.1.refs_2_), channel_id=1, source_target_pairs={{0,1},{1,0},{2,3},{3,2},{4,5},{5,4},{6,7},{7,6},{8,9},{9,8},{10,11... | collective-permute-start | bytes 393224 | tf_op jit(solution)/shard_map/ppermute | solution.py:475
  10.0 6.1 %collective-permute-start.5 = (bf16[528,128]{1,0:T(8,128)(2,1)S(1)}, bf16[528,128]{1,0:T(8,128)(2,1)S(1)}, u32[]{:S(2)}, u32[]{:S(2)}) collective-permute-start(bf16[528,128]{1,0:T(8,128)(2,1)S(1)} %get-tuple-element.45), channel_id=1, source_target_pairs={{0,6},{1,7},{2,4},{3,5},{4,2},{5,3},{6,0},{7,1},{8,14},{9,15},{10,... | collective-permute-start | bytes 405512 | tf_op jit(solution)/shard_map/ppermute | solution.py:475
  10.6 7.8 %collective-permute-start.3 = (bf16[528,128]{1,0:T(8,128)(2,1)S(1)}, bf16[528,128]{1,0:T(8,128)(2,1)S(1)}, u32[]{:S(2)}, u32[]{:S(2)}) collective-permute-start(bf16[528,128]{1,0:T(8,128)(2,1)S(1)} %get-tuple-element.45), channel_id=1, source_target_pairs={{0,4},{1,5},{2,6},{3,7},{4,0},{5,1},{6,2},{7,3},{8,12},{9,13},{10,... | collective-permute-start | bytes 405512 | tf_op jit(solution)/shard_map/ppermute | solution.py:475
  16.1 2.3 %collective-permute-start.6 = (bf16[528,128]{1,0:T(8,128)(2,1)S(1)}, bf16[528,128]{1,0:T(8,128)(2,1)S(1)}, u32[]{:S(2)}, u32[]{:S(2)}) collective-permute-start(bf16[528,128]{1,0:T(8,128)(2,1)S(1)} %collective-permute-done.5.refs_2_), channel_id=1, source_target_pairs={{0,1},{1,0},{2,3},{3,2},{4,5},{5,4},{6,7},{7,6},{8,9},{9,8},{10,11... | collective-permute-start | bytes 405512 | tf_op jit(solution)/shard_map/ppermute | solution.py:475
  18.4 1.4 %collective-permute-start.4 = (bf16[528,128]{1,0:T(8,128)(2,1)S(1)}, bf16[528,128]{1,0:T(8,128)(2,1)S(1)}, u32[]{:S(2)}, u32[]{:S(2)}) collective-permute-start(bf16[528,128]{1,0:T(8,128)(2,1)S(1)} %collective-permute-done.3.refs_0_), channel_id=1, source_target_pairs={{0,1},{1,0},{2,3},{3,2},{4,5},{5,4},{6,7},{7,6},{8,9},{9,8},{10,11... | collective-permute-start | bytes 405512 | tf_op jit(solution)/shard_map/ppermute | solution.py:475
  22.2 12.4 %collective-permute-start.16 = (bf16[272,512]{1,0:T(8,128)(2,1)S(1)}, bf16[272,512]{1,0:T(8,128)(2,1)S(1)}, u32[]{:S(2)}, u32[]{:S(2)}) collective-permute-start(bf16[272,512]{1,0:T(8,128)(2,1)S(1)} %get-tuple-element.63), channel_id=1, source_target_pairs={{0,64},{1,193},{2,66},{3,195},{8,72},{9,201},{10,74},{11,203},{16,... | collective-permute-start | bytes 835592 | tf_op jit(solution)/shard_map/ppermute | solution.py:484
  22.4 5.7 %collective-permute-start.9 = (f32[8,512]{1,0:T(8,128)S(1)}, f32[8,512]{1,0:T(8,128)S(1)}, u32[]{:S(2)}, u32[]{:S(2)}) collective-permute-start(f32[8,512]{1,0:T(8,128)S(1)} %get-tuple-element.46.own_ref), channel_id=1, source_target_pairs={{0,3},{1,2},{2,1},{3,0},{4,7},{5,6},{6,5},{7,4},{8,11},{9,10},{10,... | collective-permute-start | bytes 49160 | tf_op jit(solution)/shard_map/ppermute | solution.py:475
  26.7 5.2 %collective-permute-start.8 = (f32[8,512]{1,0:T(8,128)S(1)}, f32[8,512]{1,0:T(8,128)S(1)}, u32[]{:S(2)}, u32[]{:S(2)}) collective-permute-start(f32[8,512]{1,0:T(8,128)S(1)} %get-tuple-element.46.own_ref), channel_id=1, source_target_pairs={{0,2},{1,3},{2,0},{3,1},{4,6},{5,7},{6,4},{7,5},{8,10},{9,11},{10,... | collective-permute-start | bytes 49160 | tf_op jit(solution)/shard_map/ppermute | solution.py:475
  26.9 5.0 %collective-permute-start.7 = (f32[8,512]{1,0:T(8,128)S(1)}, f32[8,512]{1,0:T(8,128)S(1)}, u32[]{:S(2)}, u32[]{:S(2)}) collective-permute-start(f32[8,512]{1,0:T(8,128)S(1)} %get-tuple-element.46.own_ref), channel_id=1, source_target_pairs={{0,1},{1,0},{2,3},{3,2},{4,5},{5,4},{6,7},{7,6},{8,9},{9,8},{10,11... | collective-permute-start | bytes 49160 | tf_op jit(solution)/shard_map/ppermute | solution.py:475
  33.6 2.2 %collective-permute-start.10 = (bf16[1024,128]{1,0:T(8,128)(2,1)S(1)}, bf16[1024,128]{1,0:T(8,128)(2,1)S(1)}, u32[]{:S(2)}, u32[]{:S(2)}) collective-permute-start(bf16[1024,128]{1,0:T(8,128)(2,1)S(1)} %get-tuple-element.51), channel_id=1, source_target_pairs={{0,1},{1,0},{2,3},{3,2},{4,5},{5,4},{6,7},{7,6},{8,9},{9,8},{10,11... | collective-permute-start | bytes 786440 | tf_op jit(solution)/shard_map/ppermute | solution.py:475
  33.7 9.1 %collective-permute-start.18 = (bf16[272,512]{1,0:T(8,128)(2,1)S(1)}, bf16[272,512]{1,0:T(8,128)(2,1)S(1)}, u32[]{:S(2)}, u32[]{:S(2)}) collective-permute-start(bf16[272,512]{1,0:T(8,128)(2,1)S(1)} %get-tuple-element.63), channel_id=1, source_target_pairs={{0,192},{1,65},{2,194},{3,67},{8,200},{9,73},{10,202},{11,75},{16,... | collective-permute-start | bytes 835592 | tf_op jit(solution)/shard_map/ppermute | solution.py:484
  34.6 9.4 %collective-permute-start.17 = (bf16[272,512]{1,0:T(8,128)(2,1)S(1)}, bf16[272,512]{1,0:T(8,128)(2,1)S(1)}, u32[]{:S(2)}, u32[]{:S(2)}) collective-permute-start(bf16[272,512]{1,0:T(8,128)(2,1)S(1)} %collective-permute-done.16.n1_ref.refs_5_), channel_id=1, source_target_pairs={{0,64},{1,193},{2,66},{3,195},{8,72},{9,201},{10,74},{11,203},{16,... | collective-permute-start | bytes 835592 | tf_op jit(solution)/shard_map/ppermute | solution.py:484
  35.9 8.1 %collective-permute-start.11 = (bf16[544,128]{1,0:T(8,128)(2,1)S(1)}, bf16[544,128]{1,0:T(8,128)(2,1)S(1)}, u32[]{:S(2)}, u32[]{:S(2)}) collective-permute-start(bf16[544,128]{1,0:T(8,128)(2,1)S(1)} %get-tuple-element.53), channel_id=1, source_target_pairs={{0,4},{1,5},{2,6},{3,7},{4,0},{5,1},{6,2},{7,3},{8,12},{9,13},{10,... | collective-permute-start | bytes 417800 | tf_op jit(solution)/shard_map/ppermute | solution.py:475
  36.9 7.1 %collective-permute-start.12 = (bf16[512,128]{1,0:T(8,128)(2,1)S(1)}, bf16[512,128]{1,0:T(8,128)(2,1)S(1)}, u32[]{:S(2)}, u32[]{:S(2)}) collective-permute-start(bf16[512,128]{1,0:T(8,128)(2,1)S(1)} %get-tuple-element.54), channel_id=1, source_target_pairs={{0,6},{1,7},{2,4},{3,5},{4,2},{5,3},{6,0},{7,1},{8,14},{9,15},{10,... | collective-permute-start | bytes 393224 | tf_op jit(solution)/shard_map/ppermute | solution.py:475
  42.8 11.3 %collective-permute-start.20 = (bf16[272,512]{1,0:T(8,128)(2,1)S(1)}, bf16[272,512]{1,0:T(8,128)(2,1)S(1)}, u32[]{:S(2)}, u32[]{:S(2)}) collective-permute-start(bf16[272,512]{1,0:T(8,128)(2,1)S(1)} %collective-permute-done.18.n3_ref.refs_7_), channel_id=1, source_target_pairs={{0,1},{1,0},{2,3},{3,2},{4,5},{5,4},{6,7},{7,6},{8,9},{9,8},{10,11... | collective-permute-start | bytes 835592 | tf_op jit(solution)/shard_map/ppermute | solution.py:475
  42.8 11.3 %collective-permute-start.21 = (bf16[272,512]{1,0:T(8,128)(2,1)S(1)}, bf16[272,512]{1,0:T(8,128)(2,1)S(1)}, u32[]{:S(2)}, u32[]{:S(2)}) collective-permute-start(bf16[272,512]{1,0:T(8,128)(2,1)S(1)} %collective-permute-done.16.n1_ref.refs_5_), channel_id=1, source_target_pairs={{0,1},{1,0},{2,3},{3,2},{4,5},{5,4},{6,7},{7,6},{8,9},{9,8},{10,11... | collective-permute-start | bytes 835592 | tf_op jit(solution)/shard_map/ppermute | solution.py:475
  44.0 15.2 %collective-permute-start.19 = (bf16[272,512]{1,0:T(8,128)(2,1)S(1)}, bf16[272,512]{1,0:T(8,128)(2,1)S(1)}, u32[]{:S(2)}, u32[]{:S(2)}) collective-permute-start(bf16[272,512]{1,0:T(8,128)(2,1)S(1)} %collective-permute-done.17.refs_6_), channel_id=1, source_target_pairs={{0,1},{1,0},{2,3},{3,2},{4,5},{5,4},{6,7},{7,6},{8,9},{9,8},{10,11... | collective-permute-start | bytes 835592 | tf_op jit(solution)/shard_map/ppermute | solution.py:475
  45.4 7.6 %collective-permute-start.13 = (bf16[528,128]{1,0:T(8,128)(2,1)S(1)}, bf16[528,128]{1,0:T(8,128)(2,1)S(1)}, u32[]{:S(2)}, u32[]{:S(2)}) collective-permute-start(bf16[528,128]{1,0:T(8,128)(2,1)S(1)} %get-tuple-element.58.pay_ref.refs_0_), channel_id=1, source_target_pairs={{0,64},{1,193},{2,66},{3,195},{8,72},{9,201},{10,74},{11,203},{16,... | collective-permute-start | bytes 405512 | tf_op jit(solution)/shard_map/ppermute | solution.py:484
  45.5 8.7 %collective-permute-start.15 = (bf16[528,128]{1,0:T(8,128)(2,1)S(1)}, bf16[528,128]{1,0:T(8,128)(2,1)S(1)}, u32[]{:S(2)}, u32[]{:S(2)}) collective-permute-start(bf16[528,128]{1,0:T(8,128)(2,1)S(1)} %get-tuple-element.58.pay_ref.refs_0_), channel_id=1, source_target_pairs={{0,192},{1,65},{2,194},{3,67},{8,200},{9,73},{10,202},{11,75},{16,... | collective-permute-start | bytes 405512 | tf_op jit(solution)/shard_map/ppermute | solution.py:484
  53.0 6.2 %collective-permute-start.14 = (bf16[528,128]{1,0:T(8,128)(2,1)S(1)}, bf16[528,128]{1,0:T(8,128)(2,1)S(1)}, u32[]{:S(2)}, u32[]{:S(2)}) collective-permute-start(bf16[528,128]{1,0:T(8,128)(2,1)S(1)} %collective-permute-done.13.p1_ref.refs_1_), channel_id=1, source_target_pairs={{0,64},{1,193},{2,66},{3,195},{8,72},{9,201},{10,74},{11,203},{16,... | collective-permute-start | bytes 405512 | tf_op jit(solution)/shard_map/ppermute | solution.py:484
  54.1 5.1 %copy-start = (bf16[1,4608,128]{2,1,0:T(8,128)(2,1)S(1)}, bf16[1,4608,128]{2,1,0:T(8,128)(2,1)}, u32[]{:S(2)}) copy-start(bf16[1,4608,128]{2,1,0:T(8,128)(2,1)} %param.13) | copy-start | bytes 3538948
  60.7 6.4 %collective-permute-start.22 = (bf16[576,128]{1,0:T(8,128)(2,1)S(1)}, bf16[576,128]{1,0:T(8,128)(2,1)S(1)}, u32[]{:S(2)}, u32[]{:S(2)}) collective-permute-start(bf16[576,128]{1,0:T(8,128)(2,1)S(1)} %get-tuple-element.65), channel_id=1, source_target_pairs={{0,8},{1,57},{2,10},{3,59},{8,0},{9,17},{10,2},{11,19},{16,24},{17... | collective-permute-start | bytes 442376 | tf_op jit(solution)/shard_map/ppermute | solution.py:484
  63.6 11.3 %collective-permute-start.26 = (bf16[512,128]{1,0:T(8,128)(2,1)S(1)}, bf16[512,128]{1,0:T(8,128)(2,1)S(1)}, u32[]{:S(2)}, u32[]{:S(2)}) collective-permute-start(bf16[512,128]{1,0:T(8,128)(2,1)S(1)} %get-tuple-element.71), channel_id=1, source_target_pairs={{0,1},{1,0},{2,3},{3,2},{4,5},{5,4},{6,7},{7,6},{8,9},{9,8},{10,11... | collective-permute-start | bytes 393224 | tf_op jit(solution)/shard_map/ppermute | solution.py:475
  63.7 13.9 %collective-permute-start.27 = (bf16[512,128]{1,0:T(8,128)(2,1)S(1)}, bf16[512,128]{1,0:T(8,128)(2,1)S(1)}, u32[]{:S(2)}, u32[]{:S(2)}) collective-permute-start(bf16[512,128]{1,0:T(8,128)(2,1)S(1)} %get-tuple-element.72), channel_id=1, source_target_pairs={{0,2},{1,3},{2,0},{3,1},{4,6},{5,7},{6,4},{7,5},{8,10},{9,11},{10,... | collective-permute-start | bytes 393224 | tf_op jit(solution)/shard_map/ppermute | solution.py:475
  65.1 12.5 %collective-permute-start.28 = (bf16[512,128]{1,0:T(8,128)(2,1)S(1)}, bf16[512,128]{1,0:T(8,128)(2,1)S(1)}, u32[]{:S(2)}, u32[]{:S(2)}) collective-permute-start(bf16[512,128]{1,0:T(8,128)(2,1)S(1)} %get-tuple-element.73), channel_id=1, source_target_pairs={{0,3},{1,2},{2,1},{3,0},{4,7},{5,6},{6,5},{7,4},{8,11},{9,10},{10,... | collective-permute-start | bytes 393224 | tf_op jit(solution)/shard_map/ppermute | solution.py:475
  67.1 10.5 %collective-permute-start.23 = (bf16[144,128]{1,0:T(8,128)(2,1)S(1)}, bf16[144,128]{1,0:T(8,128)(2,1)S(1)}, u32[]{:S(2)}, u32[]{:S(2)}) collective-permute-start(bf16[144,128]{1,0:T(8,128)(2,1)S(1)} %get-tuple-element.67), channel_id=1, source_target_pairs={{0,16},{8,24},{16,32},{24,40},{32,48},{40,56},{48,0},{56,8},{64,80... | collective-permute-start | bytes 110600 | tf_op jit(solution)/shard_map/ppermute | solution.py:490
  70.4 7.9 %collective-permute-start.24 = (bf16[144,128]{1,0:T(8,128)(2,1)S(1)}, bf16[144,128]{1,0:T(8,128)(2,1)S(1)}, u32[]{:S(2)}, u32[]{:S(2)}) collective-permute-start(bf16[144,128]{1,0:T(8,128)(2,1)S(1)} %get-tuple-element.68), channel_id=1, source_target_pairs={{0,32},{8,40},{16,48},{24,56},{32,0},{40,8},{48,16},{56,24},{64,96... | collective-permute-start | bytes 110600 | tf_op jit(solution)/shard_map/ppermute | solution.py:490
  74.9 4.9 %collective-permute-start.25 = (bf16[144,128]{1,0:T(8,128)(2,1)S(1)}, bf16[144,128]{1,0:T(8,128)(2,1)S(1)}, u32[]{:S(2)}, u32[]{:S(2)}) collective-permute-start(bf16[144,128]{1,0:T(8,128)(2,1)S(1)} %get-tuple-element.69), channel_id=1, source_target_pairs={{0,48},{8,56},{16,0},{24,8},{32,16},{40,24},{48,32},{56,40},{64,11... | collective-permute-start | bytes 110600 | tf_op jit(solution)/shard_map/ppermute | solution.py:490

commit v2 on v0

--- a/solution.py
+++ b/solution.py
@@ -171,19 +171,25 @@
     pay_ref[count * PIX :, :] = jnp.concatenate([hi, coef - hi], axis=0).astype(bf16)
 
 
-def store_dx(gz, wslot_ref, stys_ref, put):
-    count = stys_ref.shape[0]
-    own = gz.shape[1]
+def shifted_gz(gz):
     gz = gz.astype(f32)
     by_col = [col_shift(gz, 1 - kx).astype(bf16) for kx in range(3)]
-    cols = jnp.concatenate(
-        [row_shift(by_col[k % 3], 1 - k // 3) for k in range(TAPS)], axis=1
-    )
+    return jnp.concatenate([row_shift(by_col[k % 3], 1 - k // 3) for k in range(TAPS)], axis=1)
+
+
+def store_dx(cols, wslot_ref, stys_ref, keep_ref, send_ref):
+    count = stys_ref.shape[0]
+    own = keep_ref.shape[1]
     share = lax.dot_general(cols, wslot_ref[...], NT, preferred_element_type=f32)
     for d in range(4):
         for b in range(count):
             sty = stys_ref[b : b + 1, d * own : (d + 1) * own]
-            put(d, b, share[b * PIX : (b + 1) * PIX, d * own : (d + 1) * own] * sty)
+            block = share[b * PIX : (b + 1) * PIX, d * own : (d + 1) * own] * sty
+            at = (d // 2) * count * PIX + b * PIX
+            if d % 2 == 0:
+                keep_ref[at : at + PIX, :] = block
+            else:
+                send_ref[at : at + PIX, :] = block.astype(bf16)
 
 
 def disc_kernel(
@@ -231,15 +237,8 @@
     ).astype(bf16)
     da = head_grad(dimage, rgb_ref) * slope_ref[...]
     store_gz(da, z_ref[...], demod_ref, pay_ref)
-
-    def put(d, b, block):
-        at = (d // 2) * count * PIX + b * PIX
-        if d % 2 == 0:
-            keep_ref[at : at + PIX, :] = block
-        else:
-            send_ref[at : at + PIX, :] = block.astype(bf16)
-
-    store_dx(pay_ref[: count * PIX, :], wslot_ref, stys_ref, put)
+    cols = shifted_gz(pay_ref[: count * PIX, :])
+    store_dx(cols, wslot_ref, stys_ref, keep_ref, send_ref)
 
 
 def pair_kernel(keep_ref, got_ref, tail_ref, near_ref, far_ref):
@@ -284,16 +283,19 @@
         pay_ref[...] = other_ref[...]
 
 
-def share_kernel(pay_ref, wslot_ref, stys_ref, *out_refs):
-    pixels = stys_ref.shape[0] * PIX
-
-    def put(d, b, block):
-        out_refs[d][b * PIX : (b + 1) * PIX, :] = block.astype(bf16)
-
-    store_dx(pay_ref[:pixels, :], wslot_ref, stys_ref, put)
-
-
-def turn_kernel(idx, xa_ref, xb_ref, sty_ref, out_ref, half_ref):
+def share_kernel(pay_ref, wslot_ref, stys_ref, xm_ref, keep_ref, send_ref, acc_ref):
+    cols = shifted_gz(pay_ref[: stys_ref.shape[0] * PIX, :])
+    store_dx(cols, wslot_ref, stys_ref, keep_ref, send_ref)
+    acc_ref[...] = jnp.dot(xm_ref[: acc_ref.shape[0], :], cols, preferred_element_type=f32)
+
+
+def dx_pair_kernel(keep_ref, got_ref, near_ref, far_ref):
+    rows = near_ref.shape[0]
+    near_ref[...] = keep_ref[:rows] + got_ref[:rows].astype(f32)
+    far_ref[...] = (keep_ref[rows:] + got_ref[rows:].astype(f32)).astype(bf16)
+
+
+def turn_kernel(idx, xa_ref, xb_ref, sty_ref, out_ref):
     chan = idx[1]
     full = xa_ref.shape[1]
     count = sty_ref.shape[0]
@@ -317,99 +319,56 @@
     mid = (sty - hi).astype(bf16).astype(f32)
     lo = sty - hi - mid
     rows = [hi, mid, lo]
-    tail = jnp.concatenate(
+    out_ref[full:, :] = jnp.concatenate(
         rows + [jnp.zeros((EXTRA - 3 * count, full), f32)], axis=0
     ).astype(bf16)
-    out_ref[full:, :] = tail
-    half = full // 2
-    start = pl.multiple_of((chan & 1) * half, half)
-    half_ref[:half, :] = out_ref[pl.ds(start, half), :]
-    half_ref[half:, :] = tail
-
-
-def taps_of(pay_ref, y, g_ref):
+
+
+def z_partner(z, core):
+    return ((z + core) ^ 1) - core
+
+
+def weight_kernel(
+    idx, pay_ref, other_pay_ref, xm_ref, other_xm_ref, w_ref, before_ref,
+    keep_ref, send_1_ref, send_2_ref, send_3_ref, sum_ref,
+):
+    core, y, z = idx[1] & 1, idx[2], idx[3]
+    full = before_ref.shape[0]
     own = pay_ref.shape[1]
     pixels = pay_ref.shape[0] - EXTRA
     count = pixels // PIX
-    stride = PIX + 2 * RES
-    zeros = jnp.zeros((RES, own), bf16)
-    gz = pay_ref[:pixels, :].astype(f32)
-    for kx in range(3):
-        moved = col_shift(gz, 1 - kx).astype(bf16)
-        for b in range(count):
-            at = b * stride
-            g_ref[kx, at : at + RES, :] = zeros
-            g_ref[kx, at + RES : at + RES + PIX, :] = moved[b * PIX : (b + 1) * PIX]
-            g_ref[kx, at + RES + PIX : at + stride, :] = zeros
-    taps = []
-    for j in range(3):
-        k = 2 * y + j
-        ky = k // 3
-        kx = k - 3 * ky
-        rows = []
-        for b in range(count):
-            start = b * stride + (2 - ky) * RES
-            rows.append(g_ref[kx, pl.ds(pl.multiple_of(start, RES), PIX), :])
-        taps.append(jnp.concatenate(rows, axis=0))
-    return jnp.concatenate(taps, axis=1)
-
-
-def own_weight_kernel(idx, pay_ref, own_ref, acc_ref, g_ref):
-    full = own_ref.shape[0] - EXTRA
-    acc_ref[...] = jnp.dot(
-        own_ref[:full, :], taps_of(pay_ref, idx[2], g_ref), preferred_element_type=f32
-    )
-
-
-def weight_kernel(idx, *refs):
-    pays, own_ref, near, far, w_ref, first_ref = refs[:4], refs[4], refs[5:8], refs[8:11], refs[11], refs[12]
-    keep_ref, send_ref = refs[13:15]
-    g_ref, acc_ref, sum_ref = refs[15:18]
-    core, y, z = idx[1] & 1, idx[2], idx[3]
-    full = own_ref.shape[0] - EXTRA
-    half = full // 2
-    own = pays[0].shape[1]
-    pixels = pays[0].shape[0] - EXTRA
-    count = pixels // PIX
-    rest = [taps_of(pays[n], y, g_ref.at[n - 1]) for n in (1, 2, 3)]
-    for refs_, where in ((near, core), (far, 1 - core)):
-        part = None
-        for ref, taps in zip(refs_, rest):
-            more = jnp.dot(ref[:half, :], taps, preferred_element_type=f32)
-            part = more if part is None else part + more
-        at = pl.ds(pl.multiple_of(where * half, half), half)
-        acc_ref[at, :] = first_ref[at, :] + part
+    cols = shifted_gz(other_pay_ref[:pixels, :])
+    total = before_ref[...] + jnp.dot(other_xm_ref[:full, :], cols, preferred_element_type=f32)
     sty_rows, coef_rows = [], []
-    for n in range(4):
-        tail = own_ref[full:, :] if n == 0 else near[n - 1][half:, :]
-        tail = tail.astype(f32)
+    for pay, xm in ((pay_ref, xm_ref), (other_pay_ref, other_xm_ref)):
+        tail = xm[full:, :].astype(f32)
         sty = tail[:count] + tail[count : 2 * count] + tail[2 * count : 3 * count]
         sty_rows.append(sty * sty)
-        tail = pays[n][pixels:, :].astype(f32)
+        tail = pay[pixels:, :].astype(f32)
         coef_rows.append(tail[:count] + tail[8 : 8 + count])
     left = pad_rows(jnp.concatenate(sty_rows, axis=0), own).T
     right = pad_rows(jnp.concatenate(coef_rows, axis=0), own)
     demod_term = jnp.dot(left, right, precision=lax.Precision.HIGHEST, preferred_element_type=f32)
-    for j in range(3):
-        start = pl.multiple_of((2 * y + j) * full, full)
-        w = w_ref[pl.ds(start, full), :].astype(f32)
-        sum_ref[j * full : (j + 1) * full, :] = (
-            acc_ref[:, j * own : (j + 1) * own] + w * demod_term
-        )
+    for k in range(TAPS):
+        at = slice(k * full, (k + 1) * full)
+        sum_ref[at, :] = total[:, k * own : (k + 1) * own] + w_ref[at, :].astype(f32) * demod_term
     rows = keep_ref.shape[0] // 4
-    for e in range(4):
-        for ref, first in ((keep_ref, z), (send_ref, z ^ 1)):
-            start = y * own + ((first + 2 * e) & 7) * rows
+    step = 1 - 2 * core
+    for d, ref in enumerate((keep_ref, send_1_ref, send_2_ref, send_3_ref)):
+        to_y = (y + step * d) & 3
+        for e in range(4):
+            start = (to_y * 8 + ((z + 2 * e) & 7)) * rows
             block = sum_ref[pl.ds(pl.multiple_of(start, RES), rows), :]
             ref[e * rows : (e + 1) * rows, :] = block.astype(ref.dtype)
 
 
-def z_pair_kernel(keep_ref, got_ref, own_ref, *out_refs):
+def y_sum_kernel(keep_ref, r1_ref, r2_ref, r3_ref, own_ref, *out_refs):
     rows = own_ref.shape[0]
-    own_ref[...] = keep_ref[:rows] + got_ref[:rows].astype(f32)
-    for e, ref in enumerate(out_refs):
-        at = slice((e + 1) * rows, (e + 2) * rows)
-        ref[...] = (keep_ref[at] + got_ref[at].astype(f32)).astype(bf16)
+    for e, ref in enumerate((own_ref, *out_refs)):
+        at = slice(e * rows, (e + 1) * rows)
+        total = keep_ref[at] + r1_ref[at].astype(f32)
+        total = total + (r2_ref[at].astype(f32) + r3_ref[at].astype(f32))
+        ref[...] = total.astype(ref.dtype)
 
 
 def total_kernel(count, *refs):
@@ -418,8 +377,7 @@
     for ref in refs[1:count]:
         total = total + ref[...].astype(f32)
     grad_ref[...] = total
-    shares = [ref[...].astype(f32) for ref in refs[count : count + 4]]
-    dx = ((shares[0] + shares[1]) + (shares[2] + shares[3])).astype(bf16)
+    dx = (refs[count][...] + refs[count + 1][...].astype(f32)).astype(bf16)
     for b in range(dx_ref.shape[0]):
         dx_ref[b] = dx[b * PIX : (b + 1) * PIX].T
 
@@ -464,10 +422,17 @@
     def across(value, links):
         return lax.ppermute(value, ("segment", "chan"), links)
 
+    def by_core(value, place):
+        links = []
+        for y in range(4):
+            for z in range(8):
+                for c in range(4):
+                    to_y, to_z = place(y, z, c % 2)
+                    links.append(((y * 8 + z) * 4 + c, (to_y % 4 * 8 + to_z % 8) * 4 + c))
+        return lax.ppermute(value, ("dp", "chan"), links)
+
     def over_y(value, d):
-        return lax.ppermute(
-            value, "dp", [(y * 8 + z, (y + d) % 4 * 8 + z) for y in range(4) for z in range(8)]
-        )
+        return by_core(value, lambda y, z, core: (y - d if core else y + d, z))
 
     def over_z(value, d):
         return lax.ppermute(
@@ -525,15 +490,13 @@
         [y0, y1, y2, y3, stys, wslot, demod, nb, rgbp],
     )
     images = [within(image_own, d) for d in (1, 2, 3)]
-    xm, xm_half = call(
-        turn_kernel,
-        [((full + EXTRA, pixels), bf16), ((full // 2 + EXTRA, pixels), bf16)],
-        [idx, xm_a, xm_b, sty],
-        scalars=1,
-    )
+    (xm,) = call(turn_kernel, [((full + EXTRA, pixels), bf16)], [idx, xm_a, xm_b, sty], scalars=1)
     (image_first,) = call(first_image_kernel, [((8, pixels), f32)], [y0, y1, y2, y3])
-    near = [over_y(xm_half, d) for d in (1, 2, 3)]
-    far = [within(near[n], 1) for n in range(3)]
+
+    def to_partner(value):
+        return by_core(value, lambda y, z, core: (y, z_partner(z, core)))
+
+    other_xm = to_partner(xm)
     two = (2 * pixels, own)
     tail, pay_b, dx_keep, dx_send = call(
         disc_kernel,
@@ -552,32 +515,25 @@
         [idx, *got, rgbp, slope_a, z_a, demod, pay_b, tail],
         scalars=1,
     )
-    pays = [pay_g] + [over_y(pay_g, d) for d in (1, 2, 3)]
-    shares = call(share_kernel, [share] * 4, [pay_g, wslot, stys])
-    mine = [shares[0]] + [within(shares[d], d) for d in (1, 2, 3)]
+    other_pay = to_partner(pay_g)
+    keep, send, before = call(
+        share_kernel, [(two, f32), (two, bf16), ((full, TAPS * own), f32)], [pay_g, wslot, stys, xm]
+    )
+    got = within(send, 1)
+    near, far = call(dx_pair_kernel, [((pixels, own), f32), share], [keep, got])
+    mine = [near, within(far, 2)]
     rows = weight.shape[0] // 32
-    taps = (3, count * (PIX + 2 * RES), own)
-    (first,) = call(
-        own_weight_kernel,
-        [((full, 3 * own), f32)],
-        [idx, pay_g, xm],
-        scratch=[pltpu.VMEM(taps, bf16)],
+    four = (4 * rows, own)
+    y_keep, *y_send = call(
+        weight_kernel,
+        [(four, f32)] + [(four, bf16)] * 3,
+        [idx, pay_g, other_pay, xm, other_xm, weight, before],
+        scratch=[pltpu.VMEM(weight.shape, f32)],
         scalars=1,
     )
-    z_keep, z_send = call(
-        weight_kernel,
-        [((4 * rows, own), f32), ((4 * rows, own), bf16)],
-        [idx, *pays, xm, *near, *far, weight, first],
-        scratch=[
-            pltpu.VMEM((3, *taps), bf16),
-            pltpu.VMEM((full, 3 * own), f32),
-            pltpu.VMEM((3 * full, own), f32),
-        ],
-        scalars=1,
-    )
-    z_got = lax.ppermute(z_send, "dp", [(n, n ^ 1) for n in range(32)])
+    y_got = [over_y(y_send[d - 1], d) for d in (1, 2, 3)]
     block = (rows, own)
-    z_own, *z_outs = call(z_pair_kernel, [(block, f32)] + [(block, bf16)] * 3, [z_keep, z_got])
+    z_own, *z_outs = call(y_sum_kernel, [(block, f32)] + [(block, bf16)] * 3, [y_keep, *y_got])
     parts = [z_own] + [over_z(z_outs[e - 1], 2 * e) for e in (1, 2, 3)]
     grad_rows, dx = call(
         functools.partial(total_kernel, len(parts)),

time: 87.4 us -> 76.4 us (0.87)
  the two profiles are of different devices: /device:TPU:4 before, /device:TPU:1 now
where the time goes in v2:
time: 76.4 us; the launch traced here: 76.3 us
  starting transfers between devices  35.8 us (47%)
  waiting for transfers between devices  25.5 us (33%)
  Pallas kernels  14.2 us (19%)
  between operations  0.77 us (1%)
    ppermute x15, starting transfers between devices, across(): return lax.ppermute(value, ('segment', 'chan'), links)  16.3 us
    pallas_call x13, Pallas kernels, call(): pl.pallas_call(kernel, out_shape=[jax.ShapeDtypeStruct(*o[:2]) if len(o)...  14.2 us
    ppermute x15, waiting for transfers between devices, across(): return lax.ppermute(value, ('segment', 'chan'), links)  14 us
    ppermute x5, starting transfers between devices, by_core(): return lax.ppermute(value, ('dp', 'chan'), links)  12.1 us
    ppermute x5, waiting for transfers between devices, by_core(): return lax.ppermute(value, ('dp', 'chan'), links)  10.4 us
    ppermute x3, starting transfers between devices, over_z(): lax.ppermute(value, 'dp', [(y * 8 + z, y * 8 + (z + d) % 8) for y in rang...  7.45 us
  transfers between devices with their start and end apart: 23, of which 12 were waited for; matrix products, arithmetic and copies ran while one was open for 0% of the time, Pallas kernels for 12%

profile of v2, /device:TPU:1, one launch (start us, length us, event | category | flops | bytes accessed | tf_op | source)
XLA Modules:
  0.0 76.3 jit_solution(628828755853279951)
XLA Ops:
  0.6 3.4 %collective-permute-start.1 = (bf16[2,128,256]{2,1,0:T(8,128)(2,1)}, bf16[2,128,256]{2,1,0:T(8,128)(2,1)S(1)}, u32[]{:S(2)}, u32[]{:S(2)}) collective-permute-start(bf16[2,128,256]{2,1,0:T(8,128)(2,1)} %refs_0_.1), channel_id=1, source_target_pairs={{0,6},{1,7},{2,4},{3,5},{4,2},{5,3},{6,0},{7,1},{8,14},{9,15},{10,... | collective-permute-start | bytes 393224 | tf_op jit(solution)/shard_map/ppermute | solution.py:423
  4.0 1.0 %collective-permute-start = (bf16[2,128,256]{2,1,0:T(8,128)(2,1)}, bf16[2,128,256]{2,1,0:T(8,128)(2,1)S(1)}, u32[]{:S(2)}, u32[]{:S(2)}) collective-permute-start(bf16[2,128,256]{2,1,0:T(8,128)(2,1)} %refs_0_.1), channel_id=1, source_target_pairs={{0,1},{1,0},{2,3},{3,2},{4,5},{5,4},{6,7},{7,6},{8,9},{9,8},{10,11... | collective-permute-start | bytes 393224 | tf_op jit(solution)/shard_map/ppermute | solution.py:423
  5.0 1.6 %collective-permute-done.1.refs_2_ = bf16[2,128,256]{2,1,0:T(8,128)(2,1)S(1)} collective-permute-done((bf16[2,128,256]{2,1,0:T(8,128)(2,1)}, bf16[2,128,256]{2,1,0:T(8,128)(2,1)S(1)}, u32[]{:S(2)}, u32[]{:S(2)}) %collective-permute-start.1) | collective-permute-done | bytes 131104 | tf_op jit(solution)/shard_map/ppermute | solution.py:423
  6.6 3.7 %collective-permute-start.2 = (bf16[2,128,256]{2,1,0:T(8,128)(2,1)S(1)}, bf16[2,128,256]{2,1,0:T(8,128)(2,1)S(1)}, u32[]{:S(2)}, u32[]{:S(2)}) collective-permute-start(bf16[2,128,256]{2,1,0:T(8,128)(2,1)S(1)} %collective-permute-done.1.refs_2_), channel_id=1, source_target_pairs={{0,1},{1,0},{2,3},{3,2},{4,5},{5,4},{6,7},{7,6},{8,9},{9,8},{10,11... | collective-permute-start | bytes 393224 | tf_op jit(solution)/shard_map/ppermute | solution.py:423
  10.4 2.6 %shard_map.121 = (bf16[512,1152]{1,0:T(8,128)(2,1)S(1)}, f32[2,512]{1,0:T(2,128)S(1)}, f32[2,128]{1,0:T(2,128)S(1)}, f32[512,128]{1,0:T(8,128)S(1)}, f32[5,256,1...) custom-call(s32[4]{0:T(128)S(1)} %pad_add_fusion.idx, bf16[4608,128]{1,0:T(8,128)(2,1)} %bitcast.12, ...), custom_call_target="tpu_custom_call" | custom-call | tf_op jit(solution)/shard_map/pallas_call | solution.py:396
  13.0 1.1 %shard_map.122 = (bf16[528,128]{1,0:T(8,128)(2,1)S(1)}, f32[512,128]{1,0:T(8,128)S(1)}, f32[512,128]{1,0:T(8,128)S(1)}, bf16[512,512]{1,0:T(8,128)(2,1)S(1)}) custom-call(bf16[2,128,256]{2,1,0:T(8,128)(2,1)S(1)} %copy-done.1, bf16[2,128,256]{2,1,0:T(8,128)(2,1)S(1)} %collective-permute-done.refs_1_, bf16[2,128,256]{2,1,0:T(8,128)(2,1)S(1)} %collective-permute-done.1.refs_2_, ...), custom_call_target="tpu_custom_call" | custom-call | tf_op jit(solution)/shard_map/pallas_call | solution.py:396
  14.2 1.1 %collective-permute-start.5 = (bf16[528,128]{1,0:T(8,128)(2,1)S(1)}, bf16[528,128]{1,0:T(8,128)(2,1)S(1)}, u32[]{:S(2)}, u32[]{:S(2)}) collective-permute-start(bf16[528,128]{1,0:T(8,128)(2,1)S(1)} %get-tuple-element.46), channel_id=1, source_target_pairs={{0,6},{1,7},{2,4},{3,5},{4,2},{5,3},{6,0},{7,1},{8,14},{9,15},{10,... | collective-permute-start | bytes 405512 | tf_op jit(solution)/shard_map/ppermute | solution.py:423
  15.4 4.0 %collective-permute-done.3.refs_0_ = bf16[528,128]{1,0:T(8,128)(2,1)S(1)} collective-permute-done((bf16[528,128]{1,0:T(8,128)(2,1)S(1)}, bf16[528,128]{1,0:T(8,128)(2,1)S(1)}, u32[]{:S(2)}, u32[]{:S(2)}) %collective-permute-start.3) | collective-permute-done | bytes 135200 | tf_op jit(solution)/shard_map/ppermute | solution.py:423
  19.4 0.9 %collective-permute-start.4 = (bf16[528,128]{1,0:T(8,128)(2,1)S(1)}, bf16[528,128]{1,0:T(8,128)(2,1)S(1)}, u32[]{:S(2)}, u32[]{:S(2)}) collective-permute-start(bf16[528,128]{1,0:T(8,128)(2,1)S(1)} %collective-permute-done.3.refs_0_), channel_id=1, source_target_pairs={{0,1},{1,0},{2,3},{3,2},{4,5},{5,4},{6,7},{7,6},{8,9},{9,8},{10,11... | collective-permute-start | bytes 405512 | tf_op jit(solution)/shard_map/ppermute | solution.py:423
  20.7 0.9 %collective-permute-start.6 = (bf16[528,128]{1,0:T(8,128)(2,1)S(1)}, bf16[528,128]{1,0:T(8,128)(2,1)S(1)}, u32[]{:S(2)}, u32[]{:S(2)}) collective-permute-start(bf16[528,128]{1,0:T(8,128)(2,1)S(1)} %collective-permute-done.5.refs_2_), channel_id=1, source_target_pairs={{0,1},{1,0},{2,3},{3,2},{4,5},{5,4},{6,7},{7,6},{8,9},{9,8},{10,11... | collective-permute-start | bytes 405512 | tf_op jit(solution)/shard_map/ppermute | solution.py:423
  21.5 1.0 %collective-permute-done.6.refs_3_ = bf16[528,128]{1,0:T(8,128)(2,1)S(1)} collective-permute-done((bf16[528,128]{1,0:T(8,128)(2,1)S(1)}, bf16[528,128]{1,0:T(8,128)(2,1)S(1)}, u32[]{:S(2)}, u32[]{:S(2)}) %collective-permute-start.6) | collective-permute-done | bytes 135200 | tf_op jit(solution)/shard_map/ppermute | solution.py:423
  22.5 1.7 %shard_map.123 = (bf16[528,128]{1,0:T(8,128)(2,1)}, f32[512,128]{1,0:T(8,128)S(1)}, f32[512,128]{1,0:T(8,128)S(1)}, bf16[512,512]{1,0:T(8,128)(2,1)S(1)}, f32[8,512]{1,0:T(8,128)S(1)}) custom-call(bf16[528,128]{1,0:T(8,128)(2,1)S(1)} %collective-permute-done.3.refs_0_, bf16[528,128]{1,0:T(8,128)(2,1)S(1)} %collective-permute-done.4.refs_1_, ...), custom_call_target="tpu_custom_call" | custom-call | tf_op jit(solution)/shard_map/pallas_call | solution.py:396
  24.6 0.9 %collective-permute-start.8 = (f32[8,512]{1,0:T(8,128)S(1)}, f32[8,512]{1,0:T(8,128)S(1)}, u32[]{:S(2)}, u32[]{:S(2)}) collective-permute-start(f32[8,512]{1,0:T(8,128)S(1)} %get-tuple-element.47.own_ref), channel_id=1, source_target_pairs={{0,2},{1,3},{2,0},{3,1},{4,6},{5,7},{6,4},{7,5},{8,10},{9,11},{10,... | collective-permute-start | bytes 49160 | tf_op jit(solution)/shard_map/ppermute | solution.py:423
  25.5 2.4 %collective-permute-start.9 = (f32[8,512]{1,0:T(8,128)S(1)}, f32[8,512]{1,0:T(8,128)S(1)}, u32[]{:S(2)}, u32[]{:S(2)}) collective-permute-start(f32[8,512]{1,0:T(8,128)S(1)} %get-tuple-element.47.own_ref), channel_id=1, source_target_pairs={{0,3},{1,2},{2,1},{3,0},{4,7},{5,6},{6,5},{7,4},{8,11},{9,10},{10,... | collective-permute-start | bytes 49160 | tf_op jit(solution)/shard_map/ppermute | solution.py:423
  28.7 1.5 %collective-permute-done.9.r3_ref = f32[8,512]{1,0:T(8,128)S(1)} collective-permute-done((f32[8,512]{1,0:T(8,128)S(1)}, f32[8,512]{1,0:T(8,128)S(1)}, u32[]{:S(2)}, u32[]{:S(2)}) %collective-permute-start.9) | collective-permute-done | bytes 16416 | tf_op jit(solution)/shard_map/ppermute | solution.py:423
  30.2 1.7 %shard_map.125 = (bf16[32,128]{1,0:T(8,128)(2,1)S(1)}, bf16[528,128]{1,0:T(8,128)(2,1)S(1)}, f32[1024,128]{1,0:T(8,128)S(1)}, bf16[1024,128]{1,0:T(8,128)(2,1)S(1)}) custom-call(f32[8,512]{1,0:T(8,128)S(1)} %get-tuple-element.47.own_ref, f32[8,512]{1,0:T(8,128)S(1)} %collective-permute-done.7.r1_ref, f32[8,512]{1,0:T(8,128)S(1)} %collective-permute-done.8.r2_ref, ...), custom_call_target="tpu_custom_call" | custom-call | tf_op jit(solution)/shard_map/pallas_call | solution.py:396
  32.4 0.8 shard_map.128.xm_ref
  33.1 5.7 %collective-permute-start.14 = (bf16[528,512]{1,0:T(8,128)(2,1)S(1)}, bf16[528,512]{1,0:T(8,128)(2,1)S(1)}, u32[]{:S(2)}, u32[]{:S(2)}) collective-permute-start(bf16[528,512]{1,0:T(8,128)(2,1)S(1)} %shard_map.128.xm_ref), channel_id=1, source_target_pairs={{0,8},{1,57},{2,10},{3,59},{8,0},{9,17},{10,2},{11,19},{16,24},{17... | collective-permute-start | bytes 1622024 | tf_op jit(solution)/shard_map/ppermute | solution.py:432
  38.9 0.8 %collective-permute-start.11 = (bf16[544,128]{1,0:T(8,128)(2,1)S(1)}, bf16[544,128]{1,0:T(8,128)(2,1)S(1)}, u32[]{:S(2)}, u32[]{:S(2)}) collective-permute-start(bf16[544,128]{1,0:T(8,128)(2,1)S(1)} %get-tuple-element.54), channel_id=1, source_target_pairs={{0,4},{1,5},{2,6},{3,7},{4,0},{5,1},{6,2},{7,3},{8,12},{9,13},{10,... | collective-permute-start | bytes 417800 | tf_op jit(solution)/shard_map/ppermute | solution.py:423
  39.9 4.8 %collective-permute-done.12.s1_ref = bf16[512,128]{1,0:T(8,128)(2,1)S(1)} collective-permute-done((bf16[512,128]{1,0:T(8,128)(2,1)S(1)}, bf16[512,128]{1,0:T(8,128)(2,1)S(1)}, u32[]{:S(2)}, u32[]{:S(2)}) %collective-permute-start.12) | collective-permute-done | bytes 131104 | tf_op jit(solution)/shard_map/ppermute | solution.py:423
  44.7 1.4 %shard_map.127 = (bf16[528,128]{1,0:T(8,128)(2,1)S(1)}, f32[2]{0:T(128)}) custom-call(s32[4]{0:T(128)S(1)} %pad_add_fusion.idx, bf16[544,128]{1,0:T(8,128)(2,1)S(1)} %collective-permute-done.11.s0_ref, bf16[512,128]{1,0:T(8,128)(2,1)S(1)} %collective-permute-done.12.s1_ref, bf16[16,128]{1,0:T(8,128)(2,1)S(1)} %get-tuple-element.45.refs_8_.rgb_ref, ...), custom_call_target="tpu_custom_call" | custom-call | tf_op jit(solution)/shard_map/pallas_call | solution.py:396
  46.1 1.6 %shard_map.129 = (f32[1024,128]{1,0:T(8,128)S(1)}, bf16[1024,128]{1,0:T(8,128)(2,1)S(1)}, f32[512,1152]{1,0:T(8,128)S(1)}) custom-call(bf16[528,128]{1,0:T(8,128)(2,1)S(1)} %get-tuple-element.59.pay_ref, bf16[512,1152]{1,0:T(8,128)(2,1)S(1)} %get-tuple-element.42.refs_5_.wslot_ref, f32[2,512]{1,0:T(2,128)S(1)} %get-tuple-element.41.refs_4_.stys_ref, ...), custom_call_target="tpu_custom_call" | custom-call | tf_op jit(solution)/shard_map/pallas_call | solution.py:396
  47.7 2.5 %collective-permute-start.13 = (bf16[528,128]{1,0:T(8,128)(2,1)S(1)}, bf16[528,128]{1,0:T(8,128)(2,1)S(1)}, u32[]{:S(2)}, u32[]{:S(2)}) collective-permute-start(bf16[528,128]{1,0:T(8,128)(2,1)S(1)} %get-tuple-element.59.pay_ref), channel_id=1, source_target_pairs={{0,8},{1,57},{2,10},{3,59},{8,0},{9,17},{10,2},{11,19},{16,24},{17... | collective-permute-start | bytes 405512 | tf_op jit(solution)/shard_map/ppermute | solution.py:432
  50.3 2.6 %collective-permute-done.13.other_pay_ref = bf16[528,128]{1,0:T(8,128)(2,1)S(1)} collective-permute-done((bf16[528,128]{1,0:T(8,128)(2,1)S(1)}, bf16[528,128]{1,0:T(8,128)(2,1)S(1)}, u32[]{:S(2)}, u32[]{:S(2)}) %collective-permute-start.13) | collective-permute-done | bytes 135200 | tf_op jit(solution)/shard_map/ppermute | solution.py:432
  52.9 2.2 %shard_map.130 = (f32[576,128]{1,0:T(8,128)S(1)}, bf16[576,128]{1,0:T(8,128)(2,1)S(1)}, bf16[576,128]{1,0:T(8,128)(2,1)S(1)}, bf16[576,128]{1,0:T(8,128)(2,1)S(1)}) custom-call(s32[4]{0:T(128)S(1)} %pad_add_fusion.idx, bf16[528,128]{1,0:T(8,128)(2,1)S(1)} %get-tuple-element.59.pay_ref, bf16[528,128]{1,0:T(8,128)(2,1)S(1)} %collective-permute-done.13.other_pay_ref, ...), custom_call_target="tpu_custom_call" | custom-call | tf_op jit(solution)/shard_map/pallas_call | solution.py:396
  55.1 2.8 %collective-permute-start.15 = (bf16[576,128]{1,0:T(8,128)(2,1)S(1)}, bf16[576,128]{1,0:T(8,128)(2,1)S(1)}, u32[]{:S(2)}, u32[]{:S(2)}) collective-permute-start(bf16[576,128]{1,0:T(8,128)(2,1)S(1)} %get-tuple-element.65), channel_id=1, source_target_pairs={{0,64},{1,193},{2,66},{3,195},{8,72},{9,201},{10,74},{11,203},{16,... | collective-permute-start | bytes 442376 | tf_op jit(solution)/shard_map/ppermute | solution.py:432
  59.1 4.7 %collective-permute-done.15.r1_ref = bf16[576,128]{1,0:T(8,128)(2,1)S(1)} collective-permute-done((bf16[576,128]{1,0:T(8,128)(2,1)S(1)}, bf16[576,128]{1,0:T(8,128)(2,1)S(1)}, u32[]{:S(2)}, u32[]{:S(2)}) %collective-permute-start.15) | collective-permute-done | bytes 147488 | tf_op jit(solution)/shard_map/ppermute | solution.py:432
  63.9 1.4 %collective-permute-done.16.r2_ref = bf16[576,128]{1,0:T(8,128)(2,1)S(1)} collective-permute-done((bf16[576,128]{1,0:T(8,128)(2,1)S(1)}, bf16[576,128]{1,0:T(8,128)(2,1)S(1)}, u32[]{:S(2)}, u32[]{:S(2)}) %collective-permute-start.16) | collective-permute-done | bytes 147488 | tf_op jit(solution)/shard_map/ppermute | solution.py:432
  65.3 1.6 %collective-permute-done.17.r3_ref = bf16[576,128]{1,0:T(8,128)(2,1)S(1)} collective-permute-done((bf16[576,128]{1,0:T(8,128)(2,1)S(1)}, bf16[576,128]{1,0:T(8,128)(2,1)S(1)}, u32[]{:S(2)}, u32[]{:S(2)}) %collective-permute-start.17) | collective-permute-done | bytes 147488 | tf_op jit(solution)/shard_map/ppermute | solution.py:432
  67.1 3.9 %collective-permute-start.19 = (bf16[144,128]{1,0:T(8,128)(2,1)S(1)}, bf16[144,128]{1,0:T(8,128)(2,1)S(1)}, u32[]{:S(2)}, u32[]{:S(2)}) collective-permute-start(bf16[144,128]{1,0:T(8,128)(2,1)S(1)} %get-tuple-element.70), channel_id=1, source_target_pairs={{0,32},{8,40},{16,48},{24,56},{32,0},{40,8},{48,16},{56,24},{64,96... | collective-permute-start | bytes 110600 | tf_op jit(solution)/shard_map/ppermute | solution.py:438
  71.0 3.5 %collective-permute-start.20 = (bf16[144,128]{1,0:T(8,128)(2,1)S(1)}, bf16[144,128]{1,0:T(8,128)(2,1)S(1)}, u32[]{:S(2)}, u32[]{:S(2)}) collective-permute-start(bf16[144,128]{1,0:T(8,128)(2,1)S(1)} %get-tuple-element.71), channel_id=1, source_target_pairs={{0,48},{8,56},{16,0},{24,8},{32,16},{40,24},{48,32},{56,40},{64,11... | collective-permute-start | bytes 110600 | tf_op jit(solution)/shard_map/ppermute | solution.py:438
  74.4 1.1 %collective-permute-done.20.refs_3_ = bf16[144,128]{1,0:T(8,128)(2,1)S(1)} collective-permute-done((bf16[144,128]{1,0:T(8,128)(2,1)S(1)}, bf16[144,128]{1,0:T(8,128)(2,1)S(1)}, u32[]{:S(2)}, u32[]{:S(2)}) %collective-permute-start.20) | collective-permute-done | bytes 36896 | tf_op jit(solution)/shard_map/ppermute | solution.py:438
  (32 shorter events, 4.8 us)
Async XLA Ops:
  0.6 12.4 %copy-start.1 = (bf16[2,128,256]{2,1,0:T(8,128)(2,1)S(1)}, bf16[2,128,256]{2,1,0:T(8,128)(2,1)}, u32[]{:S(2)}) copy-start(bf16[2,128,256]{2,1,0:T(8,128)(2,1)} %refs_0_.1) | copy-start | bytes 393220
  0.6 6.0 %collective-permute-start.1 = (bf16[2,128,256]{2,1,0:T(8,128)(2,1)}, bf16[2,128,256]{2,1,0:T(8,128)(2,1)S(1)}, u32[]{:S(2)}, u32[]{:S(2)}) collective-permute-start(bf16[2,128,256]{2,1,0:T(8,128)(2,1)} %refs_0_.1), channel_id=1, source_target_pairs={{0,6},{1,7},{2,4},{3,5},{4,2},{5,3},{6,0},{7,1},{8,14},{9,15},{10,... | collective-permute-start | bytes 393224 | tf_op jit(solution)/shard_map/ppermute | solution.py:423
  4.0 9.0 %collective-permute-start = (bf16[2,128,256]{2,1,0:T(8,128)(2,1)}, bf16[2,128,256]{2,1,0:T(8,128)(2,1)S(1)}, u32[]{:S(2)}, u32[]{:S(2)}) collective-permute-start(bf16[2,128,256]{2,1,0:T(8,128)(2,1)} %refs_0_.1), channel_id=1, source_target_pairs={{0,1},{1,0},{2,3},{3,2},{4,5},{5,4},{6,7},{7,6},{8,9},{9,8},{10,11... | collective-permute-start | bytes 393224 | tf_op jit(solution)/shard_map/ppermute | solution.py:423
  6.6 6.4 %collective-permute-start.2 = (bf16[2,128,256]{2,1,0:T(8,128)(2,1)S(1)}, bf16[2,128,256]{2,1,0:T(8,128)(2,1)S(1)}, u32[]{:S(2)}, u32[]{:S(2)}) collective-permute-start(bf16[2,128,256]{2,1,0:T(8,128)(2,1)S(1)} %collective-permute-done.1.refs_2_), channel_id=1, source_target_pairs={{0,1},{1,0},{2,3},{3,2},{4,5},{5,4},{6,7},{7,6},{8,9},{9,8},{10,11... | collective-permute-start | bytes 393224 | tf_op jit(solution)/shard_map/ppermute | solution.py:423
  14.1 5.2 %collective-permute-start.3 = (bf16[528,128]{1,0:T(8,128)(2,1)S(1)}, bf16[528,128]{1,0:T(8,128)(2,1)S(1)}, u32[]{:S(2)}, u32[]{:S(2)}) collective-permute-start(bf16[528,128]{1,0:T(8,128)(2,1)S(1)} %get-tuple-element.46), channel_id=1, source_target_pairs={{0,4},{1,5},{2,6},{3,7},{4,0},{5,1},{6,2},{7,3},{8,12},{9,13},{10,... | collective-permute-start | bytes 405512 | tf_op jit(solution)/shard_map/ppermute | solution.py:423
  14.2 6.4 %collective-permute-start.5 = (bf16[528,128]{1,0:T(8,128)(2,1)S(1)}, bf16[528,128]{1,0:T(8,128)(2,1)S(1)}, u32[]{:S(2)}, u32[]{:S(2)}) collective-permute-start(bf16[528,128]{1,0:T(8,128)(2,1)S(1)} %get-tuple-element.46), channel_id=1, source_target_pairs={{0,6},{1,7},{2,4},{3,5},{4,2},{5,3},{6,0},{7,1},{8,14},{9,15},{10,... | collective-permute-start | bytes 405512 | tf_op jit(solution)/shard_map/ppermute | solution.py:423
  19.4 2.2 %collective-permute-start.4 = (bf16[528,128]{1,0:T(8,128)(2,1)S(1)}, bf16[528,128]{1,0:T(8,128)(2,1)S(1)}, u32[]{:S(2)}, u32[]{:S(2)}) collective-permute-start(bf16[528,128]{1,0:T(8,128)(2,1)S(1)} %collective-permute-done.3.refs_0_), channel_id=1, source_target_pairs={{0,1},{1,0},{2,3},{3,2},{4,5},{5,4},{6,7},{7,6},{8,9},{9,8},{10,11... | collective-permute-start | bytes 405512 | tf_op jit(solution)/shard_map/ppermute | solution.py:423
  20.7 1.9 %collective-permute-start.6 = (bf16[528,128]{1,0:T(8,128)(2,1)S(1)}, bf16[528,128]{1,0:T(8,128)(2,1)S(1)}, u32[]{:S(2)}, u32[]{:S(2)}) collective-permute-start(bf16[528,128]{1,0:T(8,128)(2,1)S(1)} %collective-permute-done.5.refs_2_), channel_id=1, source_target_pairs={{0,1},{1,0},{2,3},{3,2},{4,5},{5,4},{6,7},{7,6},{8,9},{9,8},{10,11... | collective-permute-start | bytes 405512 | tf_op jit(solution)/shard_map/ppermute | solution.py:423
  24.2 3.9 %collective-permute-start.7 = (f32[8,512]{1,0:T(8,128)S(1)}, f32[8,512]{1,0:T(8,128)S(1)}, u32[]{:S(2)}, u32[]{:S(2)}) collective-permute-start(f32[8,512]{1,0:T(8,128)S(1)} %get-tuple-element.47.own_ref), channel_id=1, source_target_pairs={{0,1},{1,0},{2,3},{3,2},{4,5},{5,4},{6,7},{7,6},{8,9},{9,8},{10,11... | collective-permute-start | bytes 49160 | tf_op jit(solution)/shard_map/ppermute | solution.py:423
  24.6 4.1 %collective-permute-start.8 = (f32[8,512]{1,0:T(8,128)S(1)}, f32[8,512]{1,0:T(8,128)S(1)}, u32[]{:S(2)}, u32[]{:S(2)}) collective-permute-start(f32[8,512]{1,0:T(8,128)S(1)} %get-tuple-element.47.own_ref), channel_id=1, source_target_pairs={{0,2},{1,3},{2,0},{3,1},{4,6},{5,7},{6,4},{7,5},{8,10},{9,11},{10,... | collective-permute-start | bytes 49160 | tf_op jit(solution)/shard_map/ppermute | solution.py:423
  25.5 4.7 %collective-permute-start.9 = (f32[8,512]{1,0:T(8,128)S(1)}, f32[8,512]{1,0:T(8,128)S(1)}, u32[]{:S(2)}, u32[]{:S(2)}) collective-permute-start(f32[8,512]{1,0:T(8,128)S(1)} %get-tuple-element.47.own_ref), channel_id=1, source_target_pairs={{0,3},{1,2},{2,1},{3,0},{4,7},{5,6},{6,5},{7,4},{8,11},{9,10},{10,... | collective-permute-start | bytes 49160 | tf_op jit(solution)/shard_map/ppermute | solution.py:423
  31.9 6.9 %collective-permute-start.10 = (bf16[1024,128]{1,0:T(8,128)(2,1)S(1)}, bf16[1024,128]{1,0:T(8,128)(2,1)S(1)}, u32[]{:S(2)}, u32[]{:S(2)}) collective-permute-start(bf16[1024,128]{1,0:T(8,128)(2,1)S(1)} %get-tuple-element.52), channel_id=1, source_target_pairs={{0,1},{1,0},{2,3},{3,2},{4,5},{5,4},{6,7},{7,6},{8,9},{9,8},{10,11... | collective-permute-start | bytes 786440 | tf_op jit(solution)/shard_map/ppermute | solution.py:423
  33.1 17.1 %collective-permute-start.14 = (bf16[528,512]{1,0:T(8,128)(2,1)S(1)}, bf16[528,512]{1,0:T(8,128)(2,1)S(1)}, u32[]{:S(2)}, u32[]{:S(2)}) collective-permute-start(bf16[528,512]{1,0:T(8,128)(2,1)S(1)} %shard_map.128.xm_ref), channel_id=1, source_target_pairs={{0,8},{1,57},{2,10},{3,59},{8,0},{9,17},{10,2},{11,19},{16,24},{17... | collective-permute-start | bytes 1622024 | tf_op jit(solution)/shard_map/ppermute | solution.py:432
  38.9 5.8 %collective-permute-start.11 = (bf16[544,128]{1,0:T(8,128)(2,1)S(1)}, bf16[544,128]{1,0:T(8,128)(2,1)S(1)}, u32[]{:S(2)}, u32[]{:S(2)}) collective-permute-start(bf16[544,128]{1,0:T(8,128)(2,1)S(1)} %get-tuple-element.54), channel_id=1, source_target_pairs={{0,4},{1,5},{2,6},{3,7},{4,0},{5,1},{6,2},{7,3},{8,12},{9,13},{10,... | collective-permute-start | bytes 417800 | tf_op jit(solution)/shard_map/ppermute | solution.py:423
  39.7 5.0 %collective-permute-start.12 = (bf16[512,128]{1,0:T(8,128)(2,1)S(1)}, bf16[512,128]{1,0:T(8,128)(2,1)S(1)}, u32[]{:S(2)}, u32[]{:S(2)}) collective-permute-start(bf16[512,128]{1,0:T(8,128)(2,1)S(1)} %get-tuple-element.55), channel_id=1, source_target_pairs={{0,6},{1,7},{2,4},{3,5},{4,2},{5,3},{6,0},{7,1},{8,14},{9,15},{10,... | collective-permute-start | bytes 393224 | tf_op jit(solution)/shard_map/ppermute | solution.py:423
  44.7 8.2 %copy-start = (bf16[1,4608,128]{2,1,0:T(8,128)(2,1)S(1)}, bf16[1,4608,128]{2,1,0:T(8,128)(2,1)}, u32[]{:S(2)}) copy-start(bf16[1,4608,128]{2,1,0:T(8,128)(2,1)} %param.13) | copy-start | bytes 3538948
  47.6 11.3 %collective-permute-start.21 = (bf16[1024,128]{1,0:T(8,128)(2,1)S(1)}, bf16[1024,128]{1,0:T(8,128)(2,1)S(1)}, u32[]{:S(2)}, u32[]{:S(2)}) collective-permute-start(bf16[1024,128]{1,0:T(8,128)(2,1)S(1)} %get-tuple-element.73), channel_id=1, source_target_pairs={{0,1},{1,0},{2,3},{3,2},{4,5},{5,4},{6,7},{7,6},{8,9},{9,8},{10,11... | collective-permute-start | bytes 786440 | tf_op jit(solution)/shard_map/ppermute | solution.py:423
  47.7 5.2 %collective-permute-start.13 = (bf16[528,128]{1,0:T(8,128)(2,1)S(1)}, bf16[528,128]{1,0:T(8,128)(2,1)S(1)}, u32[]{:S(2)}, u32[]{:S(2)}) collective-permute-start(bf16[528,128]{1,0:T(8,128)(2,1)S(1)} %get-tuple-element.59.pay_ref), channel_id=1, source_target_pairs={{0,8},{1,57},{2,10},{3,59},{8,0},{9,17},{10,2},{11,19},{16,24},{17... | collective-permute-start | bytes 405512 | tf_op jit(solution)/shard_map/ppermute | solution.py:432
  55.1 8.8 %collective-permute-start.15 = (bf16[576,128]{1,0:T(8,128)(2,1)S(1)}, bf16[576,128]{1,0:T(8,128)(2,1)S(1)}, u32[]{:S(2)}, u32[]{:S(2)}) collective-permute-start(bf16[576,128]{1,0:T(8,128)(2,1)S(1)} %get-tuple-element.65), channel_id=1, source_target_pairs={{0,64},{1,193},{2,66},{3,195},{8,72},{9,201},{10,74},{11,203},{16,... | collective-permute-start | bytes 442376 | tf_op jit(solution)/shard_map/ppermute | solution.py:432
  57.9 7.4 %collective-permute-start.16 = (bf16[576,128]{1,0:T(8,128)(2,1)S(1)}, bf16[576,128]{1,0:T(8,128)(2,1)S(1)}, u32[]{:S(2)}, u32[]{:S(2)}) collective-permute-start(bf16[576,128]{1,0:T(8,128)(2,1)S(1)} %get-tuple-element.66), channel_id=1, source_target_pairs={{0,128},{1,129},{2,130},{3,131},{8,136},{9,137},{10,138},{11,139},... | collective-permute-start | bytes 442376 | tf_op jit(solution)/shard_map/ppermute | solution.py:432
  58.3 8.6 %collective-permute-start.17 = (bf16[576,128]{1,0:T(8,128)(2,1)S(1)}, bf16[576,128]{1,0:T(8,128)(2,1)S(1)}, u32[]{:S(2)}, u32[]{:S(2)}) collective-permute-start(bf16[576,128]{1,0:T(8,128)(2,1)S(1)} %get-tuple-element.67), channel_id=1, source_target_pairs={{0,192},{1,65},{2,194},{3,67},{8,200},{9,73},{10,202},{11,75},{16,... | collective-permute-start | bytes 442376 | tf_op jit(solution)/shard_map/ppermute | solution.py:432
  59.0 16.6 %collective-permute-start.22 = (bf16[512,128]{1,0:T(8,128)(2,1)S(1)}, bf16[512,128]{1,0:T(8,128)(2,1)S(1)}, u32[]{:S(2)}, u32[]{:S(2)}) collective-permute-start(bf16[512,128]{1,0:T(8,128)(2,1)S(1)} %get-tuple-element.75), channel_id=1, source_target_pairs={{0,2},{1,3},{2,0},{3,1},{4,6},{5,7},{6,4},{7,5},{8,10},{9,11},{10,... | collective-permute-start | bytes 393224 | tf_op jit(solution)/shard_map/ppermute | solution.py:423
  67.0 7.5 %collective-permute-start.18 = (bf16[144,128]{1,0:T(8,128)(2,1)S(1)}, bf16[144,128]{1,0:T(8,128)(2,1)S(1)}, u32[]{:S(2)}, u32[]{:S(2)}) collective-permute-start(bf16[144,128]{1,0:T(8,128)(2,1)S(1)} %get-tuple-element.69), channel_id=1, source_target_pairs={{0,16},{8,24},{16,32},{24,40},{32,48},{40,56},{48,0},{56,8},{64,80... | collective-permute-start | bytes 110600 | tf_op jit(solution)/shard_map/ppermute | solution.py:438
  67.1 7.4 %collective-permute-start.19 = (bf16[144,128]{1,0:T(8,128)(2,1)S(1)}, bf16[144,128]{1,0:T(8,128)(2,1)S(1)}, u32[]{:S(2)}, u32[]{:S(2)}) collective-permute-start(bf16[144,128]{1,0:T(8,128)(2,1)S(1)} %get-tuple-element.70), channel_id=1, source_target_pairs={{0,32},{8,40},{16,48},{24,56},{32,0},{40,8},{48,16},{56,24},{64,96... | collective-permute-start | bytes 110600 | tf_op jit(solution)/shard_map/ppermute | solution.py:438
  71.0 4.6 %collective-permute-start.20 = (bf16[144,128]{1,0:T(8,128)(2,1)S(1)}, bf16[144,128]{1,0:T(8,128)(2,1)S(1)}, u32[]{:S(2)}, u32[]{:S(2)}) collective-permute-start(bf16[144,128]{1,0:T(8,128)(2,1)S(1)} %get-tuple-element.71), channel_id=1, source_target_pairs={{0,48},{8,56},{16,0},{24,8},{32,16},{40,24},{48,32},{56,40},{64,11... | collective-permute-start | bytes 110600 | tf_op jit(solution)/shard_map/ppermute | solution.py:438

commit v3 on v2

--- a/solution.py
+++ b/solution.py
@@ -137,6 +137,10 @@
         refs[13][...] = lax.dot_general(rgb, y, NT, preferred_element_type=f32)[:8]
 
 
+def image_pair_kernel(own_ref, got_ref, out_ref):
+    out_ref[...] = own_ref[...] + got_ref[...]
+
+
 def first_image_kernel(*refs):
     out_ref = refs[-1]
     pixels = out_ref.shape[1]
@@ -193,10 +197,10 @@
 
 
 def disc_kernel(
-    own_ref, r1_ref, r2_ref, r3_ref, first_ref, disc_ref, rgb_ref, slope_ref, z_ref, demod_ref,
+    own_ref, other_ref, first_ref, disc_ref, rgb_ref, slope_ref, z_ref, demod_ref,
     wslot_ref, stys_ref, tail_ref, pay_ref, keep_ref, send_ref,
 ):
-    image = ((own_ref[...] + r1_ref[...]) + (r2_ref[...] + r3_ref[...])) + first_ref[...]
+    image = (own_ref[...] + other_ref[...]) + first_ref[...]
     lanes = 128
     per = PIX // lanes
     count = stys_ref.shape[0]
@@ -218,7 +222,8 @@
             )
         logit = logit / PIX
         e = jnp.exp(-jnp.abs(logit))
-        g = -jnp.where(logit >= 0.0, e, 1.0) / (1.0 + e)
+        under = 1.0 + e
+        g = jnp.where(logit >= 0.0, (1.0 - under) / under, e / under - 1.0)
         rows = [jnp.concatenate([c[ch] for c in chunks], axis=1) * g for ch in range(3)]
         out_rows.append(jnp.concatenate(rows + [jnp.zeros((5, PIX), f32)], axis=0))
         wide = jnp.broadcast_to(logit, (1, lanes))
@@ -338,7 +343,7 @@
     pixels = pay_ref.shape[0] - EXTRA
     count = pixels // PIX
     cols = shifted_gz(other_pay_ref[:pixels, :])
-    total = before_ref[...] + jnp.dot(other_xm_ref[:full, :], cols, preferred_element_type=f32)
+    other_xm = other_xm_ref[:full, :]
     sty_rows, coef_rows = [], []
     for pay, xm in ((pay_ref, xm_ref), (other_pay_ref, other_xm_ref)):
         tail = xm[full:, :].astype(f32)
@@ -349,9 +354,16 @@
     left = pad_rows(jnp.concatenate(sty_rows, axis=0), own).T
     right = pad_rows(jnp.concatenate(coef_rows, axis=0), own)
     demod_term = jnp.dot(left, right, precision=lax.Precision.HIGHEST, preferred_element_type=f32)
-    for k in range(TAPS):
-        at = slice(k * full, (k + 1) * full)
-        sum_ref[at, :] = total[:, k * own : (k + 1) * own] + w_ref[at, :].astype(f32) * demod_term
+    for first in range(0, TAPS, 2):
+        taps = range(first, min(first + 2, TAPS))
+        lanes = slice(first * own, (taps[-1] + 1) * own)
+        total = before_ref[:, lanes] + jnp.dot(
+            other_xm, cols[:, lanes], preferred_element_type=f32
+        )
+        for n, k in enumerate(taps):
+            at = slice(k * full, (k + 1) * full)
+            w = w_ref[at, :].astype(f32)
+            sum_ref[at, :] = total[:, n * own : (n + 1) * own] + w * demod_term
     rows = keep_ref.shape[0] // 4
     step = 1 - 2 * core
     for d, ref in enumerate((keep_ref, send_1_ref, send_2_ref, send_3_ref)):
@@ -371,13 +383,15 @@
         ref[...] = total.astype(ref.dtype)
 
 
-def total_kernel(count, *refs):
-    grad_ref, dx_ref = refs[-2:]
+def total_kernel(*refs):
     total = refs[0][...].astype(f32)
-    for ref in refs[1:count]:
+    for ref in refs[1:-1]:
         total = total + ref[...].astype(f32)
-    grad_ref[...] = total
-    dx = (refs[count][...] + refs[count + 1][...].astype(f32)).astype(bf16)
+    refs[-1][...] = total
+
+
+def input_grad_kernel(near_ref, far_ref, dx_ref):
+    dx = (near_ref[...] + far_ref[...].astype(f32)).astype(bf16)
     for b in range(dx_ref.shape[0]):
         dx_ref[b] = dx[b * PIX : (b + 1) * PIX].T
 
@@ -489,7 +503,9 @@
         conv_outs + [((8, pixels), f32)],
         [y0, y1, y2, y3, stys, wslot, demod, nb, rgbp],
     )
-    images = [within(image_own, d) for d in (1, 2, 3)]
+    image_got = within(image_own, 1)
+    (image_chip,) = call(image_pair_kernel, [((8, pixels), f32)], [image_own, image_got])
+    image_other = within(image_chip, 2)
     (xm,) = call(turn_kernel, [((full + EXTRA, pixels), bf16)], [idx, xm_a, xm_b, sty], scalars=1)
     (image_first,) = call(first_image_kernel, [((8, pixels), f32)], [y0, y1, y2, y3])
 
@@ -501,7 +517,7 @@
     tail, pay_b, dx_keep, dx_send = call(
         disc_kernel,
         [((TAIL, own), bf16), ((pixels + EXTRA, own), bf16), (two, f32), (two, bf16)],
-        [image_own, *images, image_first, disc, rgbp, slope_b, z_b, demod, wslot, stys],
+        [image_chip, image_other, image_first, disc, rgbp, slope_b, z_b, demod, wslot, stys],
     )
     dx_got = within(dx_send, 1)
     share = ((pixels, own), bf16)
@@ -535,12 +551,8 @@
     block = (rows, own)
     z_own, *z_outs = call(y_sum_kernel, [(block, f32)] + [(block, bf16)] * 3, [y_keep, *y_got])
     parts = [z_own] + [over_z(z_outs[e - 1], 2 * e) for e in (1, 2, 3)]
-    grad_rows, dx = call(
-        functools.partial(total_kernel, len(parts)),
-        [((rows, own), f32), ((count, own, PIX), bf16)],
-        [*parts, *mine],
-        keep=False,
-    )
+    (dx,) = call(input_grad_kernel, [((count, own, PIX), bf16)], mine, keep=False)
+    (grad_rows,) = call(total_kernel, [((rows, own), f32)], parts, keep=False)
     return (grad_rows[None], logits, dx[None])
 
 

time: 76.4 us -> 76.1 us (level)
  the two profiles are of different devices: /device:TPU:1 before, /device:TPU:4 now
where the time goes in v3:
time: 76.1 us; the launch traced here: 75.8 us
  waiting for transfers between devices  31.8 us (42%)
  starting transfers between devices  28.5 us (37%)
  Pallas kernels  14.6 us (19%)
    ppermute x14, waiting for transfers between devices, across(): return lax.ppermute(value, ('segment', 'chan'), links)  19.3 us
    pallas_call x15, Pallas kernels, call(): pl.pallas_call(kernel, out_shape=[jax.ShapeDtypeStruct(*o[:2]) if len(o)...  14.6 us
    ppermute x14, starting transfers between devices, across(): return lax.ppermute(value, ('segment', 'chan'), links)  13 us
    ppermute x5, waiting for transfers between devices, by_core(): return lax.ppermute(value, ('dp', 'chan'), links)  9.07 us
    ppermute x5, starting transfers between devices, by_core(): return lax.ppermute(value, ('dp', 'chan'), links)  7.92 us
    ppermute x3, starting transfers between devices, over_z(): lax.ppermute(value, 'dp', [(y * 8 + z, y * 8 + (z + d) % 8) for y in rang...  7.57 us
    ppermute x3, waiting for transfers between devices, over_z(): lax.ppermute(value, 'dp', [(y * 8 + z, y * 8 + (z + d) % 8) for y in rang...  3.42 us
  transfers between devices with their start and end apart: 22, of which 11 were waited for; matrix products, arithmetic and copies ran while one was open for 0% of the time, Pallas kernels for 12%

profile of v3, /device:TPU:4, one launch (start us, length us, event | category | flops | bytes accessed | tf_op | source)
XLA Modules:
  0.0 75.8 jit_solution(1410358563301698905)
XLA Ops:
  1.3 4.9 %collective-permute-done.1.refs_2_ = bf16[2,128,256]{2,1,0:T(8,128)(2,1)S(1)} collective-permute-done((bf16[2,128,256]{2,1,0:T(8,128)(2,1)}, bf16[2,128,256]{2,1,0:T(8,128)(2,1)S(1)}, u32[]{:S(2)}, u32[]{:S(2)}) %collective-permute-start.1) | collective-permute-done | bytes 131104 | tf_op jit(solution)/shard_map/ppermute | solution.py:437
  6.3 2.6 %shard_map.121 = (bf16[512,1152]{1,0:T(8,128)(2,1)S(1)}, f32[2,512]{1,0:T(2,128)S(1)}, f32[2,128]{1,0:T(2,128)S(1)}, f32[512,128]{1,0:T(8,128)S(1)}, f32[5,256,1...) custom-call(s32[4]{0:T(128)S(1)} %pad_add_fusion.idx, bf16[4608,128]{1,0:T(8,128)(2,1)} %bitcast.12, ...), custom_call_target="tpu_custom_call" | custom-call | tf_op jit(solution)/shard_map/pallas_call | solution.py:410
  8.9 1.1 %shard_map.122 = (bf16[528,128]{1,0:T(8,128)(2,1)S(1)}, f32[512,128]{1,0:T(8,128)S(1)}, f32[512,128]{1,0:T(8,128)S(1)}, bf16[512,512]{1,0:T(8,128)(2,1)S(1)}) custom-call(bf16[2,128,256]{2,1,0:T(8,128)(2,1)S(1)} %copy-done.1, bf16[2,128,256]{2,1,0:T(8,128)(2,1)S(1)} %collective-permute-done.refs_1_, bf16[2,128,256]{2,1,0:T(8,128)(2,1)S(1)} %collective-permute-done.1.refs_2_, ...), custom_call_target="tpu_custom_call" | custom-call | tf_op jit(solution)/shard_map/pallas_call | solution.py:410
  10.0 2.5 %collective-permute-start.3 = (bf16[528,128]{1,0:T(8,128)(2,1)S(1)}, bf16[528,128]{1,0:T(8,128)(2,1)S(1)}, u32[]{:S(2)}, u32[]{:S(2)}) collective-permute-start(bf16[528,128]{1,0:T(8,128)(2,1)S(1)} %get-tuple-element.44), channel_id=1, source_target_pairs={{0,4},{1,5},{2,6},{3,7},{4,0},{5,1},{6,2},{7,3},{8,12},{9,13},{10,... | collective-permute-start | bytes 405512 | tf_op jit(solution)/shard_map/ppermute | solution.py:437
  12.5 1.3 %collective-permute-start.5 = (bf16[528,128]{1,0:T(8,128)(2,1)S(1)}, bf16[528,128]{1,0:T(8,128)(2,1)S(1)}, u32[]{:S(2)}, u32[]{:S(2)}) collective-permute-start(bf16[528,128]{1,0:T(8,128)(2,1)S(1)} %get-tuple-element.44), channel_id=1, source_target_pairs={{0,6},{1,7},{2,4},{3,5},{4,2},{5,3},{6,0},{7,1},{8,14},{9,15},{10,... | collective-permute-start | bytes 405512 | tf_op jit(solution)/shard_map/ppermute | solution.py:437
  13.8 2.9 %collective-permute-done.3.refs_0_ = bf16[528,128]{1,0:T(8,128)(2,1)S(1)} collective-permute-done((bf16[528,128]{1,0:T(8,128)(2,1)S(1)}, bf16[528,128]{1,0:T(8,128)(2,1)S(1)}, u32[]{:S(2)}, u32[]{:S(2)}) %collective-permute-start.3) | collective-permute-done | bytes 135200 | tf_op jit(solution)/shard_map/ppermute | solution.py:437
  16.8 1.5 %collective-permute-done.5.refs_2_ = bf16[528,128]{1,0:T(8,128)(2,1)S(1)} collective-permute-done((bf16[528,128]{1,0:T(8,128)(2,1)S(1)}, bf16[528,128]{1,0:T(8,128)(2,1)S(1)}, u32[]{:S(2)}, u32[]{:S(2)}) %collective-permute-start.5) | collective-permute-done | bytes 135200 | tf_op jit(solution)/shard_map/ppermute | solution.py:437
  18.2 1.3 %collective-permute-done.6.refs_3_ = bf16[528,128]{1,0:T(8,128)(2,1)S(1)} collective-permute-done((bf16[528,128]{1,0:T(8,128)(2,1)S(1)}, bf16[528,128]{1,0:T(8,128)(2,1)S(1)}, u32[]{:S(2)}, u32[]{:S(2)}) %collective-permute-start.6) | collective-permute-done | bytes 135200 | tf_op jit(solution)/shard_map/ppermute | solution.py:437
  19.6 1.7 %shard_map.123 = (bf16[528,128]{1,0:T(8,128)(2,1)}, f32[512,128]{1,0:T(8,128)S(1)}, f32[512,128]{1,0:T(8,128)S(1)}, bf16[512,512]{1,0:T(8,128)(2,1)S(1)}, f32[8,512]{1,0:T(8,128)S(1)}) custom-call(bf16[528,128]{1,0:T(8,128)(2,1)S(1)} %collective-permute-done.3.refs_0_, bf16[528,128]{1,0:T(8,128)(2,1)S(1)} %collective-permute-done.4.refs_1_, ...), custom_call_target="tpu_custom_call" | custom-call | tf_op jit(solution)/shard_map/pallas_call | solution.py:410
  21.4 1.0 %collective-permute-done.7.got_ref = f32[8,512]{1,0:T(8,128)S(1)} collective-permute-done((f32[8,512]{1,0:T(8,128)S(1)}, f32[8,512]{1,0:T(8,128)S(1)}, u32[]{:S(2)}, u32[]{:S(2)}) %collective-permute-start.7) | collective-permute-done | bytes 16416 | tf_op jit(solution)/shard_map/ppermute | solution.py:437
  22.4 2.3 %collective-permute-start.8 = (f32[8,512]{1,0:T(8,128)S(1)}, f32[8,512]{1,0:T(8,128)S(1)}, u32[]{:S(2)}, u32[]{:S(2)}) collective-permute-start(f32[8,512]{1,0:T(8,128)S(1)} %shard_map.124.own_ref), channel_id=1, source_target_pairs={{0,2},{1,3},{2,0},{3,1},{4,6},{5,7},{6,4},{7,5},{8,10},{9,11},{10,... | collective-permute-start | bytes 49160 | tf_op jit(solution)/shard_map/ppermute | solution.py:437
  25.0 2.7 %collective-permute-done.8.other_ref = f32[8,512]{1,0:T(8,128)S(1)} collective-permute-done((f32[8,512]{1,0:T(8,128)S(1)}, f32[8,512]{1,0:T(8,128)S(1)}, u32[]{:S(2)}, u32[]{:S(2)}) %collective-permute-start.8) | collective-permute-done | bytes 16416 | tf_op jit(solution)/shard_map/ppermute | solution.py:437
  27.7 1.7 %shard_map.126 = (bf16[32,128]{1,0:T(8,128)(2,1)S(1)}, bf16[528,128]{1,0:T(8,128)(2,1)S(1)}, f32[1024,128]{1,0:T(8,128)S(1)}, bf16[1024,128]{1,0:T(8,128)(2,1)S(1)}) custom-call(f32[8,512]{1,0:T(8,128)S(1)} %shard_map.124.own_ref, f32[8,512]{1,0:T(8,128)S(1)} %collective-permute-done.8.other_ref, f32[8,512]{1,0:T(8,128)S(1)} %shard_map.125.first_ref, ...), custom_call_target="tpu_custom_call" | custom-call | tf_op jit(solution)/shard_map/pallas_call | solution.py:410
  29.5 0.8 %shard_map.129.xm_ref = bf16[528,512]{1,0:T(8,128)(2,1)S(1)} custom-call(s32[4]{0:T(128)S(1)} %pad_add_fusion.idx, bf16[512,512]{1,0:T(8,128)(2,1)S(1)} %get-tuple-element.58.xa_ref, bf16[512,512]{1,0:T(8,128)(2,1)S(1)} %get-tuple-element.59.xb_ref, f32[2,512]{1,0:T(2,128)S(1)} %get-tuple-element.60.sty_ref), custom_call_target="tpu_custom_call" | custom-call | tf_op jit(solution)/shard_map/pallas_call | solution.py:410
  30.3 2.0 %collective-permute-start.13 = (bf16[528,512]{1,0:T(8,128)(2,1)S(1)}, bf16[528,512]{1,0:T(8,128)(2,1)S(1)}, u32[]{:S(2)}, u32[]{:S(2)}) collective-permute-start(bf16[528,512]{1,0:T(8,128)(2,1)S(1)} %shard_map.129.xm_ref), channel_id=1, source_target_pairs={{0,8},{1,57},{2,10},{3,59},{8,0},{9,17},{10,2},{11,19},{16,24},{17... | collective-permute-start | bytes 1622024 | tf_op jit(solution)/shard_map/ppermute | solution.py:446
  32.3 1.7 %collective-permute-start.10 = (bf16[544,128]{1,0:T(8,128)(2,1)S(1)}, bf16[544,128]{1,0:T(8,128)(2,1)S(1)}, u32[]{:S(2)}, u32[]{:S(2)}) collective-permute-start(bf16[544,128]{1,0:T(8,128)(2,1)S(1)} %get-tuple-element.52), channel_id=1, source_target_pairs={{0,4},{1,5},{2,6},{3,7},{4,0},{5,1},{6,2},{7,3},{8,12},{9,13},{10,... | collective-permute-start | bytes 417800 | tf_op jit(solution)/shard_map/ppermute | solution.py:437
  34.1 4.9 %collective-permute-done.11.s1_ref = bf16[512,128]{1,0:T(8,128)(2,1)S(1)} collective-permute-done((bf16[512,128]{1,0:T(8,128)(2,1)S(1)}, bf16[512,128]{1,0:T(8,128)(2,1)S(1)}, u32[]{:S(2)}, u32[]{:S(2)}) %collective-permute-start.11) | collective-permute-done | bytes 131104 | tf_op jit(solution)/shard_map/ppermute | solution.py:437
  39.0 1.5 %shard_map.128 = (bf16[528,128]{1,0:T(8,128)(2,1)S(1)}, f32[2]{0:T(128)}) custom-call(s32[4]{0:T(128)S(1)} %pad_add_fusion.idx, bf16[544,128]{1,0:T(8,128)(2,1)S(1)} %collective-permute-done.10.s0_ref, bf16[512,128]{1,0:T(8,128)(2,1)S(1)} %collective-permute-done.11.s1_ref, bf16[16,128]{1,0:T(8,128)(2,1)S(1)} %get-tuple-element.43.refs_8_.rgb_ref, ...), custom_call_target="tpu_custom_call" | custom-call | tf_op jit(solution)/shard_map/pallas_call | solution.py:410
  40.5 1.6 %shard_map.130 = (f32[1024,128]{1,0:T(8,128)S(1)}, bf16[1024,128]{1,0:T(8,128)(2,1)S(1)}, f32[512,1152]{1,0:T(8,128)S(1)}) custom-call(bf16[528,128]{1,0:T(8,128)(2,1)S(1)} %get-tuple-element.57.pay_ref, bf16[512,1152]{1,0:T(8,128)(2,1)S(1)} %get-tuple-element.40.refs_5_.wslot_ref, f32[2,512]{1,0:T(2,128)S(1)} %get-tuple-element.39.refs_4_.stys_ref, ...), custom_call_target="tpu_custom_call" | custom-call | tf_op jit(solution)/shard_map/pallas_call | solution.py:410
  42.1 2.8 %collective-permute-start.20 = (bf16[1024,128]{1,0:T(8,128)(2,1)S(1)}, bf16[1024,128]{1,0:T(8,128)(2,1)S(1)}, u32[]{:S(2)}, u32[]{:S(2)}) collective-permute-start(bf16[1024,128]{1,0:T(8,128)(2,1)S(1)} %get-tuple-element.72), channel_id=1, source_target_pairs={{0,1},{1,0},{2,3},{3,2},{4,5},{5,4},{6,7},{7,6},{8,9},{9,8},{10,11... | collective-permute-start | bytes 786440 | tf_op jit(solution)/shard_map/ppermute | solution.py:437
  44.9 5.0 %collective-permute-done.12.other_pay_ref = bf16[528,128]{1,0:T(8,128)(2,1)S(1)} collective-permute-done((bf16[528,128]{1,0:T(8,128)(2,1)S(1)}, bf16[528,128]{1,0:T(8,128)(2,1)S(1)}, u32[]{:S(2)}, u32[]{:S(2)}) %collective-permute-start.12) | collective-permute-done | bytes 135200 | tf_op jit(solution)/shard_map/ppermute | solution.py:446
  49.9 1.8 %shard_map.131 = (f32[576,128]{1,0:T(8,128)S(1)}, bf16[576,128]{1,0:T(8,128)(2,1)S(1)}, bf16[576,128]{1,0:T(8,128)(2,1)S(1)}, bf16[576,128]{1,0:T(8,128)(2,1)S(1)}) custom-call(s32[4]{0:T(128)S(1)} %pad_add_fusion.idx, bf16[528,128]{1,0:T(8,128)(2,1)S(1)} %get-tuple-element.57.pay_ref, bf16[528,128]{1,0:T(8,128)(2,1)S(1)} %collective-permute-done.12.other_pay_ref, ...), custom_call_target="tpu_custom_call" | custom-call | tf_op jit(solution)/shard_map/pallas_call | solution.py:410
  51.8 1.7 %collective-permute-start.14 = (bf16[576,128]{1,0:T(8,128)(2,1)S(1)}, bf16[576,128]{1,0:T(8,128)(2,1)S(1)}, u32[]{:S(2)}, u32[]{:S(2)}) collective-permute-start(bf16[576,128]{1,0:T(8,128)(2,1)S(1)} %get-tuple-element.63), channel_id=1, source_target_pairs={{0,64},{1,193},{2,66},{3,195},{8,72},{9,201},{10,74},{11,203},{16,... | collective-permute-start | bytes 442376 | tf_op jit(solution)/shard_map/ppermute | solution.py:446
  53.4 2.9 %collective-permute-start.15 = (bf16[576,128]{1,0:T(8,128)(2,1)S(1)}, bf16[576,128]{1,0:T(8,128)(2,1)S(1)}, u32[]{:S(2)}, u32[]{:S(2)}) collective-permute-start(bf16[576,128]{1,0:T(8,128)(2,1)S(1)} %get-tuple-element.64), channel_id=1, source_target_pairs={{0,128},{1,129},{2,130},{3,131},{8,136},{9,137},{10,138},{11,139},... | collective-permute-start | bytes 442376 | tf_op jit(solution)/shard_map/ppermute | solution.py:446
  56.3 1.3 %collective-permute-start.16 = (bf16[576,128]{1,0:T(8,128)(2,1)S(1)}, bf16[576,128]{1,0:T(8,128)(2,1)S(1)}, u32[]{:S(2)}, u32[]{:S(2)}) collective-permute-start(bf16[576,128]{1,0:T(8,128)(2,1)S(1)} %get-tuple-element.65), channel_id=1, source_target_pairs={{0,192},{1,65},{2,194},{3,67},{8,200},{9,73},{10,202},{11,75},{16,... | collective-permute-start | bytes 442376 | tf_op jit(solution)/shard_map/ppermute | solution.py:446
  57.8 1.4 %collective-permute-start.21 = (bf16[512,128]{1,0:T(8,128)(2,1)S(1)}, bf16[512,128]{1,0:T(8,128)(2,1)S(1)}, u32[]{:S(2)}, u32[]{:S(2)}) collective-permute-start(bf16[512,128]{1,0:T(8,128)(2,1)S(1)} %get-tuple-element.74), channel_id=1, source_target_pairs={{0,2},{1,3},{2,0},{3,1},{4,6},{5,7},{6,4},{7,5},{8,10},{9,11},{10,... | collective-permute-start | bytes 393224 | tf_op jit(solution)/shard_map/ppermute | solution.py:437
  59.2 4.1 %collective-permute-done.15.r2_ref = bf16[576,128]{1,0:T(8,128)(2,1)S(1)} collective-permute-done((bf16[576,128]{1,0:T(8,128)(2,1)S(1)}, bf16[576,128]{1,0:T(8,128)(2,1)S(1)}, u32[]{:S(2)}, u32[]{:S(2)}) %collective-permute-start.15) | collective-permute-done | bytes 147488 | tf_op jit(solution)/shard_map/ppermute | solution.py:446
  63.4 1.4 %collective-permute-start.17 = (bf16[144,128]{1,0:T(8,128)(2,1)S(1)}, bf16[144,128]{1,0:T(8,128)(2,1)S(1)}, u32[]{:S(2)}, u32[]{:S(2)}) collective-permute-start(bf16[144,128]{1,0:T(8,128)(2,1)S(1)} %get-tuple-element.67), channel_id=1, source_target_pairs={{0,16},{8,24},{16,32},{24,40},{32,48},{40,56},{48,0},{56,8},{64,80... | collective-permute-start | bytes 110600 | tf_op jit(solution)/shard_map/ppermute | solution.py:452
  64.8 4.7 %collective-permute-start.18 = (bf16[144,128]{1,0:T(8,128)(2,1)S(1)}, bf16[144,128]{1,0:T(8,128)(2,1)S(1)}, u32[]{:S(2)}, u32[]{:S(2)}) collective-permute-start(bf16[144,128]{1,0:T(8,128)(2,1)S(1)} %get-tuple-element.68), channel_id=1, source_target_pairs={{0,32},{8,40},{16,48},{24,56},{32,0},{40,8},{48,16},{56,24},{64,96... | collective-permute-start | bytes 110600 | tf_op jit(solution)/shard_map/ppermute | solution.py:452
  69.5 1.4 %collective-permute-start.19 = (bf16[144,128]{1,0:T(8,128)(2,1)S(1)}, bf16[144,128]{1,0:T(8,128)(2,1)S(1)}, u32[]{:S(2)}, u32[]{:S(2)}) collective-permute-start(bf16[144,128]{1,0:T(8,128)(2,1)S(1)} %get-tuple-element.69), channel_id=1, source_target_pairs={{0,48},{8,56},{16,0},{24,8},{32,16},{40,24},{48,32},{56,40},{64,11... | collective-permute-start | bytes 110600 | tf_op jit(solution)/shard_map/ppermute | solution.py:452
  70.9 1.8 %collective-permute-done.18.refs_2_ = bf16[144,128]{1,0:T(8,128)(2,1)S(1)} collective-permute-done((bf16[144,128]{1,0:T(8,128)(2,1)S(1)}, bf16[144,128]{1,0:T(8,128)(2,1)S(1)}, u32[]{:S(2)}, u32[]{:S(2)}) %collective-permute-start.18) | collective-permute-done | bytes 36896 | tf_op jit(solution)/shard_map/ppermute | solution.py:452
  72.8 1.6 %collective-permute-done.19.refs_3_ = bf16[144,128]{1,0:T(8,128)(2,1)S(1)} collective-permute-done((bf16[144,128]{1,0:T(8,128)(2,1)S(1)}, bf16[144,128]{1,0:T(8,128)(2,1)S(1)}, u32[]{:S(2)}, u32[]{:S(2)}) %collective-permute-start.19) | collective-permute-done | bytes 36896 | tf_op jit(solution)/shard_map/ppermute | solution.py:452
  (32 shorter events, 2.9 us)
Async XLA Ops:
  0.6 8.3 %copy-start.1 = (bf16[2,128,256]{2,1,0:T(8,128)(2,1)S(1)}, bf16[2,128,256]{2,1,0:T(8,128)(2,1)}, u32[]{:S(2)}) copy-start(bf16[2,128,256]{2,1,0:T(8,128)(2,1)} %refs_0_.1) | copy-start | bytes 393220
  0.6 5.5 %collective-permute-start.1 = (bf16[2,128,256]{2,1,0:T(8,128)(2,1)}, bf16[2,128,256]{2,1,0:T(8,128)(2,1)S(1)}, u32[]{:S(2)}, u32[]{:S(2)}) collective-permute-start(bf16[2,128,256]{2,1,0:T(8,128)(2,1)} %refs_0_.1), channel_id=1, source_target_pairs={{0,6},{1,7},{2,4},{3,5},{4,2},{5,3},{6,0},{7,1},{8,14},{9,15},{10,... | collective-permute-start | bytes 393224 | tf_op jit(solution)/shard_map/ppermute | solution.py:437
  1.3 7.6 %collective-permute-start = (bf16[2,128,256]{2,1,0:T(8,128)(2,1)}, bf16[2,128,256]{2,1,0:T(8,128)(2,1)S(1)}, u32[]{:S(2)}, u32[]{:S(2)}) collective-permute-start(bf16[2,128,256]{2,1,0:T(8,128)(2,1)} %refs_0_.1), channel_id=1, source_target_pairs={{0,1},{1,0},{2,3},{3,2},{4,5},{5,4},{6,7},{7,6},{8,9},{9,8},{10,11... | collective-permute-start | bytes 393224 | tf_op jit(solution)/shard_map/ppermute | solution.py:437
  6.2 2.7 %collective-permute-start.2 = (bf16[2,128,256]{2,1,0:T(8,128)(2,1)S(1)}, bf16[2,128,256]{2,1,0:T(8,128)(2,1)S(1)}, u32[]{:S(2)}, u32[]{:S(2)}) collective-permute-start(bf16[2,128,256]{2,1,0:T(8,128)(2,1)S(1)} %collective-permute-done.1.refs_2_), channel_id=1, source_target_pairs={{0,1},{1,0},{2,3},{3,2},{4,5},{5,4},{6,7},{7,6},{8,9},{9,8},{10,11... | collective-permute-start | bytes 393224 | tf_op jit(solution)/shard_map/ppermute | solution.py:437
  10.0 6.8 %collective-permute-start.3 = (bf16[528,128]{1,0:T(8,128)(2,1)S(1)}, bf16[528,128]{1,0:T(8,128)(2,1)S(1)}, u32[]{:S(2)}, u32[]{:S(2)}) collective-permute-start(bf16[528,128]{1,0:T(8,128)(2,1)S(1)} %get-tuple-element.44), channel_id=1, source_target_pairs={{0,4},{1,5},{2,6},{3,7},{4,0},{5,1},{6,2},{7,3},{8,12},{9,13},{10,... | collective-permute-start | bytes 405512 | tf_op jit(solution)/shard_map/ppermute | solution.py:437
  12.5 5.7 %collective-permute-start.5 = (bf16[528,128]{1,0:T(8,128)(2,1)S(1)}, bf16[528,128]{1,0:T(8,128)(2,1)S(1)}, u32[]{:S(2)}, u32[]{:S(2)}) collective-permute-start(bf16[528,128]{1,0:T(8,128)(2,1)S(1)} %get-tuple-element.44), channel_id=1, source_target_pairs={{0,6},{1,7},{2,4},{3,5},{4,2},{5,3},{6,0},{7,1},{8,14},{9,15},{10,... | collective-permute-start | bytes 405512 | tf_op jit(solution)/shard_map/ppermute | solution.py:437
  16.8 1.5 %collective-permute-start.4 = (bf16[528,128]{1,0:T(8,128)(2,1)S(1)}, bf16[528,128]{1,0:T(8,128)(2,1)S(1)}, u32[]{:S(2)}, u32[]{:S(2)}) collective-permute-start(bf16[528,128]{1,0:T(8,128)(2,1)S(1)} %collective-permute-done.3.refs_0_), channel_id=1, source_target_pairs={{0,1},{1,0},{2,3},{3,2},{4,5},{5,4},{6,7},{7,6},{8,9},{9,8},{10,11... | collective-permute-start | bytes 405512 | tf_op jit(solution)/shard_map/ppermute | solution.py:437
  18.2 1.4 %collective-permute-start.6 = (bf16[528,128]{1,0:T(8,128)(2,1)S(1)}, bf16[528,128]{1,0:T(8,128)(2,1)S(1)}, u32[]{:S(2)}, u32[]{:S(2)}) collective-permute-start(bf16[528,128]{1,0:T(8,128)(2,1)S(1)} %collective-permute-done.5.refs_2_), channel_id=1, source_target_pairs={{0,1},{1,0},{2,3},{3,2},{4,5},{5,4},{6,7},{7,6},{8,9},{9,8},{10,11... | collective-permute-start | bytes 405512 | tf_op jit(solution)/shard_map/ppermute | solution.py:437
  21.2 1.2 %collective-permute-start.7 = (f32[8,512]{1,0:T(8,128)S(1)}, f32[8,512]{1,0:T(8,128)S(1)}, u32[]{:S(2)}, u32[]{:S(2)}) collective-permute-start(f32[8,512]{1,0:T(8,128)S(1)} %get-tuple-element.45.own_ref), channel_id=1, source_target_pairs={{0,1},{1,0},{2,3},{3,2},{4,5},{5,4},{6,7},{7,6},{8,9},{9,8},{10,11... | collective-permute-start | bytes 49160 | tf_op jit(solution)/shard_map/ppermute | solution.py:437
  22.4 5.2 %collective-permute-start.8 = (f32[8,512]{1,0:T(8,128)S(1)}, f32[8,512]{1,0:T(8,128)S(1)}, u32[]{:S(2)}, u32[]{:S(2)}) collective-permute-start(f32[8,512]{1,0:T(8,128)S(1)} %shard_map.124.own_ref), channel_id=1, source_target_pairs={{0,2},{1,3},{2,0},{3,1},{4,6},{5,7},{6,4},{7,5},{8,10},{9,11},{10,... | collective-permute-start | bytes 49160 | tf_op jit(solution)/shard_map/ppermute | solution.py:437
  29.4 2.9 %collective-permute-start.9 = (bf16[1024,128]{1,0:T(8,128)(2,1)S(1)}, bf16[1024,128]{1,0:T(8,128)(2,1)S(1)}, u32[]{:S(2)}, u32[]{:S(2)}) collective-permute-start(bf16[1024,128]{1,0:T(8,128)(2,1)S(1)} %get-tuple-element.50), channel_id=1, source_target_pairs={{0,1},{1,0},{2,3},{3,2},{4,5},{5,4},{6,7},{7,6},{8,9},{9,8},{10,11... | collective-permute-start | bytes 786440 | tf_op jit(solution)/shard_map/ppermute | solution.py:437
  30.3 14.7 %collective-permute-start.13 = (bf16[528,512]{1,0:T(8,128)(2,1)S(1)}, bf16[528,512]{1,0:T(8,128)(2,1)S(1)}, u32[]{:S(2)}, u32[]{:S(2)}) collective-permute-start(bf16[528,512]{1,0:T(8,128)(2,1)S(1)} %shard_map.129.xm_ref), channel_id=1, source_target_pairs={{0,8},{1,57},{2,10},{3,59},{8,0},{9,17},{10,2},{11,19},{16,24},{17... | collective-permute-start | bytes 1622024 | tf_op jit(solution)/shard_map/ppermute | solution.py:446
  32.3 6.7 %collective-permute-start.10 = (bf16[544,128]{1,0:T(8,128)(2,1)S(1)}, bf16[544,128]{1,0:T(8,128)(2,1)S(1)}, u32[]{:S(2)}, u32[]{:S(2)}) collective-permute-start(bf16[544,128]{1,0:T(8,128)(2,1)S(1)} %get-tuple-element.52), channel_id=1, source_target_pairs={{0,4},{1,5},{2,6},{3,7},{4,0},{5,1},{6,2},{7,3},{8,12},{9,13},{10,... | collective-permute-start | bytes 417800 | tf_op jit(solution)/shard_map/ppermute | solution.py:437
  34.0 5.0 %collective-permute-start.11 = (bf16[512,128]{1,0:T(8,128)(2,1)S(1)}, bf16[512,128]{1,0:T(8,128)(2,1)S(1)}, u32[]{:S(2)}, u32[]{:S(2)}) collective-permute-start(bf16[512,128]{1,0:T(8,128)(2,1)S(1)} %get-tuple-element.53), channel_id=1, source_target_pairs={{0,6},{1,7},{2,4},{3,5},{4,2},{5,3},{6,0},{7,1},{8,14},{9,15},{10,... | collective-permute-start | bytes 393224 | tf_op jit(solution)/shard_map/ppermute | solution.py:437
  39.0 10.9 %copy-start = (bf16[1,4608,128]{2,1,0:T(8,128)(2,1)S(1)}, bf16[1,4608,128]{2,1,0:T(8,128)(2,1)}, u32[]{:S(2)}) copy-start(bf16[1,4608,128]{2,1,0:T(8,128)(2,1)} %param.13) | copy-start | bytes 3538948
  42.1 15.6 %collective-permute-start.20 = (bf16[1024,128]{1,0:T(8,128)(2,1)S(1)}, bf16[1024,128]{1,0:T(8,128)(2,1)S(1)}, u32[]{:S(2)}, u32[]{:S(2)}) collective-permute-start(bf16[1024,128]{1,0:T(8,128)(2,1)S(1)} %get-tuple-element.72), channel_id=1, source_target_pairs={{0,1},{1,0},{2,3},{3,2},{4,5},{5,4},{6,7},{7,6},{8,9},{9,8},{10,11... | collective-permute-start | bytes 786440 | tf_op jit(solution)/shard_map/ppermute | solution.py:437
  44.9 5.0 %collective-permute-start.12 = (bf16[528,128]{1,0:T(8,128)(2,1)S(1)}, bf16[528,128]{1,0:T(8,128)(2,1)S(1)}, u32[]{:S(2)}, u32[]{:S(2)}) collective-permute-start(bf16[528,128]{1,0:T(8,128)(2,1)S(1)} %get-tuple-element.57.pay_ref), channel_id=1, source_target_pairs={{0,8},{1,57},{2,10},{3,59},{8,0},{9,17},{10,2},{11,19},{16,24},{17... | collective-permute-start | bytes 405512 | tf_op jit(solution)/shard_map/ppermute | solution.py:446
  51.8 7.4 %collective-permute-start.14 = (bf16[576,128]{1,0:T(8,128)(2,1)S(1)}, bf16[576,128]{1,0:T(8,128)(2,1)S(1)}, u32[]{:S(2)}, u32[]{:S(2)}) collective-permute-start(bf16[576,128]{1,0:T(8,128)(2,1)S(1)} %get-tuple-element.63), channel_id=1, source_target_pairs={{0,64},{1,193},{2,66},{3,195},{8,72},{9,201},{10,74},{11,203},{16,... | collective-permute-start | bytes 442376 | tf_op jit(solution)/shard_map/ppermute | solution.py:446
  53.4 9.8 %collective-permute-start.15 = (bf16[576,128]{1,0:T(8,128)(2,1)S(1)}, bf16[576,128]{1,0:T(8,128)(2,1)S(1)}, u32[]{:S(2)}, u32[]{:S(2)}) collective-permute-start(bf16[576,128]{1,0:T(8,128)(2,1)S(1)} %get-tuple-element.64), channel_id=1, source_target_pairs={{0,128},{1,129},{2,130},{3,131},{8,136},{9,137},{10,138},{11,139},... | collective-permute-start | bytes 442376 | tf_op jit(solution)/shard_map/ppermute | solution.py:446
  56.3 6.9 %collective-permute-start.16 = (bf16[576,128]{1,0:T(8,128)(2,1)S(1)}, bf16[576,128]{1,0:T(8,128)(2,1)S(1)}, u32[]{:S(2)}, u32[]{:S(2)}) collective-permute-start(bf16[576,128]{1,0:T(8,128)(2,1)S(1)} %get-tuple-element.65), channel_id=1, source_target_pairs={{0,192},{1,65},{2,194},{3,67},{8,200},{9,73},{10,202},{11,75},{16,... | collective-permute-start | bytes 442376 | tf_op jit(solution)/shard_map/ppermute | solution.py:446
  57.8 17.2 %collective-permute-start.21 = (bf16[512,128]{1,0:T(8,128)(2,1)S(1)}, bf16[512,128]{1,0:T(8,128)(2,1)S(1)}, u32[]{:S(2)}, u32[]{:S(2)}) collective-permute-start(bf16[512,128]{1,0:T(8,128)(2,1)S(1)} %get-tuple-element.74), channel_id=1, source_target_pairs={{0,2},{1,3},{2,0},{3,1},{4,6},{5,7},{6,4},{7,5},{8,10},{9,11},{10,... | collective-permute-start | bytes 393224 | tf_op jit(solution)/shard_map/ppermute | solution.py:437
  63.4 7.6 %collective-permute-start.17 = (bf16[144,128]{1,0:T(8,128)(2,1)S(1)}, bf16[144,128]{1,0:T(8,128)(2,1)S(1)}, u32[]{:S(2)}, u32[]{:S(2)}) collective-permute-start(bf16[144,128]{1,0:T(8,128)(2,1)S(1)} %get-tuple-element.67), channel_id=1, source_target_pairs={{0,16},{8,24},{16,32},{24,40},{32,48},{40,56},{48,0},{56,8},{64,80... | collective-permute-start | bytes 110600 | tf_op jit(solution)/shard_map/ppermute | solution.py:452
  64.8 8.0 %collective-permute-start.18 = (bf16[144,128]{1,0:T(8,128)(2,1)S(1)}, bf16[144,128]{1,0:T(8,128)(2,1)S(1)}, u32[]{:S(2)}, u32[]{:S(2)}) collective-permute-start(bf16[144,128]{1,0:T(8,128)(2,1)S(1)} %get-tuple-element.68), channel_id=1, source_target_pairs={{0,32},{8,40},{16,48},{24,56},{32,0},{40,8},{48,16},{56,24},{64,96... | collective-permute-start | bytes 110600 | tf_op jit(solution)/shard_map/ppermute | solution.py:452
  69.5 4.9 %collective-permute-start.19 = (bf16[144,128]{1,0:T(8,128)(2,1)S(1)}, bf16[144,128]{1,0:T(8,128)(2,1)S(1)}, u32[]{:S(2)}, u32[]{:S(2)}) collective-permute-start(bf16[144,128]{1,0:T(8,128)(2,1)S(1)} %get-tuple-element.69), channel_id=1, source_target_pairs={{0,48},{8,56},{16,0},{24,8},{32,16},{40,24},{48,32},{56,40},{64,11... | collective-permute-start | bytes 110600 | tf_op jit(solution)/shard_map/ppermute | solution.py:452

commit v4 on v3

--- a/solution.py
+++ b/solution.py
@@ -99,20 +99,31 @@
         disc_ref[n] = jnp.broadcast_to(row, (own, row.shape[1])).T
 
 
-def conv_kernel(second, *refs):
-    x_refs = refs[:4]
-    stys_ref, wslot_ref, demod_ref, nb_ref, rgb_ref = refs[4:9]
-    pay_ref, slope_ref, z_ref, xm_ref = refs[9:13]
+def modulated_products(second, slots, x_refs, stys_ref, wslot_ref, xm_ref):
+    count = stys_ref.shape[0]
+    own = stys_ref.shape[1] // 4
+    for n, d in enumerate(slots):
+        for b in range(count):
+            sty = stys_ref[b : b + 1, d * own : (d + 1) * own]
+            x = x_refs[n][b * PIX : (b + 1) * PIX, :] if second else x_refs[n][b].T
+            x = x.astype(f32)
+            xm_ref[b * PIX : (b + 1) * PIX, n * own : (n + 1) * own] = (x * sty).astype(bf16)
+    w = jnp.concatenate([wslot_ref[d * own : (d + 1) * own, :] for d in slots], axis=0)
+    return jnp.dot(xm_ref[...], w, preferred_element_type=f32)
+
+
+def half_conv_kernel(second, slots, xa_ref, xb_ref, stys_ref, wslot_ref, xm_ref, part_ref):
+    part_ref[...] = modulated_products(second, slots, (xa_ref, xb_ref), stys_ref, wslot_ref, xm_ref)
+
+
+def conv_kernel(second, slots, *refs):
+    x_refs = refs[:2]
+    stys_ref, wslot_ref, demod_ref, nb_ref, rgb_ref, part_ref = refs[2:8]
+    pay_ref, slope_ref, z_ref, xm_ref = refs[8:12]
     count = stys_ref.shape[0]
     own = demod_ref.shape[1]
     pixels = count * PIX
-    for d in range(4):
-        for b in range(count):
-            sty = stys_ref[b : b + 1, d * own : (d + 1) * own]
-            x = x_refs[d][b * PIX : (b + 1) * PIX, :] if second else x_refs[d][b].T
-            x = x.astype(f32)
-            xm_ref[b * PIX : (b + 1) * PIX, d * own : (d + 1) * own] = (x * sty).astype(bf16)
-    products = jnp.dot(xm_ref[...], wslot_ref[...], preferred_element_type=f32)
+    products = part_ref[...] + modulated_products(second, slots, x_refs, stys_ref, wslot_ref, xm_ref)
     z = None
     for kx in range(3):
         total = None
@@ -134,7 +145,7 @@
     pay_ref[:pixels, :] = y
     pay_ref[pixels:, :] = rgb
     if second:
-        refs[13][...] = lax.dot_general(rgb, y, NT, preferred_element_type=f32)[:8]
+        refs[12][...] = lax.dot_general(rgb, y, NT, preferred_element_type=f32)[:8]
 
 
 def image_pair_kernel(own_ref, got_ref, out_ref):
@@ -300,24 +311,26 @@
     far_ref[...] = (keep_ref[rows:] + got_ref[rows:].astype(f32)).astype(bf16)
 
 
-def turn_kernel(idx, xa_ref, xb_ref, sty_ref, out_ref):
+def turn_kernel(idx, a01_ref, a23_ref, b02_ref, b13_ref, sty_ref, out_ref):
     chan = idx[1]
-    full = xa_ref.shape[1]
+    full = sty_ref.shape[1]
     count = sty_ref.shape[0]
     own = full // 4
 
-    def turn(ref):
-        for d in range(4):
+    def turn(ref, slots):
+        for n, d in enumerate(slots):
             start = pl.multiple_of((chan ^ d) * own, own)
-            out_ref[pl.ds(start, own), :] = ref[:, d * own : (d + 1) * own].T
+            out_ref[pl.ds(start, own), :] = ref[:, n * own : (n + 1) * own].T
 
     @pl.when(idx[0] == 0)
     def _():
-        turn(xa_ref)
+        turn(a01_ref, (0, 1))
+        turn(a23_ref, (2, 3))
 
     @pl.when(idx[0] != 0)
     def _():
-        turn(xb_ref)
+        turn(b02_ref, (0, 2))
+        turn(b13_ref, (1, 3))
 
     sty = sty_ref[...]
     hi = sty.astype(bf16).astype(f32)
@@ -483,30 +496,42 @@
         scalars=1,
         raws=len(sources),
     )
+    half_outs = [((pixels, full // 2), bf16), ((pixels, TAPS * own), f32)]
     conv_outs = [
         ((pixels + EXTRA, own), bf16),
         ((pixels, own), f32),
         ((pixels, own), f32),
-        ((pixels, full), bf16),
+        half_outs[0],
     ]
-    pay, slope_a, z_a, xm_a = call(
-        functools.partial(conv_kernel, False),
+    xm_a01, part_a = call(
+        functools.partial(half_conv_kernel, False, (0, 1)), half_outs, [base, x1, stys, wslot]
+    )
+    pay, slope_a, z_a, xm_a23 = call(
+        functools.partial(conv_kernel, False, (2, 3)),
         conv_outs,
-        [base, x1, x2, x3, stys, wslot, demod, nb, rgbp],
+        [x2, x3, stys, wslot, demod, nb, rgbp, part_a],
     )
     y0 = flip(pay, 0)
     y2 = flip(pay, 2)
     y1 = within(y0, 1)
     y3 = within(y2, 1)
-    _, slope_b, z_b, xm_b, image_own = call(
-        functools.partial(conv_kernel, True),
+    xm_b02, part_b = call(
+        functools.partial(half_conv_kernel, True, (0, 2)), half_outs, [y0, y2, stys, wslot]
+    )
+    _, slope_b, z_b, xm_b13, image_own = call(
+        functools.partial(conv_kernel, True, (1, 3)),
         conv_outs + [((8, pixels), f32)],
-        [y0, y1, y2, y3, stys, wslot, demod, nb, rgbp],
+        [y1, y3, stys, wslot, demod, nb, rgbp, part_b],
     )
     image_got = within(image_own, 1)
     (image_chip,) = call(image_pair_kernel, [((8, pixels), f32)], [image_own, image_got])
     image_other = within(image_chip, 2)
-    (xm,) = call(turn_kernel, [((full + EXTRA, pixels), bf16)], [idx, xm_a, xm_b, sty], scalars=1)
+    (xm,) = call(
+        turn_kernel,
+        [((full + EXTRA, pixels), bf16)],
+        [idx, xm_a01, xm_a23, xm_b02, xm_b13, sty],
+        scalars=1,
+    )
     (image_first,) = call(first_image_kernel, [((8, pixels), f32)], [y0, y1, y2, y3])
 
     def to_partner(value):

time: 76.1 us -> 77.2 us (1.014)
  waiting for transfers between devices: 31.8 us -> 29.4 us
  starting transfers between devices: 28.5 us -> 30.5 us
  local copies, waits for them, and re-layouts: 0.01 us -> 0.91 us
    ppermute x14, starting transfers between devices: 13 us -> 16.4 us  [across(): return lax.ppermute(value, ('segment', 'chan'), links)]
    ppermute x14, waiting for transfers between devices: 19.3 us -> 17.7 us  [across(): return lax.ppermute(value, ('segment', 'chan'), links)]
    ppermute x5, starting transfers between devices: 7.92 us -> 6.47 us  [by_core(): return lax.ppermute(value, ('dp', 'chan'), links)]
    unnamed x4, local copies, waits for them, and re-layouts: 0.01 us -> 0.91 us
    ppermute x5, waiting for transfers between devices: 9.07 us -> 8.27 us  [by_core(): return lax.ppermute(value, ('dp', 'chan'), links)]
    pallas_call x15 -> x17, Pallas kernels: 14.6 us -> 15 us  [call(): pl.pallas_call(kernel, out_shape=[jax.ShapeDtypeStruct(*o[:2]) if len(o)...]
  transfers between devices with their start and end apart: 22 -> 22, of which waited for: 11 -> 12; matrix products, arithmetic and copies ran while one was open for 0% -> 0% of each run, Pallas kernels for 12% -> 13%
where the time goes in v4:
time: 77.2 us; the launch traced here: 76.5 us
  starting transfers between devices  30.5 us (40%)
  waiting for transfers between devices  29.4 us (38%)
  Pallas kernels  15 us (19%)
  local copies, waits for them, and re-layouts  0.91 us (1%)
    ppermute x14, waiting for transfers between devices, across(): return lax.ppermute(value, ('segment', 'chan'), links)  17.7 us
    ppermute x14, starting transfers between devices, across(): return lax.ppermute(value, ('segment', 'chan'), links)  16.4 us
    pallas_call x17, Pallas kernels, call(): pl.pallas_call(kernel, out_shape=[jax.ShapeDtypeStruct(*o[:2]) if len(o)...  15 us
    ppermute x5, waiting for transfers between devices, by_core(): return lax.ppermute(value, ('dp', 'chan'), links)  8.27 us
    ppermute x3, starting transfers between devices, over_z(): lax.ppermute(value, 'dp', [(y * 8 + z, y * 8 + (z + d) % 8) for y in rang...  7.59 us
    ppermute x5, starting transfers between devices, by_core(): return lax.ppermute(value, ('dp', 'chan'), links)  6.47 us
    ppermute x3, waiting for transfers between devices, over_z(): lax.ppermute(value, 'dp', [(y * 8 + z, y * 8 + (z + d) % 8) for y in rang...  3.39 us
  transfers between devices with their start and end apart: 22, of which 12 were waited for; matrix products, arithmetic and copies ran while one was open for 0% of the time, Pallas kernels for 13%

profile of v4, /device:TPU:4, one launch (start us, length us, event | category | flops | bytes accessed | tf_op | source)
XLA Modules:
  0.0 76.5 jit_solution(1849907042613801457)
XLA Ops:
  1.3 4.9 %collective-permute-done.refs_0_ = bf16[2,128,256]{2,1,0:T(8,128)(2,1)S(1)} collective-permute-done((bf16[2,128,256]{2,1,0:T(8,128)(2,1)}, bf16[2,128,256]{2,1,0:T(8,128)(2,1)S(1)}, u32[]{:S(2)}, u32[]{:S(2)}) %collective-permute-start) | collective-permute-done | bytes 131104 | tf_op jit(solution)/shard_map/ppermute | solution.py:450
  6.2 2.6 %shard_map.121 = (bf16[512,1152]{1,0:T(8,128)(2,1)S(1)}, f32[2,512]{1,0:T(2,128)S(1)}, f32[2,128]{1,0:T(2,128)S(1)}, f32[512,128]{1,0:T(8,128)S(1)}, f32[5,256,1...) custom-call(s32[4]{0:T(128)S(1)} %pad_add_fusion.idx, bf16[4608,128]{1,0:T(8,128)(2,1)} %bitcast.12, ...), custom_call_target="tpu_custom_call" | custom-call | tf_op jit(solution)/shard_map/pallas_call | solution.py:423
  8.9 0.9 %copy-done.1 = bf16[2,128,256]{2,1,0:T(8,128)(2,1)S(1)} copy-done((bf16[2,128,256]{2,1,0:T(8,128)(2,1)S(1)}, bf16[2,128,256]{2,1,0:T(8,128)(2,1)}, u32[]{:S(2)}) %copy-start.1) | copy-done | bytes 131096
  10.3 0.8 %shard_map.123 = (bf16[528,128]{1,0:T(8,128)(2,1)S(1)}, f32[512,128]{1,0:T(8,128)S(1)}, f32[512,128]{1,0:T(8,128)S(1)}, bf16[512,256]{1,0:T(8,128)(2,1)S(1)}) custom-call(bf16[2,128,256]{2,1,0:T(8,128)(2,1)S(1)} %collective-permute-done.refs_0_, bf16[2,128,256]{2,1,0:T(8,128)(2,1)S(1)} %collective-permute-done.1.refs_1_, ...), custom_call_target="tpu_custom_call" | custom-call | tf_op jit(solution)/shard_map/pallas_call | solution.py:423
  11.7 3.8 %collective-permute-start.3 = (bf16[528,128]{1,0:T(8,128)(2,1)S(1)}, bf16[528,128]{1,0:T(8,128)(2,1)S(1)}, u32[]{:S(2)}, u32[]{:S(2)}) collective-permute-start(bf16[528,128]{1,0:T(8,128)(2,1)S(1)} %get-tuple-element.49), channel_id=1, source_target_pairs={{0,4},{1,5},{2,6},{3,7},{4,0},{5,1},{6,2},{7,3},{8,12},{9,13},{10,... | collective-permute-start | bytes 405512 | tf_op jit(solution)/shard_map/ppermute | solution.py:450
  15.5 1.7 %collective-permute-done.5.xb_ref.refs_2_ = bf16[528,128]{1,0:T(8,128)(2,1)S(1)} collective-permute-done((bf16[528,128]{1,0:T(8,128)(2,1)S(1)}, bf16[528,128]{1,0:T(8,128)(2,1)S(1)}, u32[]{:S(2)}, u32[]{:S(2)}) %collective-permute-start.5) | collective-permute-done | bytes 135200 | tf_op jit(solution)/shard_map/ppermute | solution.py:450
  17.2 2.3 %collective-permute-done.3.xa_ref.refs_0_ = bf16[528,128]{1,0:T(8,128)(2,1)S(1)} collective-permute-done((bf16[528,128]{1,0:T(8,128)(2,1)S(1)}, bf16[528,128]{1,0:T(8,128)(2,1)S(1)}, u32[]{:S(2)}, u32[]{:S(2)}) %collective-permute-start.3) | collective-permute-done | bytes 135200 | tf_op jit(solution)/shard_map/ppermute | solution.py:450
  20.0 0.8 %collective-permute-done.4.refs_0_.refs_1_ = bf16[528,128]{1,0:T(8,128)(2,1)S(1)} collective-permute-done((bf16[528,128]{1,0:T(8,128)(2,1)S(1)}, bf16[528,128]{1,0:T(8,128)(2,1)S(1)}, u32[]{:S(2)}, u32[]{:S(2)}) %collective-permute-start.4) | collective-permute-done | bytes 135200 | tf_op jit(solution)/shard_map/ppermute | solution.py:450
  20.9 1.4 %shard_map.125 = (bf16[528,128]{1,0:T(8,128)(2,1)}, f32[512,128]{1,0:T(8,128)S(1)}, f32[512,128]{1,0:T(8,128)S(1)}, bf16[512,256]{1,0:T(8,128)(2,1)S(1)}, f32[8,512]{1,0:T(8,128)S(1)}) custom-call(bf16[528,128]{1,0:T(8,128)(2,1)S(1)} %collective-permute-done.4.refs_0_.refs_1_, bf16[528,128]{1,0:T(8,128)(2,1)S(1)} %collective-permute-done.6.refs_1_.refs_3_, ...), custom_call_target="tpu_custom_call" | custom-call | tf_op jit(solution)/shard_map/pallas_call | solution.py:423
  22.4 1.0 %collective-permute-done.7.got_ref = f32[8,512]{1,0:T(8,128)S(1)} collective-permute-done((f32[8,512]{1,0:T(8,128)S(1)}, f32[8,512]{1,0:T(8,128)S(1)}, u32[]{:S(2)}, u32[]{:S(2)}) %collective-permute-start.7) | collective-permute-done | bytes 16416 | tf_op jit(solution)/shard_map/ppermute | solution.py:450
  23.5 2.3 %collective-permute-start.8 = (f32[8,512]{1,0:T(8,128)S(1)}, f32[8,512]{1,0:T(8,128)S(1)}, u32[]{:S(2)}, u32[]{:S(2)}) collective-permute-start(f32[8,512]{1,0:T(8,128)S(1)} %shard_map.126.own_ref), channel_id=1, source_target_pairs={{0,2},{1,3},{2,0},{3,1},{4,6},{5,7},{6,4},{7,5},{8,10},{9,11},{10,... | collective-permute-start | bytes 49160 | tf_op jit(solution)/shard_map/ppermute | solution.py:450
  25.9 2.8 %collective-permute-done.8.other_ref = f32[8,512]{1,0:T(8,128)S(1)} collective-permute-done((f32[8,512]{1,0:T(8,128)S(1)}, f32[8,512]{1,0:T(8,128)S(1)}, u32[]{:S(2)}, u32[]{:S(2)}) %collective-permute-start.8) | collective-permute-done | bytes 16416 | tf_op jit(solution)/shard_map/ppermute | solution.py:450
  28.7 1.7 %shard_map.128 = (bf16[32,128]{1,0:T(8,128)(2,1)S(1)}, bf16[528,128]{1,0:T(8,128)(2,1)S(1)}, f32[1024,128]{1,0:T(8,128)S(1)}, bf16[1024,128]{1,0:T(8,128)(2,1)S(1)}) custom-call(f32[8,512]{1,0:T(8,128)S(1)} %shard_map.126.own_ref, f32[8,512]{1,0:T(8,128)S(1)} %collective-permute-done.8.other_ref, f32[8,512]{1,0:T(8,128)S(1)} %shard_map.127.first_ref, ...), custom_call_target="tpu_custom_call" | custom-call | tf_op jit(solution)/shard_map/pallas_call | solution.py:423
  30.5 0.8 shard_map.131.xm_ref
  32.1 2.9 %collective-permute-start.10 = (bf16[544,128]{1,0:T(8,128)(2,1)S(1)}, bf16[544,128]{1,0:T(8,128)(2,1)S(1)}, u32[]{:S(2)}, u32[]{:S(2)}) collective-permute-start(bf16[544,128]{1,0:T(8,128)(2,1)S(1)} %get-tuple-element.58), channel_id=1, source_target_pairs={{0,4},{1,5},{2,6},{3,7},{4,0},{5,1},{6,2},{7,3},{8,12},{9,13},{10,... | collective-permute-start | bytes 417800 | tf_op jit(solution)/shard_map/ppermute | solution.py:450
  35.0 0.9 %collective-permute-start.11 = (bf16[512,128]{1,0:T(8,128)(2,1)S(1)}, bf16[512,128]{1,0:T(8,128)(2,1)S(1)}, u32[]{:S(2)}, u32[]{:S(2)}) collective-permute-start(bf16[512,128]{1,0:T(8,128)(2,1)S(1)} %get-tuple-element.59), channel_id=1, source_target_pairs={{0,6},{1,7},{2,4},{3,5},{4,2},{5,3},{6,0},{7,1},{8,14},{9,15},{10,... | collective-permute-start | bytes 393224 | tf_op jit(solution)/shard_map/ppermute | solution.py:450
  35.9 4.0 %collective-permute-done.11.s1_ref = bf16[512,128]{1,0:T(8,128)(2,1)S(1)} collective-permute-done((bf16[512,128]{1,0:T(8,128)(2,1)S(1)}, bf16[512,128]{1,0:T(8,128)(2,1)S(1)}, u32[]{:S(2)}, u32[]{:S(2)}) %collective-permute-start.11) | collective-permute-done | bytes 131104 | tf_op jit(solution)/shard_map/ppermute | solution.py:450
  39.9 1.4 %shard_map.130 = (bf16[528,128]{1,0:T(8,128)(2,1)S(1)}, f32[2]{0:T(128)}) custom-call(s32[4]{0:T(128)S(1)} %pad_add_fusion.idx, bf16[544,128]{1,0:T(8,128)(2,1)S(1)} %collective-permute-done.10.s0_ref, bf16[512,128]{1,0:T(8,128)(2,1)S(1)} %collective-permute-done.11.s1_ref, bf16[16,128]{1,0:T(8,128)(2,1)S(1)} %get-tuple-element.47.refs_6_.rgb_ref, ...), custom_call_target="tpu_custom_call" | custom-call | tf_op jit(solution)/shard_map/pallas_call | solution.py:423
  41.3 1.6 %shard_map.132 = (f32[1024,128]{1,0:T(8,128)S(1)}, bf16[1024,128]{1,0:T(8,128)(2,1)S(1)}, f32[512,1152]{1,0:T(8,128)S(1)}) custom-call(bf16[528,128]{1,0:T(8,128)(2,1)S(1)} %get-tuple-element.63.pay_ref, bf16[512,1152]{1,0:T(8,128)(2,1)S(1)} %get-tuple-element.44.wslot_ref.refs_3_, f32[2,512]{1,0:T(2,128)S(1)} %get-tuple-element.43.stys_ref.refs_2_, ...), custom_call_target="tpu_custom_call" | custom-call | tf_op jit(solution)/shard_map/pallas_call | solution.py:423
  42.9 2.8 %collective-permute-start.20 = (bf16[1024,128]{1,0:T(8,128)(2,1)S(1)}, bf16[1024,128]{1,0:T(8,128)(2,1)S(1)}, u32[]{:S(2)}, u32[]{:S(2)}) collective-permute-start(bf16[1024,128]{1,0:T(8,128)(2,1)S(1)} %get-tuple-element.80), channel_id=1, source_target_pairs={{0,1},{1,0},{2,3},{3,2},{4,5},{5,4},{6,7},{7,6},{8,9},{9,8},{10,11... | collective-permute-start | bytes 786440 | tf_op jit(solution)/shard_map/ppermute | solution.py:450
  45.7 5.0 %collective-permute-done.12.other_pay_ref = bf16[528,128]{1,0:T(8,128)(2,1)S(1)} collective-permute-done((bf16[528,128]{1,0:T(8,128)(2,1)S(1)}, bf16[528,128]{1,0:T(8,128)(2,1)S(1)}, u32[]{:S(2)}, u32[]{:S(2)}) %collective-permute-start.12) | collective-permute-done | bytes 135200 | tf_op jit(solution)/shard_map/ppermute | solution.py:459
  50.7 1.8 %shard_map.133 = (f32[576,128]{1,0:T(8,128)S(1)}, bf16[576,128]{1,0:T(8,128)(2,1)S(1)}, bf16[576,128]{1,0:T(8,128)(2,1)S(1)}, bf16[576,128]{1,0:T(8,128)(2,1)S(1)}) custom-call(s32[4]{0:T(128)S(1)} %pad_add_fusion.idx, bf16[528,128]{1,0:T(8,128)(2,1)S(1)} %get-tuple-element.63.pay_ref, bf16[528,128]{1,0:T(8,128)(2,1)S(1)} %collective-permute-done.12.other_pay_ref, ...), custom_call_target="tpu_custom_call" | custom-call | tf_op jit(solution)/shard_map/pallas_call | solution.py:423
  52.6 1.7 %collective-permute-start.14 = (bf16[576,128]{1,0:T(8,128)(2,1)S(1)}, bf16[576,128]{1,0:T(8,128)(2,1)S(1)}, u32[]{:S(2)}, u32[]{:S(2)}) collective-permute-start(bf16[576,128]{1,0:T(8,128)(2,1)S(1)} %get-tuple-element.71), channel_id=1, source_target_pairs={{0,64},{1,193},{2,66},{3,195},{8,72},{9,201},{10,74},{11,203},{16,... | collective-permute-start | bytes 442376 | tf_op jit(solution)/shard_map/ppermute | solution.py:459
  54.2 2.9 %collective-permute-start.15 = (bf16[576,128]{1,0:T(8,128)(2,1)S(1)}, bf16[576,128]{1,0:T(8,128)(2,1)S(1)}, u32[]{:S(2)}, u32[]{:S(2)}) collective-permute-start(bf16[576,128]{1,0:T(8,128)(2,1)S(1)} %get-tuple-element.72), channel_id=1, source_target_pairs={{0,128},{1,129},{2,130},{3,131},{8,136},{9,137},{10,138},{11,139},... | collective-permute-start | bytes 442376 | tf_op jit(solution)/shard_map/ppermute | solution.py:459
  57.1 1.3 %collective-permute-start.16 = (bf16[576,128]{1,0:T(8,128)(2,1)S(1)}, bf16[576,128]{1,0:T(8,128)(2,1)S(1)}, u32[]{:S(2)}, u32[]{:S(2)}) collective-permute-start(bf16[576,128]{1,0:T(8,128)(2,1)S(1)} %get-tuple-element.73), channel_id=1, source_target_pairs={{0,192},{1,65},{2,194},{3,67},{8,200},{9,73},{10,202},{11,75},{16,... | collective-permute-start | bytes 442376 | tf_op jit(solution)/shard_map/ppermute | solution.py:459
  58.5 2.2 %collective-permute-start.21 = (bf16[512,128]{1,0:T(8,128)(2,1)S(1)}, bf16[512,128]{1,0:T(8,128)(2,1)S(1)}, u32[]{:S(2)}, u32[]{:S(2)}) collective-permute-start(bf16[512,128]{1,0:T(8,128)(2,1)S(1)} %get-tuple-element.82), channel_id=1, source_target_pairs={{0,2},{1,3},{2,0},{3,1},{4,6},{5,7},{6,4},{7,5},{8,10},{9,11},{10,... | collective-permute-start | bytes 393224 | tf_op jit(solution)/shard_map/ppermute | solution.py:450
  60.8 3.3 %collective-permute-done.15.r2_ref = bf16[576,128]{1,0:T(8,128)(2,1)S(1)} collective-permute-done((bf16[576,128]{1,0:T(8,128)(2,1)S(1)}, bf16[576,128]{1,0:T(8,128)(2,1)S(1)}, u32[]{:S(2)}, u32[]{:S(2)}) %collective-permute-start.15) | collective-permute-done | bytes 147488 | tf_op jit(solution)/shard_map/ppermute | solution.py:459
  64.1 1.3 %collective-permute-start.17 = (bf16[144,128]{1,0:T(8,128)(2,1)S(1)}, bf16[144,128]{1,0:T(8,128)(2,1)S(1)}, u32[]{:S(2)}, u32[]{:S(2)}) collective-permute-start(bf16[144,128]{1,0:T(8,128)(2,1)S(1)} %get-tuple-element.75), channel_id=1, source_target_pairs={{0,16},{8,24},{16,32},{24,40},{32,48},{40,56},{48,0},{56,8},{64,80... | collective-permute-start | bytes 110600 | tf_op jit(solution)/shard_map/ppermute | solution.py:465
  65.4 4.9 %collective-permute-start.18 = (bf16[144,128]{1,0:T(8,128)(2,1)S(1)}, bf16[144,128]{1,0:T(8,128)(2,1)S(1)}, u32[]{:S(2)}, u32[]{:S(2)}) collective-permute-start(bf16[144,128]{1,0:T(8,128)(2,1)S(1)} %get-tuple-element.76), channel_id=1, source_target_pairs={{0,32},{8,40},{16,48},{24,56},{32,0},{40,8},{48,16},{56,24},{64,96... | collective-permute-start | bytes 110600 | tf_op jit(solution)/shard_map/ppermute | solution.py:465
  70.3 1.5 %collective-permute-start.19 = (bf16[144,128]{1,0:T(8,128)(2,1)S(1)}, bf16[144,128]{1,0:T(8,128)(2,1)S(1)}, u32[]{:S(2)}, u32[]{:S(2)}) collective-permute-start(bf16[144,128]{1,0:T(8,128)(2,1)S(1)} %get-tuple-element.77), channel_id=1, source_target_pairs={{0,48},{8,56},{16,0},{24,8},{32,16},{40,24},{48,32},{56,40},{64,11... | collective-permute-start | bytes 110600 | tf_op jit(solution)/shard_map/ppermute | solution.py:465
  71.7 1.6 %collective-permute-done.18.refs_2_ = bf16[144,128]{1,0:T(8,128)(2,1)S(1)} collective-permute-done((bf16[144,128]{1,0:T(8,128)(2,1)S(1)}, bf16[144,128]{1,0:T(8,128)(2,1)S(1)}, u32[]{:S(2)}, u32[]{:S(2)}) %collective-permute-start.18) | collective-permute-done | bytes 36896 | tf_op jit(solution)/shard_map/ppermute | solution.py:465
  73.3 1.8 %collective-permute-done.19.refs_3_ = bf16[144,128]{1,0:T(8,128)(2,1)S(1)} collective-permute-done((bf16[144,128]{1,0:T(8,128)(2,1)S(1)}, bf16[144,128]{1,0:T(8,128)(2,1)S(1)}, u32[]{:S(2)}, u32[]{:S(2)}) %collective-permute-start.19) | collective-permute-done | bytes 36896 | tf_op jit(solution)/shard_map/ppermute | solution.py:465
  (34 shorter events, 5.3 us)
Async XLA Ops:
  0.6 5.5 %collective-permute-start = (bf16[2,128,256]{2,1,0:T(8,128)(2,1)}, bf16[2,128,256]{2,1,0:T(8,128)(2,1)S(1)}, u32[]{:S(2)}, u32[]{:S(2)}) collective-permute-start(bf16[2,128,256]{2,1,0:T(8,128)(2,1)} %xa_ref.1), channel_id=1, source_target_pairs={{0,6},{1,7},{2,4},{3,5},{4,2},{5,3},{6,0},{7,1},{8,14},{9,15},{10,... | collective-permute-start | bytes 393224 | tf_op jit(solution)/shard_map/ppermute | solution.py:450
  1.3 7.6 %collective-permute-start.2 = (bf16[2,128,256]{2,1,0:T(8,128)(2,1)}, bf16[2,128,256]{2,1,0:T(8,128)(2,1)S(1)}, u32[]{:S(2)}, u32[]{:S(2)}) collective-permute-start(bf16[2,128,256]{2,1,0:T(8,128)(2,1)} %xa_ref.1), channel_id=1, source_target_pairs={{0,1},{1,0},{2,3},{3,2},{4,5},{5,4},{6,7},{7,6},{8,9},{9,8},{10,11... | collective-permute-start | bytes 393224 | tf_op jit(solution)/shard_map/ppermute | solution.py:450
  6.2 4.2 %collective-permute-start.1 = (bf16[2,128,256]{2,1,0:T(8,128)(2,1)S(1)}, bf16[2,128,256]{2,1,0:T(8,128)(2,1)S(1)}, u32[]{:S(2)}, u32[]{:S(2)}) collective-permute-start(bf16[2,128,256]{2,1,0:T(8,128)(2,1)S(1)} %collective-permute-done.refs_0_), channel_id=1, source_target_pairs={{0,1},{1,0},{2,3},{3,2},{4,5},{5,4},{6,7},{7,6},{8,9},{9,8},{10,11... | collective-permute-start | bytes 393224 | tf_op jit(solution)/shard_map/ppermute | solution.py:450
  8.9 0.9 %copy-start.1 = (bf16[2,128,256]{2,1,0:T(8,128)(2,1)S(1)}, bf16[2,128,256]{2,1,0:T(8,128)(2,1)}, u32[]{:S(2)}) copy-start(bf16[2,128,256]{2,1,0:T(8,128)(2,1)} %xa_ref.1) | copy-start | bytes 393220
  11.1 6.1 %collective-permute-start.5 = (bf16[528,128]{1,0:T(8,128)(2,1)S(1)}, bf16[528,128]{1,0:T(8,128)(2,1)S(1)}, u32[]{:S(2)}, u32[]{:S(2)}) collective-permute-start(bf16[528,128]{1,0:T(8,128)(2,1)S(1)} %get-tuple-element.49), channel_id=1, source_target_pairs={{0,6},{1,7},{2,4},{3,5},{4,2},{5,3},{6,0},{7,1},{8,14},{9,15},{10,... | collective-permute-start | bytes 405512 | tf_op jit(solution)/shard_map/ppermute | solution.py:450
  11.7 7.8 %collective-permute-start.3 = (bf16[528,128]{1,0:T(8,128)(2,1)S(1)}, bf16[528,128]{1,0:T(8,128)(2,1)S(1)}, u32[]{:S(2)}, u32[]{:S(2)}) collective-permute-start(bf16[528,128]{1,0:T(8,128)(2,1)S(1)} %get-tuple-element.49), channel_id=1, source_target_pairs={{0,4},{1,5},{2,6},{3,7},{4,0},{5,1},{6,2},{7,3},{8,12},{9,13},{10,... | collective-permute-start | bytes 405512 | tf_op jit(solution)/shard_map/ppermute | solution.py:450
  17.2 2.8 %collective-permute-start.6 = (bf16[528,128]{1,0:T(8,128)(2,1)S(1)}, bf16[528,128]{1,0:T(8,128)(2,1)S(1)}, u32[]{:S(2)}, u32[]{:S(2)}) collective-permute-start(bf16[528,128]{1,0:T(8,128)(2,1)S(1)} %collective-permute-done.5.xb_ref.refs_2_), channel_id=1, source_target_pairs={{0,1},{1,0},{2,3},{3,2},{4,5},{5,4},{6,7},{7,6},{8,9},{9,8},{10,11... | collective-permute-start | bytes 405512 | tf_op jit(solution)/shard_map/ppermute | solution.py:450
  19.5 1.4 %collective-permute-start.4 = (bf16[528,128]{1,0:T(8,128)(2,1)S(1)}, bf16[528,128]{1,0:T(8,128)(2,1)S(1)}, u32[]{:S(2)}, u32[]{:S(2)}) collective-permute-start(bf16[528,128]{1,0:T(8,128)(2,1)S(1)} %collective-permute-done.3.xa_ref.refs_0_), channel_id=1, source_target_pairs={{0,1},{1,0},{2,3},{3,2},{4,5},{5,4},{6,7},{7,6},{8,9},{9,8},{10,11... | collective-permute-start | bytes 405512 | tf_op jit(solution)/shard_map/ppermute | solution.py:450
  22.3 1.2 %collective-permute-start.7 = (f32[8,512]{1,0:T(8,128)S(1)}, f32[8,512]{1,0:T(8,128)S(1)}, u32[]{:S(2)}, u32[]{:S(2)}) collective-permute-start(f32[8,512]{1,0:T(8,128)S(1)} %get-tuple-element.51.own_ref), channel_id=1, source_target_pairs={{0,1},{1,0},{2,3},{3,2},{4,5},{5,4},{6,7},{7,6},{8,9},{9,8},{10,11... | collective-permute-start | bytes 49160 | tf_op jit(solution)/shard_map/ppermute | solution.py:450
  23.5 5.2 %collective-permute-start.8 = (f32[8,512]{1,0:T(8,128)S(1)}, f32[8,512]{1,0:T(8,128)S(1)}, u32[]{:S(2)}, u32[]{:S(2)}) collective-permute-start(f32[8,512]{1,0:T(8,128)S(1)} %shard_map.126.own_ref), channel_id=1, source_target_pairs={{0,2},{1,3},{2,0},{3,1},{4,6},{5,7},{6,4},{7,5},{8,10},{9,11},{10,... | collective-permute-start | bytes 49160 | tf_op jit(solution)/shard_map/ppermute | solution.py:450
  30.4 1.6 %collective-permute-start.9 = (bf16[1024,128]{1,0:T(8,128)(2,1)S(1)}, bf16[1024,128]{1,0:T(8,128)(2,1)S(1)}, u32[]{:S(2)}, u32[]{:S(2)}) collective-permute-start(bf16[1024,128]{1,0:T(8,128)(2,1)S(1)} %get-tuple-element.56), channel_id=1, source_target_pairs={{0,1},{1,0},{2,3},{3,2},{4,5},{5,4},{6,7},{7,6},{8,9},{9,8},{10,11... | collective-permute-start | bytes 786440 | tf_op jit(solution)/shard_map/ppermute | solution.py:450
  30.5 20.2 %copy-start = (bf16[1,4608,128]{2,1,0:T(8,128)(2,1)S(1)}, bf16[1,4608,128]{2,1,0:T(8,128)(2,1)}, u32[]{:S(2)}) copy-start(bf16[1,4608,128]{2,1,0:T(8,128)(2,1)} %param.13) | copy-start | bytes 3538948
  31.3 14.4 %collective-permute-start.13 = (bf16[528,512]{1,0:T(8,128)(2,1)S(1)}, bf16[528,512]{1,0:T(8,128)(2,1)S(1)}, u32[]{:S(2)}, u32[]{:S(2)}) collective-permute-start(bf16[528,512]{1,0:T(8,128)(2,1)S(1)} %shard_map.131.xm_ref), channel_id=1, source_target_pairs={{0,8},{1,57},{2,10},{3,59},{8,0},{9,17},{10,2},{11,19},{16,24},{17... | collective-permute-start | bytes 1622024 | tf_op jit(solution)/shard_map/ppermute | solution.py:459
  32.1 7.8 %collective-permute-start.10 = (bf16[544,128]{1,0:T(8,128)(2,1)S(1)}, bf16[544,128]{1,0:T(8,128)(2,1)S(1)}, u32[]{:S(2)}, u32[]{:S(2)}) collective-permute-start(bf16[544,128]{1,0:T(8,128)(2,1)S(1)} %get-tuple-element.58), channel_id=1, source_target_pairs={{0,4},{1,5},{2,6},{3,7},{4,0},{5,1},{6,2},{7,3},{8,12},{9,13},{10,... | collective-permute-start | bytes 417800 | tf_op jit(solution)/shard_map/ppermute | solution.py:450
  35.0 5.0 %collective-permute-start.11 = (bf16[512,128]{1,0:T(8,128)(2,1)S(1)}, bf16[512,128]{1,0:T(8,128)(2,1)S(1)}, u32[]{:S(2)}, u32[]{:S(2)}) collective-permute-start(bf16[512,128]{1,0:T(8,128)(2,1)S(1)} %get-tuple-element.59), channel_id=1, source_target_pairs={{0,6},{1,7},{2,4},{3,5},{4,2},{5,3},{6,0},{7,1},{8,14},{9,15},{10,... | collective-permute-start | bytes 393224 | tf_op jit(solution)/shard_map/ppermute | solution.py:450
  42.9 15.6 %collective-permute-start.20 = (bf16[1024,128]{1,0:T(8,128)(2,1)S(1)}, bf16[1024,128]{1,0:T(8,128)(2,1)S(1)}, u32[]{:S(2)}, u32[]{:S(2)}) collective-permute-start(bf16[1024,128]{1,0:T(8,128)(2,1)S(1)} %get-tuple-element.80), channel_id=1, source_target_pairs={{0,1},{1,0},{2,3},{3,2},{4,5},{5,4},{6,7},{7,6},{8,9},{9,8},{10,11... | collective-permute-start | bytes 786440 | tf_op jit(solution)/shard_map/ppermute | solution.py:450
  45.7 5.0 %collective-permute-start.12 = (bf16[528,128]{1,0:T(8,128)(2,1)S(1)}, bf16[528,128]{1,0:T(8,128)(2,1)S(1)}, u32[]{:S(2)}, u32[]{:S(2)}) collective-permute-start(bf16[528,128]{1,0:T(8,128)(2,1)S(1)} %get-tuple-element.63.pay_ref), channel_id=1, source_target_pairs={{0,8},{1,57},{2,10},{3,59},{8,0},{9,17},{10,2},{11,19},{16,24},{17... | collective-permute-start | bytes 405512 | tf_op jit(solution)/shard_map/ppermute | solution.py:459
  52.6 8.2 %collective-permute-start.14 = (bf16[576,128]{1,0:T(8,128)(2,1)S(1)}, bf16[576,128]{1,0:T(8,128)(2,1)S(1)}, u32[]{:S(2)}, u32[]{:S(2)}) collective-permute-start(bf16[576,128]{1,0:T(8,128)(2,1)S(1)} %get-tuple-element.71), channel_id=1, source_target_pairs={{0,64},{1,193},{2,66},{3,195},{8,72},{9,201},{10,74},{11,203},{16,... | collective-permute-start | bytes 442376 | tf_op jit(solution)/shard_map/ppermute | solution.py:459
  54.2 9.8 %collective-permute-start.15 = (bf16[576,128]{1,0:T(8,128)(2,1)S(1)}, bf16[576,128]{1,0:T(8,128)(2,1)S(1)}, u32[]{:S(2)}, u32[]{:S(2)}) collective-permute-start(bf16[576,128]{1,0:T(8,128)(2,1)S(1)} %get-tuple-element.72), channel_id=1, source_target_pairs={{0,128},{1,129},{2,130},{3,131},{8,136},{9,137},{10,138},{11,139},... | collective-permute-start | bytes 442376 | tf_op jit(solution)/shard_map/ppermute | solution.py:459
  57.1 6.9 %collective-permute-start.16 = (bf16[576,128]{1,0:T(8,128)(2,1)S(1)}, bf16[576,128]{1,0:T(8,128)(2,1)S(1)}, u32[]{:S(2)}, u32[]{:S(2)}) collective-permute-start(bf16[576,128]{1,0:T(8,128)(2,1)S(1)} %get-tuple-element.73), channel_id=1, source_target_pairs={{0,192},{1,65},{2,194},{3,67},{8,200},{9,73},{10,202},{11,75},{16,... | collective-permute-start | bytes 442376 | tf_op jit(solution)/shard_map/ppermute | solution.py:459
  58.5 17.2 %collective-permute-start.21 = (bf16[512,128]{1,0:T(8,128)(2,1)S(1)}, bf16[512,128]{1,0:T(8,128)(2,1)S(1)}, u32[]{:S(2)}, u32[]{:S(2)}) collective-permute-start(bf16[512,128]{1,0:T(8,128)(2,1)S(1)} %get-tuple-element.82), channel_id=1, source_target_pairs={{0,2},{1,3},{2,0},{3,1},{4,6},{5,7},{6,4},{7,5},{8,10},{9,11},{10,... | collective-permute-start | bytes 393224 | tf_op jit(solution)/shard_map/ppermute | solution.py:450
  64.1 7.6 %collective-permute-start.17 = (bf16[144,128]{1,0:T(8,128)(2,1)S(1)}, bf16[144,128]{1,0:T(8,128)(2,1)S(1)}, u32[]{:S(2)}, u32[]{:S(2)}) collective-permute-start(bf16[144,128]{1,0:T(8,128)(2,1)S(1)} %get-tuple-element.75), channel_id=1, source_target_pairs={{0,16},{8,24},{16,32},{24,40},{32,48},{40,56},{48,0},{56,8},{64,80... | collective-permute-start | bytes 110600 | tf_op jit(solution)/shard_map/ppermute | solution.py:465
  65.4 7.9 %collective-permute-start.18 = (bf16[144,128]{1,0:T(8,128)(2,1)S(1)}, bf16[144,128]{1,0:T(8,128)(2,1)S(1)}, u32[]{:S(2)}, u32[]{:S(2)}) collective-permute-start(bf16[144,128]{1,0:T(8,128)(2,1)S(1)} %get-tuple-element.76), channel_id=1, source_target_pairs={{0,32},{8,40},{16,48},{24,56},{32,0},{40,8},{48,16},{56,24},{64,96... | collective-permute-start | bytes 110600 | tf_op jit(solution)/shard_map/ppermute | solution.py:465
  70.3 4.9 %collective-permute-start.19 = (bf16[144,128]{1,0:T(8,128)(2,1)S(1)}, bf16[144,128]{1,0:T(8,128)(2,1)S(1)}, u32[]{:S(2)}, u32[]{:S(2)}) collective-permute-start(bf16[144,128]{1,0:T(8,128)(2,1)S(1)} %get-tuple-element.77), channel_id=1, source_target_pairs={{0,48},{8,56},{16,0},{24,8},{32,16},{40,24},{48,32},{56,40},{64,11... | collective-permute-start | bytes 110600 | tf_op jit(solution)/shard_map/ppermute | solution.py:465

commit v5 on v4

--- a/solution.py
+++ b/solution.py
@@ -144,8 +144,13 @@
     rgb = rgb_ref[...]
     pay_ref[:pixels, :] = y
     pay_ref[pixels:, :] = rgb
-    if second:
-        refs[12][...] = lax.dot_general(rgb, y, NT, preferred_element_type=f32)[:8]
+
+
+def own_image_kernel(pay_ref, out_ref):
+    pixels = out_ref.shape[1]
+    out_ref[...] = lax.dot_general(
+        pay_ref[pixels:, :], pay_ref[:pixels, :], NT, preferred_element_type=f32
+    )[:8]
 
 
 def image_pair_kernel(own_ref, got_ref, out_ref):
@@ -234,7 +239,7 @@
         logit = logit / PIX
         e = jnp.exp(-jnp.abs(logit))
         under = 1.0 + e
-        g = jnp.where(logit >= 0.0, (1.0 - under) / under, e / under - 1.0)
+        g = jnp.where(logit >= 0.0, 1.0 / under, e / under) - 1.0
         rows = [jnp.concatenate([c[ch] for c in chunks], axis=1) * g for ch in range(3)]
         out_rows.append(jnp.concatenate(rows + [jnp.zeros((5, PIX), f32)], axis=0))
         wide = jnp.broadcast_to(logit, (1, lanes))
@@ -265,23 +270,16 @@
 
 
 def first_grad_kernel(
-    idx, s0_ref, s1_ref, rgb_ref, slope_ref, z_ref, demod_ref, other_ref, tail_ref,
-    pay_ref, logit_ref,
+    idx, s0_ref, s1_ref, rgb_ref, slope_ref, z_ref, demod_ref, other_ref, pay_ref,
 ):
     count = demod_ref.shape[0]
     pixels = count * PIX
     chunks = pixels // 128
 
-    def put_logits(tail):
-        for b in range(count):
-            at = 6 * chunks + 3 * b
-            logit_ref[b] = jnp.max((tail[at : at + 1] + tail[at + 1 : at + 2]) + tail[at + 2 : at + 3])
-
     @pl.when(idx[0] == 0)
     def _():
         dx = (s0_ref[:pixels, :].astype(f32) + s1_ref[...].astype(f32)).astype(bf16)
         tail = s0_ref[pixels:, :].astype(f32)
-        put_logits(tail)
         both = tail[: 3 * chunks] + tail[3 * chunks : 6 * chunks]
         rows = [
             jnp.concatenate(
@@ -295,7 +293,6 @@
 
     @pl.when(idx[0] != 0)
     def _():
-        put_logits(tail_ref[...].astype(f32))
         pay_ref[...] = other_ref[...]
 
 
@@ -303,6 +300,25 @@
     cols = shifted_gz(pay_ref[: stys_ref.shape[0] * PIX, :])
     store_dx(cols, wslot_ref, stys_ref, keep_ref, send_ref)
     acc_ref[...] = jnp.dot(xm_ref[: acc_ref.shape[0], :], cols, preferred_element_type=f32)
+
+
+def logits_kernel(idx, s0_ref, tail_ref, logit_ref):
+    count = logit_ref.shape[0]
+    pixels = count * PIX
+    chunks = pixels // 128
+
+    def put(tail):
+        for b in range(count):
+            at = 6 * chunks + 3 * b
+            logit_ref[b] = jnp.max((tail[at : at + 1] + tail[at + 1 : at + 2]) + tail[at + 2 : at + 3])
+
+    @pl.when(idx[0] == 0)
+    def _():
+        put(s0_ref[pixels:, :].astype(f32))
+
+    @pl.when(idx[0] != 0)
+    def _():
+        put(tail_ref[...].astype(f32))
 
 
 def dx_pair_kernel(keep_ref, got_ref, near_ref, far_ref):
@@ -364,9 +380,17 @@
         sty_rows.append(sty * sty)
         tail = pay[pixels:, :].astype(f32)
         coef_rows.append(tail[:count] + tail[8 : 8 + count])
-    left = pad_rows(jnp.concatenate(sty_rows, axis=0), own).T
-    right = pad_rows(jnp.concatenate(coef_rows, axis=0), own)
-    demod_term = jnp.dot(left, right, precision=lax.Precision.HIGHEST, preferred_element_type=f32)
+    sty = jnp.concatenate(sty_rows, axis=0)
+    coef = jnp.concatenate(coef_rows, axis=0)
+    sty_high = sty.astype(bf16).astype(f32)
+    coef_high = coef.astype(bf16).astype(f32)
+    left = jnp.concatenate([sty_high, sty_high, sty - sty_high, sty - sty_high], axis=0)
+    right = jnp.concatenate([coef_high, coef - coef_high, coef_high, coef - coef_high], axis=0)
+    demod_term = jnp.dot(
+        pad_rows(left, own).T.astype(bf16),
+        pad_rows(right, own).astype(bf16),
+        preferred_element_type=f32,
+    )
     for first in range(0, TAPS, 2):
         taps = range(first, min(first + 2, TAPS))
         lanes = slice(first * own, (taps[-1] + 1) * own)
@@ -376,7 +400,7 @@
         for n, k in enumerate(taps):
             at = slice(k * full, (k + 1) * full)
             w = w_ref[at, :].astype(f32)
-            sum_ref[at, :] = total[:, n * own : (n + 1) * own] + w * demod_term
+            sum_ref[at, :] = (total[:, n * own : (n + 1) * own] + w * demod_term).astype(bf16)
     rows = keep_ref.shape[0] // 4
     step = 1 - 2 * core
     for d, ref in enumerate((keep_ref, send_1_ref, send_2_ref, send_3_ref)):
@@ -384,14 +408,14 @@
         for e in range(4):
             start = (to_y * 8 + ((z + 2 * e) & 7)) * rows
             block = sum_ref[pl.ds(pl.multiple_of(start, RES), rows), :]
-            ref[e * rows : (e + 1) * rows, :] = block.astype(ref.dtype)
+            ref[e * rows : (e + 1) * rows, :] = block
 
 
 def y_sum_kernel(keep_ref, r1_ref, r2_ref, r3_ref, own_ref, *out_refs):
     rows = own_ref.shape[0]
     for e, ref in enumerate((own_ref, *out_refs)):
         at = slice(e * rows, (e + 1) * rows)
-        total = keep_ref[at] + r1_ref[at].astype(f32)
+        total = keep_ref[at].astype(f32) + r1_ref[at].astype(f32)
         total = total + (r2_ref[at].astype(f32) + r3_ref[at].astype(f32))
         ref[...] = total.astype(ref.dtype)
 
@@ -518,11 +542,12 @@
     xm_b02, part_b = call(
         functools.partial(half_conv_kernel, True, (0, 2)), half_outs, [y0, y2, stys, wslot]
     )
-    _, slope_b, z_b, xm_b13, image_own = call(
+    pay_last, slope_b, z_b, xm_b13 = call(
         functools.partial(conv_kernel, True, (1, 3)),
-        conv_outs + [((8, pixels), f32)],
+        conv_outs,
         [y1, y3, stys, wslot, demod, nb, rgbp, part_b],
     )
+    (image_own,) = call(own_image_kernel, [((8, pixels), f32)], [pay_last])
     image_got = within(image_own, 1)
     (image_chip,) = call(image_pair_kernel, [((8, pixels), f32)], [image_own, image_got])
     image_other = within(image_chip, 2)
@@ -550,12 +575,13 @@
         pair_kernel, [((pixels + TAIL, own), bf16), share], [dx_keep, dx_got, tail]
     )
     got = [flip(dx_near, 0), flip(dx_far, 2)]
-    pay_g, logits = call(
+    (pay_g,) = call(
         first_grad_kernel,
-        [((pixels + EXTRA, own), bf16), ((count,), f32, True)],
-        [idx, *got, rgbp, slope_a, z_a, demod, pay_b, tail],
+        [((pixels + EXTRA, own), bf16)],
+        [idx, *got, rgbp, slope_a, z_a, demod, pay_b],
         scalars=1,
     )
+    (logits,) = call(logits_kernel, [((count,), f32, True)], [idx, got[0], tail], scalars=1)
     other_pay = to_partner(pay_g)
     keep, send, before = call(
         share_kernel, [(two, f32), (two, bf16), ((full, TAPS * own), f32)], [pay_g, wslot, stys, xm]
@@ -567,9 +593,9 @@
     four = (4 * rows, own)
     y_keep, *y_send = call(
         weight_kernel,
-        [(four, f32)] + [(four, bf16)] * 3,
+        [(four, bf16)] * 4,
         [idx, pay_g, other_pay, xm, other_xm, weight, before],
-        scratch=[pltpu.VMEM(weight.shape, f32)],
+        scratch=[pltpu.VMEM(weight.shape, bf16)],
         scalars=1,
     )
     y_got = [over_y(y_send[d - 1], d) for d in (1, 2, 3)]

time: 77.2 us -> 76 us (0.984)
  waiting for transfers between devices: 29.4 us -> 28.4 us
    ppermute x3, waiting for transfers between devices: 3.39 us -> 2.21 us  [over_z(): lax.ppermute(value, 'dp', [(y * 8 + z, y * 8 + (z + d) % 8) for y in rang...]
    pallas_call x17 -> x19, Pallas kernels: 15 us -> 15 us  [call(): pl.pallas_call(kernel, out_shape=[jax.ShapeDtypeStruct(*o[:2]) if len(o)...]
  transfers between devices with their start and end apart: 22 -> 22, of which waited for: 12 -> 12; matrix products, arithmetic and copies ran while one was open for 0% -> 0% of each run, Pallas kernels for 13% -> 14%
where the time goes in v5:
time: 76 us; the launch traced here: 75.5 us
  starting transfers between devices  30.3 us (40%)
  waiting for transfers between devices  28.4 us (37%)
  Pallas kernels  15 us (20%)
  local copies, waits for them, and re-layouts  0.91 us (1%)
  between operations  0.78 us (1%)
    ppermute x14, waiting for transfers between devices, across(): return lax.ppermute(value, ('segment', 'chan'), links)  17.7 us
    ppermute x14, starting transfers between devices, across(): return lax.ppermute(value, ('segment', 'chan'), links)  16.2 us
    pallas_call x19, Pallas kernels, call(): pl.pallas_call(kernel, out_shape=[jax.ShapeDtypeStruct(*o[:2]) if len(o)...  15 us
    ppermute x5, waiting for transfers between devices, by_core(): return lax.ppermute(value, ('dp', 'chan'), links)  8.46 us
    ppermute x3, starting transfers between devices, over_z(): lax.ppermute(value, 'dp', [(y * 8 + z, y * 8 + (z + d) % 8) for y in rang...  7.58 us
    ppermute x5, starting transfers between devices, by_core(): return lax.ppermute(value, ('dp', 'chan'), links)  6.47 us
    ppermute x3, waiting for transfers between devices, over_z(): lax.ppermute(value, 'dp', [(y * 8 + z, y * 8 + (z + d) % 8) for y in rang...  2.21 us
  transfers between devices with their start and end apart: 22, of which 12 were waited for; matrix products, arithmetic and copies ran while one was open for 0% of the time, Pallas kernels for 14%

profile of v5, /device:TPU:4, one launch (start us, length us, event | category | flops | bytes accessed | tf_op | source)
XLA Modules:
  0.0 75.5 jit_solution(12404269179524460287)
XLA Ops:
  1.3 4.9 %collective-permute-done.refs_0_ = bf16[2,128,256]{2,1,0:T(8,128)(2,1)S(1)} collective-permute-done((bf16[2,128,256]{2,1,0:T(8,128)(2,1)}, bf16[2,128,256]{2,1,0:T(8,128)(2,1)S(1)}, u32[]{:S(2)}, u32[]{:S(2)}) %collective-permute-start) | collective-permute-done | bytes 131104 | tf_op jit(solution)/shard_map/ppermute | solution.py:474
  6.2 2.6 %shard_map.121 = (bf16[512,1152]{1,0:T(8,128)(2,1)S(1)}, f32[2,512]{1,0:T(2,128)S(1)}, f32[2,128]{1,0:T(2,128)S(1)}, f32[512,128]{1,0:T(8,128)S(1)}, f32[5,256,1...) custom-call(s32[4]{0:T(128)S(1)} %pad_add_fusion.idx, bf16[4608,128]{1,0:T(8,128)(2,1)} %bitcast.12, ...), custom_call_target="tpu_custom_call" | custom-call | tf_op jit(solution)/shard_map/pallas_call | solution.py:447
  8.9 0.9 %copy-done.1 = bf16[2,128,256]{2,1,0:T(8,128)(2,1)S(1)} copy-done((bf16[2,128,256]{2,1,0:T(8,128)(2,1)S(1)}, bf16[2,128,256]{2,1,0:T(8,128)(2,1)}, u32[]{:S(2)}) %copy-start.1) | copy-done | bytes 131096
  10.3 0.8 %shard_map.123 = (bf16[528,128]{1,0:T(8,128)(2,1)S(1)}, f32[512,128]{1,0:T(8,128)S(1)}, f32[512,128]{1,0:T(8,128)S(1)}, bf16[512,256]{1,0:T(8,128)(2,1)S(1)}) custom-call(bf16[2,128,256]{2,1,0:T(8,128)(2,1)S(1)} %collective-permute-done.refs_0_, bf16[2,128,256]{2,1,0:T(8,128)(2,1)S(1)} %collective-permute-done.1.refs_1_, ...), custom_call_target="tpu_custom_call" | custom-call | tf_op jit(solution)/shard_map/pallas_call | solution.py:447
  11.7 3.8 %collective-permute-start.3 = (bf16[528,128]{1,0:T(8,128)(2,1)S(1)}, bf16[528,128]{1,0:T(8,128)(2,1)S(1)}, u32[]{:S(2)}, u32[]{:S(2)}) collective-permute-start(bf16[528,128]{1,0:T(8,128)(2,1)S(1)} %get-tuple-element.47), channel_id=1, source_target_pairs={{0,4},{1,5},{2,6},{3,7},{4,0},{5,1},{6,2},{7,3},{8,12},{9,13},{10,... | collective-permute-start | bytes 405512 | tf_op jit(solution)/shard_map/ppermute | solution.py:474
  15.5 1.7 %collective-permute-done.5.xb_ref.refs_2_ = bf16[528,128]{1,0:T(8,128)(2,1)S(1)} collective-permute-done((bf16[528,128]{1,0:T(8,128)(2,1)S(1)}, bf16[528,128]{1,0:T(8,128)(2,1)S(1)}, u32[]{:S(2)}, u32[]{:S(2)}) %collective-permute-start.5) | collective-permute-done | bytes 135200 | tf_op jit(solution)/shard_map/ppermute | solution.py:474
  17.2 2.3 %collective-permute-done.3.xa_ref.refs_0_ = bf16[528,128]{1,0:T(8,128)(2,1)S(1)} collective-permute-done((bf16[528,128]{1,0:T(8,128)(2,1)S(1)}, bf16[528,128]{1,0:T(8,128)(2,1)S(1)}, u32[]{:S(2)}, u32[]{:S(2)}) %collective-permute-start.3) | collective-permute-done | bytes 135200 | tf_op jit(solution)/shard_map/ppermute | solution.py:474
  20.0 0.8 %collective-permute-done.4.refs_0_.refs_1_ = bf16[528,128]{1,0:T(8,128)(2,1)S(1)} collective-permute-done((bf16[528,128]{1,0:T(8,128)(2,1)S(1)}, bf16[528,128]{1,0:T(8,128)(2,1)S(1)}, u32[]{:S(2)}, u32[]{:S(2)}) %collective-permute-start.4) | collective-permute-done | bytes 135200 | tf_op jit(solution)/shard_map/ppermute | solution.py:474
  20.9 0.8 %shard_map.125 = (bf16[528,128]{1,0:T(8,128)(2,1)S(1)}, f32[512,128]{1,0:T(8,128)S(1)}, f32[512,128]{1,0:T(8,128)S(1)}, bf16[512,256]{1,0:T(8,128)(2,1)S(1)}) custom-call(bf16[528,128]{1,0:T(8,128)(2,1)S(1)} %collective-permute-done.4.refs_0_.refs_1_, bf16[528,128]{1,0:T(8,128)(2,1)S(1)} %collective-permute-done.6.refs_1_.refs_3_, ...), custom_call_target="tpu_custom_call" | custom-call | tf_op jit(solution)/shard_map/pallas_call | solution.py:447
  21.9 1.0 %collective-permute-done.7.got_ref = f32[8,512]{1,0:T(8,128)S(1)} collective-permute-done((f32[8,512]{1,0:T(8,128)S(1)}, f32[8,512]{1,0:T(8,128)S(1)}, u32[]{:S(2)}, u32[]{:S(2)}) %collective-permute-start.7) | collective-permute-done | bytes 16416 | tf_op jit(solution)/shard_map/ppermute | solution.py:474
  23.0 2.3 %collective-permute-start.8 = (f32[8,512]{1,0:T(8,128)S(1)}, f32[8,512]{1,0:T(8,128)S(1)}, u32[]{:S(2)}, u32[]{:S(2)}) collective-permute-start(f32[8,512]{1,0:T(8,128)S(1)} %shard_map.127.own_ref), channel_id=1, source_target_pairs={{0,2},{1,3},{2,0},{3,1},{4,6},{5,7},{6,4},{7,5},{8,10},{9,11},{10,... | collective-permute-start | bytes 49160 | tf_op jit(solution)/shard_map/ppermute | solution.py:474
  25.5 2.7 %collective-permute-done.8.other_ref = f32[8,512]{1,0:T(8,128)S(1)} collective-permute-done((f32[8,512]{1,0:T(8,128)S(1)}, f32[8,512]{1,0:T(8,128)S(1)}, u32[]{:S(2)}, u32[]{:S(2)}) %collective-permute-start.8) | collective-permute-done | bytes 16416 | tf_op jit(solution)/shard_map/ppermute | solution.py:474
  28.2 1.7 %shard_map.129 = (bf16[32,128]{1,0:T(8,128)(2,1)S(1)}, bf16[528,128]{1,0:T(8,128)(2,1)S(1)}, f32[1024,128]{1,0:T(8,128)S(1)}, bf16[1024,128]{1,0:T(8,128)(2,1)S(1)}) custom-call(f32[8,512]{1,0:T(8,128)S(1)} %shard_map.127.own_ref, f32[8,512]{1,0:T(8,128)S(1)} %collective-permute-done.8.other_ref, f32[8,512]{1,0:T(8,128)S(1)} %shard_map.128.first_ref, ...), custom_call_target="tpu_custom_call" | custom-call | tf_op jit(solution)/shard_map/pallas_call | solution.py:447
  30.0 0.8 %shard_map.132.xm_ref = bf16[528,512]{1,0:T(8,128)(2,1)S(1)} custom-call(s32[4]{0:T(128)S(1)} %pad_add_fusion.idx, bf16[512,256]{1,0:T(8,128)(2,1)S(1)} %get-tuple-element.61.a01_ref, bf16[512,256]{1,0:T(8,128)(2,1)S(1)} %get-tuple-element.62.a23_ref, bf16[512,256]{1,0:T(8,128)(2,1)S(1)} %get-tuple-element.63.b02_ref, ...), custom_call_target="tpu_custom_call" | custom-call | tf_op jit(solution)/shard_map/pallas_call | solution.py:447
  31.6 2.9 %collective-permute-start.10 = (bf16[544,128]{1,0:T(8,128)(2,1)S(1)}, bf16[544,128]{1,0:T(8,128)(2,1)S(1)}, u32[]{:S(2)}, u32[]{:S(2)}) collective-permute-start(bf16[544,128]{1,0:T(8,128)(2,1)S(1)} %get-tuple-element.56), channel_id=1, source_target_pairs={{0,4},{1,5},{2,6},{3,7},{4,0},{5,1},{6,2},{7,3},{8,12},{9,13},{10,... | collective-permute-start | bytes 417800 | tf_op jit(solution)/shard_map/ppermute | solution.py:474
  34.5 0.9 %collective-permute-start.11 = (bf16[512,128]{1,0:T(8,128)(2,1)S(1)}, bf16[512,128]{1,0:T(8,128)(2,1)S(1)}, u32[]{:S(2)}, u32[]{:S(2)}) collective-permute-start(bf16[512,128]{1,0:T(8,128)(2,1)S(1)} %get-tuple-element.57), channel_id=1, source_target_pairs={{0,6},{1,7},{2,4},{3,5},{4,2},{5,3},{6,0},{7,1},{8,14},{9,15},{10,... | collective-permute-start | bytes 393224 | tf_op jit(solution)/shard_map/ppermute | solution.py:474
  35.4 4.0 %collective-permute-done.11.s1_ref = bf16[512,128]{1,0:T(8,128)(2,1)S(1)} collective-permute-done((bf16[512,128]{1,0:T(8,128)(2,1)S(1)}, bf16[512,128]{1,0:T(8,128)(2,1)S(1)}, u32[]{:S(2)}, u32[]{:S(2)}) %collective-permute-start.11) | collective-permute-done | bytes 131104 | tf_op jit(solution)/shard_map/ppermute | solution.py:474
  39.4 1.0 %shard_map.131.pay_ref = bf16[528,128]{1,0:T(8,128)(2,1)S(1)} custom-call(s32[4]{0:T(128)S(1)} %pad_add_fusion.idx, bf16[544,128]{1,0:T(8,128)(2,1)S(1)} %collective-permute-done.10.s0_ref, bf16[512,128]{1,0:T(8,128)(2,1)S(1)} %collective-permute-done.11.s1_ref, bf16[16,128]{1,0:T(8,128)(2,1)S(1)} %get-tuple-element.45.refs_6_.rgb_ref, ...), custom_call_target="tpu_custom_call" | custom-call | tf_op jit(solution)/shard_map/pallas_call | solution.py:447
  40.5 1.6 %shard_map.133 = (f32[1024,128]{1,0:T(8,128)S(1)}, bf16[1024,128]{1,0:T(8,128)(2,1)S(1)}, f32[512,1152]{1,0:T(8,128)S(1)}) custom-call(bf16[528,128]{1,0:T(8,128)(2,1)S(1)} %shard_map.131.pay_ref, bf16[512,1152]{1,0:T(8,128)(2,1)S(1)} %get-tuple-element.42.wslot_ref.refs_3_, f32[2,512]{1,0:T(2,128)S(1)} %get-tuple-element.41.stys_ref.refs_2_, ...), custom_call_target="tpu_custom_call" | custom-call | tf_op jit(solution)/shard_map/pallas_call | solution.py:447
  42.0 2.8 %collective-permute-start.20 = (bf16[1024,128]{1,0:T(8,128)(2,1)S(1)}, bf16[1024,128]{1,0:T(8,128)(2,1)S(1)}, u32[]{:S(2)}, u32[]{:S(2)}) collective-permute-start(bf16[1024,128]{1,0:T(8,128)(2,1)S(1)} %get-tuple-element.76), channel_id=1, source_target_pairs={{0,1},{1,0},{2,3},{3,2},{4,5},{5,4},{6,7},{7,6},{8,9},{9,8},{10,11... | collective-permute-start | bytes 786440 | tf_op jit(solution)/shard_map/ppermute | solution.py:474
  44.9 5.0 %collective-permute-done.12.other_pay_ref = bf16[528,128]{1,0:T(8,128)(2,1)S(1)} collective-permute-done((bf16[528,128]{1,0:T(8,128)(2,1)S(1)}, bf16[528,128]{1,0:T(8,128)(2,1)S(1)}, u32[]{:S(2)}, u32[]{:S(2)}) %collective-permute-start.12) | collective-permute-done | bytes 135200 | tf_op jit(solution)/shard_map/ppermute | solution.py:483
  49.9 1.6 %shard_map.134 = (bf16[576,128]{1,0:T(8,128)(2,1)S(1)}, bf16[576,128]{1,0:T(8,128)(2,1)S(1)}, bf16[576,128]{1,0:T(8,128)(2,1)S(1)}, bf16[576,128]{1,0:T(8,128)(2,1)S(1)}) custom-call(s32[4]{0:T(128)S(1)} %pad_add_fusion.idx, bf16[528,128]{1,0:T(8,128)(2,1)S(1)} %shard_map.131.pay_ref, bf16[528,128]{1,0:T(8,128)(2,1)S(1)} %collective-permute-done.12.other_pay_ref, ...), custom_call_target="tpu_custom_call" | custom-call | tf_op jit(solution)/shard_map/pallas_call | solution.py:447
  51.5 1.6 %collective-permute-start.14 = (bf16[576,128]{1,0:T(8,128)(2,1)S(1)}, bf16[576,128]{1,0:T(8,128)(2,1)S(1)}, u32[]{:S(2)}, u32[]{:S(2)}) collective-permute-start(bf16[576,128]{1,0:T(8,128)(2,1)S(1)} %get-tuple-element.68), channel_id=1, source_target_pairs={{0,64},{1,193},{2,66},{3,195},{8,72},{9,201},{10,74},{11,203},{16,... | collective-permute-start | bytes 442376 | tf_op jit(solution)/shard_map/ppermute | solution.py:483
  53.1 2.9 %collective-permute-start.15 = (bf16[576,128]{1,0:T(8,128)(2,1)S(1)}, bf16[576,128]{1,0:T(8,128)(2,1)S(1)}, u32[]{:S(2)}, u32[]{:S(2)}) collective-permute-start(bf16[576,128]{1,0:T(8,128)(2,1)S(1)} %get-tuple-element.69), channel_id=1, source_target_pairs={{0,128},{1,129},{2,130},{3,131},{8,136},{9,137},{10,138},{11,139},... | collective-permute-start | bytes 442376 | tf_op jit(solution)/shard_map/ppermute | solution.py:483
  56.0 1.3 %collective-permute-start.16 = (bf16[576,128]{1,0:T(8,128)(2,1)S(1)}, bf16[576,128]{1,0:T(8,128)(2,1)S(1)}, u32[]{:S(2)}, u32[]{:S(2)}) collective-permute-start(bf16[576,128]{1,0:T(8,128)(2,1)S(1)} %get-tuple-element.70), channel_id=1, source_target_pairs={{0,192},{1,65},{2,194},{3,67},{8,200},{9,73},{10,202},{11,75},{16,... | collective-permute-start | bytes 442376 | tf_op jit(solution)/shard_map/ppermute | solution.py:483
  57.5 2.1 %collective-permute-start.21 = (bf16[512,128]{1,0:T(8,128)(2,1)S(1)}, bf16[512,128]{1,0:T(8,128)(2,1)S(1)}, u32[]{:S(2)}, u32[]{:S(2)}) collective-permute-start(bf16[512,128]{1,0:T(8,128)(2,1)S(1)} %get-tuple-element.78), channel_id=1, source_target_pairs={{0,2},{1,3},{2,0},{3,1},{4,6},{5,7},{6,4},{7,5},{8,10},{9,11},{10,... | collective-permute-start | bytes 393224 | tf_op jit(solution)/shard_map/ppermute | solution.py:474
  59.5 3.4 %collective-permute-done.15.r2_ref = bf16[576,128]{1,0:T(8,128)(2,1)S(1)} collective-permute-done((bf16[576,128]{1,0:T(8,128)(2,1)S(1)}, bf16[576,128]{1,0:T(8,128)(2,1)S(1)}, u32[]{:S(2)}, u32[]{:S(2)}) %collective-permute-start.15) | collective-permute-done | bytes 147488 | tf_op jit(solution)/shard_map/ppermute | solution.py:483
  63.0 1.3 %collective-permute-start.17 = (bf16[144,128]{1,0:T(8,128)(2,1)S(1)}, bf16[144,128]{1,0:T(8,128)(2,1)S(1)}, u32[]{:S(2)}, u32[]{:S(2)}) collective-permute-start(bf16[144,128]{1,0:T(8,128)(2,1)S(1)} %get-tuple-element.72), channel_id=1, source_target_pairs={{0,16},{8,24},{16,32},{24,40},{32,48},{40,56},{48,0},{56,8},{64,80... | collective-permute-start | bytes 110600 | tf_op jit(solution)/shard_map/ppermute | solution.py:489
  64.4 4.8 %collective-permute-start.18 = (bf16[144,128]{1,0:T(8,128)(2,1)S(1)}, bf16[144,128]{1,0:T(8,128)(2,1)S(1)}, u32[]{:S(2)}, u32[]{:S(2)}) collective-permute-start(bf16[144,128]{1,0:T(8,128)(2,1)S(1)} %get-tuple-element.73), channel_id=1, source_target_pairs={{0,32},{8,40},{16,48},{24,56},{32,0},{40,8},{48,16},{56,24},{64,96... | collective-permute-start | bytes 110600 | tf_op jit(solution)/shard_map/ppermute | solution.py:489
  69.2 1.4 %collective-permute-start.19 = (bf16[144,128]{1,0:T(8,128)(2,1)S(1)}, bf16[144,128]{1,0:T(8,128)(2,1)S(1)}, u32[]{:S(2)}, u32[]{:S(2)}) collective-permute-start(bf16[144,128]{1,0:T(8,128)(2,1)S(1)} %get-tuple-element.74), channel_id=1, source_target_pairs={{0,48},{8,56},{16,0},{24,8},{32,16},{40,24},{48,32},{56,40},{64,11... | collective-permute-start | bytes 110600 | tf_op jit(solution)/shard_map/ppermute | solution.py:489
  70.6 1.2 %shard_map.137 = f32[2]{0:T(128)} custom-call(s32[4]{0:T(128)S(1)} %pad_add_fusion.idx, bf16[544,128]{1,0:T(8,128)(2,1)S(1)} %collective-permute-done.10.s0_ref, bf16[32,128]{1,0:T(8,128)(2,1)S(1)} %get-tuple-element.55.tail_ref), custom_call_target="tpu_custom_call" | custom-call | tf_op jit(solution)/shard_map/pallas_call | solution.py:447
  72.3 1.8 %collective-permute-done.19.refs_3_ = bf16[144,128]{1,0:T(8,128)(2,1)S(1)} collective-permute-done((bf16[144,128]{1,0:T(8,128)(2,1)S(1)}, bf16[144,128]{1,0:T(8,128)(2,1)S(1)}, u32[]{:S(2)}, u32[]{:S(2)}) %collective-permute-start.19) | collective-permute-done | bytes 36896 | tf_op jit(solution)/shard_map/ppermute | solution.py:489
  (36 shorter events, 5.8 us)
Async XLA Ops:
  0.6 5.5 %collective-permute-start = (bf16[2,128,256]{2,1,0:T(8,128)(2,1)}, bf16[2,128,256]{2,1,0:T(8,128)(2,1)S(1)}, u32[]{:S(2)}, u32[]{:S(2)}) collective-permute-start(bf16[2,128,256]{2,1,0:T(8,128)(2,1)} %xa_ref.1), channel_id=1, source_target_pairs={{0,6},{1,7},{2,4},{3,5},{4,2},{5,3},{6,0},{7,1},{8,14},{9,15},{10,... | collective-permute-start | bytes 393224 | tf_op jit(solution)/shard_map/ppermute | solution.py:474
  1.3 7.6 %collective-permute-start.2 = (bf16[2,128,256]{2,1,0:T(8,128)(2,1)}, bf16[2,128,256]{2,1,0:T(8,128)(2,1)S(1)}, u32[]{:S(2)}, u32[]{:S(2)}) collective-permute-start(bf16[2,128,256]{2,1,0:T(8,128)(2,1)} %xa_ref.1), channel_id=1, source_target_pairs={{0,1},{1,0},{2,3},{3,2},{4,5},{5,4},{6,7},{7,6},{8,9},{9,8},{10,11... | collective-permute-start | bytes 393224 | tf_op jit(solution)/shard_map/ppermute | solution.py:474
  6.2 4.2 %collective-permute-start.1 = (bf16[2,128,256]{2,1,0:T(8,128)(2,1)S(1)}, bf16[2,128,256]{2,1,0:T(8,128)(2,1)S(1)}, u32[]{:S(2)}, u32[]{:S(2)}) collective-permute-start(bf16[2,128,256]{2,1,0:T(8,128)(2,1)S(1)} %collective-permute-done.refs_0_), channel_id=1, source_target_pairs={{0,1},{1,0},{2,3},{3,2},{4,5},{5,4},{6,7},{7,6},{8,9},{9,8},{10,11... | collective-permute-start | bytes 393224 | tf_op jit(solution)/shard_map/ppermute | solution.py:474
  8.9 0.9 %copy-start.1 = (bf16[2,128,256]{2,1,0:T(8,128)(2,1)S(1)}, bf16[2,128,256]{2,1,0:T(8,128)(2,1)}, u32[]{:S(2)}) copy-start(bf16[2,128,256]{2,1,0:T(8,128)(2,1)} %xa_ref.1) | copy-start | bytes 393220
  11.1 6.1 %collective-permute-start.5 = (bf16[528,128]{1,0:T(8,128)(2,1)S(1)}, bf16[528,128]{1,0:T(8,128)(2,1)S(1)}, u32[]{:S(2)}, u32[]{:S(2)}) collective-permute-start(bf16[528,128]{1,0:T(8,128)(2,1)S(1)} %get-tuple-element.47), channel_id=1, source_target_pairs={{0,6},{1,7},{2,4},{3,5},{4,2},{5,3},{6,0},{7,1},{8,14},{9,15},{10,... | collective-permute-start | bytes 405512 | tf_op jit(solution)/shard_map/ppermute | solution.py:474
  11.7 7.8 %collective-permute-start.3 = (bf16[528,128]{1,0:T(8,128)(2,1)S(1)}, bf16[528,128]{1,0:T(8,128)(2,1)S(1)}, u32[]{:S(2)}, u32[]{:S(2)}) collective-permute-start(bf16[528,128]{1,0:T(8,128)(2,1)S(1)} %get-tuple-element.47), channel_id=1, source_target_pairs={{0,4},{1,5},{2,6},{3,7},{4,0},{5,1},{6,2},{7,3},{8,12},{9,13},{10,... | collective-permute-start | bytes 405512 | tf_op jit(solution)/shard_map/ppermute | solution.py:474
  17.2 2.8 %collective-permute-start.6 = (bf16[528,128]{1,0:T(8,128)(2,1)S(1)}, bf16[528,128]{1,0:T(8,128)(2,1)S(1)}, u32[]{:S(2)}, u32[]{:S(2)}) collective-permute-start(bf16[528,128]{1,0:T(8,128)(2,1)S(1)} %collective-permute-done.5.xb_ref.refs_2_), channel_id=1, source_target_pairs={{0,1},{1,0},{2,3},{3,2},{4,5},{5,4},{6,7},{7,6},{8,9},{9,8},{10,11... | collective-permute-start | bytes 405512 | tf_op jit(solution)/shard_map/ppermute | solution.py:474
  19.5 1.4 %collective-permute-start.4 = (bf16[528,128]{1,0:T(8,128)(2,1)S(1)}, bf16[528,128]{1,0:T(8,128)(2,1)S(1)}, u32[]{:S(2)}, u32[]{:S(2)}) collective-permute-start(bf16[528,128]{1,0:T(8,128)(2,1)S(1)} %collective-permute-done.3.xa_ref.refs_0_), channel_id=1, source_target_pairs={{0,1},{1,0},{2,3},{3,2},{4,5},{5,4},{6,7},{7,6},{8,9},{9,8},{10,11... | collective-permute-start | bytes 405512 | tf_op jit(solution)/shard_map/ppermute | solution.py:474
  21.8 1.2 %collective-permute-start.7 = (f32[8,512]{1,0:T(8,128)S(1)}, f32[8,512]{1,0:T(8,128)S(1)}, u32[]{:S(2)}, u32[]{:S(2)}) collective-permute-start(f32[8,512]{1,0:T(8,128)S(1)} %shard_map.126.own_ref), channel_id=1, source_target_pairs={{0,1},{1,0},{2,3},{3,2},{4,5},{5,4},{6,7},{7,6},{8,9},{9,8},{10,11... | collective-permute-start | bytes 49160 | tf_op jit(solution)/shard_map/ppermute | solution.py:474
  23.0 5.2 %collective-permute-start.8 = (f32[8,512]{1,0:T(8,128)S(1)}, f32[8,512]{1,0:T(8,128)S(1)}, u32[]{:S(2)}, u32[]{:S(2)}) collective-permute-start(f32[8,512]{1,0:T(8,128)S(1)} %shard_map.127.own_ref), channel_id=1, source_target_pairs={{0,2},{1,3},{2,0},{3,1},{4,6},{5,7},{6,4},{7,5},{8,10},{9,11},{10,... | collective-permute-start | bytes 49160 | tf_op jit(solution)/shard_map/ppermute | solution.py:474
  29.9 1.6 %collective-permute-start.9 = (bf16[1024,128]{1,0:T(8,128)(2,1)S(1)}, bf16[1024,128]{1,0:T(8,128)(2,1)S(1)}, u32[]{:S(2)}, u32[]{:S(2)}) collective-permute-start(bf16[1024,128]{1,0:T(8,128)(2,1)S(1)} %get-tuple-element.54), channel_id=1, source_target_pairs={{0,1},{1,0},{2,3},{3,2},{4,5},{5,4},{6,7},{7,6},{8,9},{9,8},{10,11... | collective-permute-start | bytes 786440 | tf_op jit(solution)/shard_map/ppermute | solution.py:474
  30.0 19.8 %copy-start = (bf16[1,4608,128]{2,1,0:T(8,128)(2,1)S(1)}, bf16[1,4608,128]{2,1,0:T(8,128)(2,1)}, u32[]{:S(2)}) copy-start(bf16[1,4608,128]{2,1,0:T(8,128)(2,1)} %param.13) | copy-start | bytes 3538948
  30.8 14.1 %collective-permute-start.13 = (bf16[528,512]{1,0:T(8,128)(2,1)S(1)}, bf16[528,512]{1,0:T(8,128)(2,1)S(1)}, u32[]{:S(2)}, u32[]{:S(2)}) collective-permute-start(bf16[528,512]{1,0:T(8,128)(2,1)S(1)} %shard_map.132.xm_ref), channel_id=1, source_target_pairs={{0,8},{1,57},{2,10},{3,59},{8,0},{9,17},{10,2},{11,19},{16,24},{17... | collective-permute-start | bytes 1622024 | tf_op jit(solution)/shard_map/ppermute | solution.py:483
  31.6 7.8 %collective-permute-start.10 = (bf16[544,128]{1,0:T(8,128)(2,1)S(1)}, bf16[544,128]{1,0:T(8,128)(2,1)S(1)}, u32[]{:S(2)}, u32[]{:S(2)}) collective-permute-start(bf16[544,128]{1,0:T(8,128)(2,1)S(1)} %get-tuple-element.56), channel_id=1, source_target_pairs={{0,4},{1,5},{2,6},{3,7},{4,0},{5,1},{6,2},{7,3},{8,12},{9,13},{10,... | collective-permute-start | bytes 417800 | tf_op jit(solution)/shard_map/ppermute | solution.py:474
  34.5 5.0 %collective-permute-start.11 = (bf16[512,128]{1,0:T(8,128)(2,1)S(1)}, bf16[512,128]{1,0:T(8,128)(2,1)S(1)}, u32[]{:S(2)}, u32[]{:S(2)}) collective-permute-start(bf16[512,128]{1,0:T(8,128)(2,1)S(1)} %get-tuple-element.57), channel_id=1, source_target_pairs={{0,6},{1,7},{2,4},{3,5},{4,2},{5,3},{6,0},{7,1},{8,14},{9,15},{10,... | collective-permute-start | bytes 393224 | tf_op jit(solution)/shard_map/ppermute | solution.py:474
  42.0 15.4 %collective-permute-start.20 = (bf16[1024,128]{1,0:T(8,128)(2,1)S(1)}, bf16[1024,128]{1,0:T(8,128)(2,1)S(1)}, u32[]{:S(2)}, u32[]{:S(2)}) collective-permute-start(bf16[1024,128]{1,0:T(8,128)(2,1)S(1)} %get-tuple-element.76), channel_id=1, source_target_pairs={{0,1},{1,0},{2,3},{3,2},{4,5},{5,4},{6,7},{7,6},{8,9},{9,8},{10,11... | collective-permute-start | bytes 786440 | tf_op jit(solution)/shard_map/ppermute | solution.py:474
  44.8 5.0 %collective-permute-start.12 = (bf16[528,128]{1,0:T(8,128)(2,1)S(1)}, bf16[528,128]{1,0:T(8,128)(2,1)S(1)}, u32[]{:S(2)}, u32[]{:S(2)}) collective-permute-start(bf16[528,128]{1,0:T(8,128)(2,1)S(1)} %shard_map.131.pay_ref), channel_id=1, source_target_pairs={{0,8},{1,57},{2,10},{3,59},{8,0},{9,17},{10,2},{11,19},{16,24},{17... | collective-permute-start | bytes 405512 | tf_op jit(solution)/shard_map/ppermute | solution.py:483
  51.5 8.0 %collective-permute-start.14 = (bf16[576,128]{1,0:T(8,128)(2,1)S(1)}, bf16[576,128]{1,0:T(8,128)(2,1)S(1)}, u32[]{:S(2)}, u32[]{:S(2)}) collective-permute-start(bf16[576,128]{1,0:T(8,128)(2,1)S(1)} %get-tuple-element.68), channel_id=1, source_target_pairs={{0,64},{1,193},{2,66},{3,195},{8,72},{9,201},{10,74},{11,203},{16,... | collective-permute-start | bytes 442376 | tf_op jit(solution)/shard_map/ppermute | solution.py:483
  53.1 9.8 %collective-permute-start.15 = (bf16[576,128]{1,0:T(8,128)(2,1)S(1)}, bf16[576,128]{1,0:T(8,128)(2,1)S(1)}, u32[]{:S(2)}, u32[]{:S(2)}) collective-permute-start(bf16[576,128]{1,0:T(8,128)(2,1)S(1)} %get-tuple-element.69), channel_id=1, source_target_pairs={{0,128},{1,129},{2,130},{3,131},{8,136},{9,137},{10,138},{11,139},... | collective-permute-start | bytes 442376 | tf_op jit(solution)/shard_map/ppermute | solution.py:483
  56.0 6.9 %collective-permute-start.16 = (bf16[576,128]{1,0:T(8,128)(2,1)S(1)}, bf16[576,128]{1,0:T(8,128)(2,1)S(1)}, u32[]{:S(2)}, u32[]{:S(2)}) collective-permute-start(bf16[576,128]{1,0:T(8,128)(2,1)S(1)} %get-tuple-element.70), channel_id=1, source_target_pairs={{0,192},{1,65},{2,194},{3,67},{8,200},{9,73},{10,202},{11,75},{16,... | collective-permute-start | bytes 442376 | tf_op jit(solution)/shard_map/ppermute | solution.py:483
  57.5 17.2 %collective-permute-start.21 = (bf16[512,128]{1,0:T(8,128)(2,1)S(1)}, bf16[512,128]{1,0:T(8,128)(2,1)S(1)}, u32[]{:S(2)}, u32[]{:S(2)}) collective-permute-start(bf16[512,128]{1,0:T(8,128)(2,1)S(1)} %get-tuple-element.78), channel_id=1, source_target_pairs={{0,2},{1,3},{2,0},{3,1},{4,6},{5,7},{6,4},{7,5},{8,10},{9,11},{10,... | collective-permute-start | bytes 393224 | tf_op jit(solution)/shard_map/ppermute | solution.py:474
  63.0 8.8 %collective-permute-start.17 = (bf16[144,128]{1,0:T(8,128)(2,1)S(1)}, bf16[144,128]{1,0:T(8,128)(2,1)S(1)}, u32[]{:S(2)}, u32[]{:S(2)}) collective-permute-start(bf16[144,128]{1,0:T(8,128)(2,1)S(1)} %get-tuple-element.72), channel_id=1, source_target_pairs={{0,16},{8,24},{16,32},{24,40},{32,48},{40,56},{48,0},{56,8},{64,80... | collective-permute-start | bytes 110600 | tf_op jit(solution)/shard_map/ppermute | solution.py:489
  64.4 7.9 %collective-permute-start.18 = (bf16[144,128]{1,0:T(8,128)(2,1)S(1)}, bf16[144,128]{1,0:T(8,128)(2,1)S(1)}, u32[]{:S(2)}, u32[]{:S(2)}) collective-permute-start(bf16[144,128]{1,0:T(8,128)(2,1)S(1)} %get-tuple-element.73), channel_id=1, source_target_pairs={{0,32},{8,40},{16,48},{24,56},{32,0},{40,8},{48,16},{56,24},{64,96... | collective-permute-start | bytes 110600 | tf_op jit(solution)/shard_map/ppermute | solution.py:489
  69.2 4.9 %collective-permute-start.19 = (bf16[144,128]{1,0:T(8,128)(2,1)S(1)}, bf16[144,128]{1,0:T(8,128)(2,1)S(1)}, u32[]{:S(2)}, u32[]{:S(2)}) collective-permute-start(bf16[144,128]{1,0:T(8,128)(2,1)S(1)} %get-tuple-element.74), channel_id=1, source_target_pairs={{0,48},{8,56},{16,0},{24,8},{32,16},{40,24},{48,32},{56,40},{64,11... | collective-permute-start | bytes 110600 | tf_op jit(solution)/shard_map/ppermute | solution.py:489
